TPU v7x, 128 devices: a whole 4x4x4 slice. The times are simulated.
128 devices in a mesh: band: 4 (over x_hi, core), dom: 32 (over y, x_lo, z).
Axes of the slice: x: 4 (x_hi: 2, x_lo: 2; x = x_hi * 2 + x_lo), y: 4, z: 4, core: 2. Of those that a mesh axis runs over, the one named last changes fastest.
Arguments:
- orbitals: float32 [16, 128, 128, 128], P('band', 'dom'), may hold values from -24 to 24
- potential: float32 [128, 128, 128], P('dom'), may hold values from -1.25 to 1.25
- rotation: float32 [16, 16], replicated, may hold values from -1.5 to 1.5
Outputs:
- rotated: float32 [16, 128, 128, 128], P('band', 'dom')
- correlation: float32 [16, 16], P('band')
All inputs are finite; a program needn't handle non-finite values.
Results may differ from a plain program's by a relative error of at most 0.00022.
Values sent between devices are 32-bit elements; how exact they have to be, the bound alone decides.
No kernel may reach another device: no remote copies, remote signals or barrier semaphores. Data moves between devices by JAX's collectives and lax.ppermute only.
A program may use at most 128 MiB of HBM per device.

v0:
```python
import jax
import jax.numpy as jnp
import numpy as np
from jax import lax
from jax.experimental import pallas as pl
from jax.experimental.pallas import tpu as pltpu
from jax.sharding import Mesh, PartitionSpec as P

DEGREE = 8
CENTER = 4.5
HALF_WIDTH = 5.0
AXES = ("x_hi", "core", "y", "x_lo", "z")
SIZES = (2, 2, 4, 2, 4)
N = 128
PAD = 8
ROWS = N + 2 * PAD
OWN = 16
SPAN = 3 * OWN


def moved(array, where):
    pairs = []
    for i in range(int(np.prod(SIZES))):
        c = dict(zip(AXES, (int(k) for k in np.unravel_index(i, SIZES))))
        d = where(c)
        j = int(np.ravel_multi_index([d[a] % s for a, s in zip(AXES, SIZES)], SIZES))
        pairs.append((i, j))
    return lax.ppermute(array, AXES, pairs)


def to_orbital(shift):
    return lambda c: {**c, "core": c["x_lo"], "x_lo": c["core"], "z": c["z"] + shift}


def to_outer(c):
    return {**c, "core": 1 - c["core"], "y": c["y"] + (1 if c["core"] == 1 else -1)}


def to_sibling(c):
    return {**c, "core": 1 - c["core"]}


def to_home(a, e):
    return lambda c: {
        **c,
        "x_hi": c["x_hi"] ^ a,
        "core": c["x_lo"] ^ e,
        "x_lo": c["core"],
    }


FACTOR = 2.0 / HALF_WIDTH
DIAG = FACTOR * (0.5 * 7.5 - CENTER)
NEAR = FACTOR * (-0.5 * 4.0 / 3.0)
FAR = -1.0 / 16.0


def filter_kernel(place, *refs):
    blocks = refs[:12]
    out = refs[12]
    one, two, pot, sems, out_sem = refs[13:]
    core = place[0]
    z = place[1]
    rows = pl.ds(PAD, N)
    copies = []
    for part in range(3):
        offset = [OWN, 2 * OWN * (1 - core), 2 * OWN * core][part]
        for shift in range(4):
            ref = blocks[4 * part + shift]
            first = offset + 4 * lax.rem(z + 4 - shift, 4)
            for kind, target in ((0, one), (1, pot)):
                n = len(copies)
                copies.append(
                    pltpu.make_async_copy(
                        ref.at[pl.ds(4 * kind, 4)],
                        target.at[pl.ds(first, 4), rows, :],
                        sems.at[n],
                    )
                )
    for copy in copies:
        copy.start()
    for copy in copies:
        copy.wait()

    @pl.loop(0, SPAN)
    def _(p):
        one[p, 0:PAD, :] = one[p, N : N + PAD, :]
        one[p, N + PAD : ROWS, :] = one[p, PAD : 2 * PAD, :]
        pot[p, PAD : PAD + N, :] = FACTOR * pot[p, PAD : PAD + N, :] + DIAG

    for step in range(1, DEGREE + 1):
        src, dst = (one, two) if step % 2 == 1 else (two, one)

        @pl.loop(0, (SPAN - 4 * step) // 4)
        def _(group):
            p = 2 * step + 4 * group
            for t in range(N // 8):
                r = PAD + 8 * t
                column = [src[p + k - 2, r : r + 8, :] for k in range(8)]
                for k in range(4):
                    v = column[k + 2]
                    near = column[k + 1] + column[k + 3]
                    far = column[k] + column[k + 4]
                    near = near + (src[p + k, r - 1 : r + 7, :] + src[p + k, r + 1 : r + 9, :])
                    far = far + (src[p + k, r - 2 : r + 6, :] + src[p + k, r + 2 : r + 10, :])
                    near = near + (pltpu.roll(v, 1, 1) + pltpu.roll(v, N - 1, 1))
                    far = far + (pltpu.roll(v, 2, 1) + pltpu.roll(v, N - 2, 1))
                    res = pot[p + k, r : r + 8, :] * v + NEAR * (near + FAR * far)
                    if step == 1:
                        res = 0.5 * res
                    else:
                        res = res - dst[p + k, r : r + 8, :]
                    dst[p + k, r : r + 8, :] = res
                    if t == 0:
                        dst[p + k, N + PAD : ROWS, :] = res
                    if t == N // 8 - 1:
                        dst[p + k, 0:PAD, :] = res

    last = one if DEGREE % 2 == 0 else two
    copies = []
    for n in range(OWN):
        q = 4 * (n % 4) + n // 4
        copies.append(
            pltpu.make_async_copy(last.at[OWN + q, rows, :], out.at[n], out_sem.at[n])
        )
    for copy in copies:
        copy.start()
    for copy in copies:
        copy.wait()


def filtered(place, blocks):
    anywhere = pl.BlockSpec(memory_space=pl.ANY)
    return pl.pallas_call(
        filter_kernel,
        out_shape=jax.ShapeDtypeStruct((OWN, N, N), jnp.float32),
        grid_spec=pltpu.PrefetchScalarGridSpec(
            num_scalar_prefetch=1,
            grid=(1,),
            in_specs=[anywhere] * 12,
            out_specs=anywhere,
            scratch_shapes=[pltpu.VMEM((SPAN, ROWS, N), jnp.float32)] * 3
            + [pltpu.SemaphoreType.DMA((24,)), pltpu.SemaphoreType.DMA((OWN,))],
        ),
        compiler_params=pltpu.CompilerParams(vmem_limit_bytes=40 << 20),
        name="chebyshev",
    )(place, *blocks)


def rotate_kernel(place, rotation, x, o0, o1, o2, o3, gram, rot):
    band = place[0]
    outs = (o0, o1, o2, o3)
    for rel in range(4):
        b = band ^ rel

        @pl.loop(0, 4)
        def _(j, rel=rel, b=b):
            col = 4 * b + j
            coeffs = [rotation[i, col] for i in range(16)]

            @pl.loop(0, 4)
            def _(tt):
                for u in range(4):
                    r = pl.multiple_of(32 * tt + 8 * u, 8)
                    total = coeffs[0] * x[0, pl.ds(r, 8), :]
                    for i in range(1, 16):
                        total = total + coeffs[i] * x[i, pl.ds(r, 8), :]
                    outs[rel][j, pl.ds(r, 8), :] = total
                    rot[col, pl.ds(r, 8), :] = total

    @pl.loop(0, 16)
    def _(j):
        sums = [jnp.zeros((8, N), jnp.float32) for _ in range(16)]
        for t in range(N // 8):
            a = rot[j, 8 * t : 8 * t + 8, :]
            sums = [s + a * rot[k, 8 * t : 8 * t + 8, :] for k, s in enumerate(sums)]
        for k in range(16):
            gram[j, k : k + 1, :] = jnp.sum(sums[k], axis=0, keepdims=True)


def rotated_parts(place, rotation, planes):
    vmem = pl.BlockSpec(memory_space=pltpu.VMEM)
    smem = pl.BlockSpec(memory_space=pltpu.SMEM)
    part = jax.ShapeDtypeStruct((4, N, N), jnp.float32)
    return pl.pallas_call(
        rotate_kernel,
        out_shape=[part] * 4 + [jax.ShapeDtypeStruct((16, 16, N), jnp.float32)],
        in_specs=[smem, smem, vmem],
        out_specs=[vmem] * 5,
        scratch_shapes=[pltpu.VMEM((16, N, N), jnp.float32)],
        compiler_params=pltpu.CompilerParams(vmem_limit_bytes=32 << 20),
        name="rotate",
    )(place, rotation, planes)


def local(orbitals, potential, rotation):
    x_hi = lax.axis_index("x_hi")
    core = lax.axis_index("core")
    x_lo = lax.axis_index("x_lo")
    z = lax.axis_index("z")
    order = (0, 2, 1, 3)
    own = {}
    for shift in order:
        orbital = lax.dynamic_index_in_dim(orbitals, (z + shift) % 4, 0, keepdims=False)
        block = jnp.concatenate([orbital, potential], axis=0)
        own[shift] = moved(block, to_orbital(shift))
    outer = {s: moved(own[s], to_outer) for s in order}
    sibling = {s: moved(own[s], to_sibling) for s in order}
    place = jnp.stack([core, z]).astype(jnp.int32)
    blocks = [d[s] for d in (own, sibling, outer) for s in range(4)]
    mine = filtered(place, blocks)
    planes = lax.all_to_all(mine, ("x_hi", "x_lo", "z"), 0, 0, tiled=True)
    *parts, gram = rotated_parts(
        jnp.stack([2 * x_hi + x_lo]).astype(jnp.int32), rotation, planes
    )
    home = [moved(parts[2 * a + e], to_home(a, e)) for a in range(2) for e in range(2)]
    rows = jnp.sum(gram, axis=2).reshape(4, 64)
    rows = jnp.pad(rows, ((0, 0), (0, 64)))
    rows = jnp.broadcast_to(rows[:, None], (4, 32, 128)).reshape(128, 128)
    rows = lax.all_to_all(rows, AXES, 0, 0, tiled=True)
    correlation = (jnp.sum(rows, axis=0)[:64] / (N * N * N)).reshape(4, 16)
    band = 2 * x_hi + core
    pieces = []
    for p in range(4):
        rel = band ^ p
        piece = jnp.where(
            rel < 2,
            jnp.where(rel == 0, home[0], home[1]),
            jnp.where(rel == 2, home[2], home[3]),
        )
        pieces.append(piece)
    return jnp.stack(pieces, axis=1), correlation


def solution(mesh):
    fine = Mesh(mesh.devices.reshape(SIZES), AXES)
    band, dom = ("x_hi", "core"), ("y", "x_lo", "z")
    return jax.shard_map(
        local,
        mesh=fine,
        in_specs=(P(band, dom, None, None), P(dom, None, None), P()),
        out_specs=(P(band, dom, None, None), P(band, None)),
        check_vma=False,
    )
```

profile of v0, /device:TPU:1, one launch (start us, length us, event | category | flops | bytes accessed | tf_op | source)
XLA Modules:
  0.0 137.3 jit_solution(3227634403634637484)
XLA Ops:
  0.7 1.3 dynamic-slice_bitcast_fusion
  2.3 6.0 %collective-permute-start.2 = (f32[8,128,128]{2,1,0:T(8,128)S(1)}, f32[8,128,128]{2,1,0:T(8,128)S(1)}, u32[]{:S(2)}, u32[]{:S(2)}) collective-permute-start(f32[8,128,128]{2,1,0:T(8,128)S(1)} %get-tuple-element.26), channel_id=1, source_target_pairs={{0,2},{1,3},{2,0},{3,1},{4,34},{5,35},{6,32},{7,33},{8,10},{9,11},... | collective-permute-start | bytes 1572872 | tf_op jit(solution)/shard_map/ppermute | solution.py:28
  8.3 0.2 collective-permute-start.3
  8.5 3.5 %collective-permute-start = (f32[8,128,128]{2,1,0:T(8,128)S(1)}, f32[8,128,128]{2,1,0:T(8,128)S(1)}, u32[]{:S(2)}, u32[]{:S(2)}) collective-permute-start(f32[8,128,128]{2,1,0:T(8,128)S(1)} %get-tuple-element.27), channel_id=1, source_target_pairs={{0,0},{1,1},{2,2},{3,3},{4,32},{5,33},{6,34},{7,35},{8,8},{9,9},{1... | collective-permute-start | bytes 1572872 | tf_op jit(solution)/shard_map/ppermute | solution.py:28
  12.1 0.8 collective-permute-start.1
  12.9 2.4 %collective-permute-done.2.refs_2_ = f32[8,128,128]{2,1,0:T(8,128)S(1)} collective-permute-done((f32[8,128,128]{2,1,0:T(8,128)S(1)}, f32[8,128,128]{2,1,0:T(8,128)S(1)}, u32[]{:S(2)}, u32[]{:S(2)}) %collective-permute-start.2) | collective-permute-done | bytes 524320 | tf_op jit(solution)/shard_map/ppermute | solution.py:28
  15.3 6.5 %collective-permute-start.10 = (f32[8,128,128]{2,1,0:T(8,128)S(1)}, f32[8,128,128]{2,1,0:T(8,128)S(1)}, u32[]{:S(2)}, u32[]{:S(2)}) collective-permute-start(f32[8,128,128]{2,1,0:T(8,128)S(1)} %collective-permute-done.2.refs_2_), channel_id=1, source_target_pairs={{0,56},{1,57},{2,58},{3,59},{4,60},{5,61},{6,62},{7,63},{8,32},{9,... | collective-permute-start | bytes 1572872 | tf_op jit(solution)/shard_map/ppermute | solution.py:28
  21.8 12.2 %collective-permute-start.11 = (f32[8,128,128]{2,1,0:T(8,128)S(1)}, f32[8,128,128]{2,1,0:T(8,128)S(1)}, u32[]{:S(2)}, u32[]{:S(2)}) collective-permute-start(f32[8,128,128]{2,1,0:T(8,128)S(1)} %collective-permute-done.3.refs_3_), channel_id=1, source_target_pairs={{0,56},{1,57},{2,58},{3,59},{4,60},{5,61},{6,62},{7,63},{8,32},{9,... | collective-permute-start | bytes 1572872 | tf_op jit(solution)/shard_map/ppermute | solution.py:28
  34.0 0.5 collective-permute-start.6
  34.5 0.5 collective-permute-start.5
  35.0 6.1 %collective-permute-done.11.refs_11_ = f32[8,128,128]{2,1,0:T(8,128)S(1)} collective-permute-done((f32[8,128,128]{2,1,0:T(8,128)S(1)}, f32[8,128,128]{2,1,0:T(8,128)S(1)}, u32[]{:S(2)}, u32[]{:S(2)}) %collective-permute-start.11) | collective-permute-done | bytes 524320 | tf_op jit(solution)/shard_map/ppermute | solution.py:28
  41.1 1.4 %collective-permute-start.8 = (f32[8,128,128]{2,1,0:T(8,128)S(1)}, f32[8,128,128]{2,1,0:T(8,128)}, u32[]{:S(2)}, u32[]{:S(2)}) collective-permute-start(f32[8,128,128]{2,1,0:T(8,128)S(1)} %collective-permute-done.refs_0_), channel_id=1, source_target_pairs={{0,56},{1,57},{2,58},{3,59},{4,60},{5,61},{6,62},{7,63},{8,32},{9,... | collective-permute-start | bytes 1572872 | tf_op jit(solution)/shard_map/ppermute | solution.py:28
  42.6 0.8 copy-done
  43.4 0.3 collective-permute-start.9
  43.8 6.4 %collective-permute-done.8.refs_8_ = f32[8,128,128]{2,1,0:T(8,128)} collective-permute-done((f32[8,128,128]{2,1,0:T(8,128)S(1)}, f32[8,128,128]{2,1,0:T(8,128)}, u32[]{:S(2)}, u32[]{:S(2)}) %collective-permute-start.8) | collective-permute-done | bytes 524320 | tf_op jit(solution)/shard_map/ppermute | solution.py:28
  50.1 5.6 %collective-permute-done.9.refs_9_ = f32[8,128,128]{2,1,0:T(8,128)} collective-permute-done((f32[8,128,128]{2,1,0:T(8,128)S(1)}, f32[8,128,128]{2,1,0:T(8,128)}, u32[]{:S(2)}, u32[]{:S(2)}) %collective-permute-start.9) | collective-permute-done | bytes 524320 | tf_op jit(solution)/shard_map/ppermute | solution.py:28
  55.8 1.0 copy-done.1
  56.8 24.8 %chebyshev.1 = f32[16,128,128]{2,1,0:T(8,128)} custom-call(s32[2]{0:T(128)S(1)} %pad_add_fusion.place, f32[8,128,128]{2,1,0:T(8,128)S(1)} %collective-permute-done.refs_0_, f32[8,128,128]{2,1,0:T(8,128)S(1)} %collective-permute-done.1.refs_1_, f32[8,128,128]{2,1,0:T(8,128)S(1)} %collective-permute-done.2.refs_2_, ...), custom_call_target="tpu_custom_call" | custom-call | tf_op jit(solution)/shard_map/chebyshev/pallas_call | solution.py:134
  81.6 6.3 %all-to-all-start = ((f32[16,128,128]{2,1,0:T(8,128)}), f32[16,128,128]{2,1,0:T(8,128)S(1)}, u32[]{:S(2)}, u32[]{:S(2)}) async-start(f32[16,128,128]{2,1,0:T(8,128)} %chebyshev.1), calls=%async_computation | async-start | bytes 2097152 | tf_op jit(solution)/shard_map/all_to_all | solution.py:212
  88.0 14.5 %all-to-all-done.x = f32[16,128,128]{2,1,0:T(8,128)S(1)} async-done(((f32[16,128,128]{2,1,0:T(8,128)}), f32[16,128,128]{2,1,0:T(8,128)S(1)}, u32[]{:S(2)}, u32[]{:S(2)}) %all-to-all-start) | async-done | bytes 1048608 | tf_op jit(solution)/shard_map/all_to_all | solution.py:212
  102.4 4.1 %rotate.1 = (f32[4,128,128]{2,1,0:T(8,128)S(1)}, f32[4,128,128]{2,1,0:T(8,128)S(1)}, f32[4,128,128]{2,1,0:T(8,128)S(1)}, f32[4,128,128]{2,1,0:T(8,128)S(1)}, f32[16,16,128]{2,1,0:T(8,128)S(1)}) custom-call(s32[1]{0:T(128)} %bitcast.place, f32[16,16]{1,0:T(8,128)S(1)} %copy-done.2, f32[16,128,128]{2,1,0:T(8,128)S(1)} %all-to-all-done.x), custom_call_target="tpu_custom_call" | custom-call | tf_op jit(solution)/shard_map/rotate/pallas_call | solution.py:185
  106.8 0.6 broadcast_in_dim.2
  107.4 10.3 %all-to-all-start.1 = ((f32[128,1,128]{2,1,0:T(1,128)}), f32[128,1,128]{2,1,0:T(1,128)S(1)}, u32[]{:S(2)}, u32[]{:S(2)}) async-start(f32[128,1,128]{2,1,0:T(1,128)} %bitcast.11), calls=%async_computation.1 | async-start | bytes 131072 | tf_op jit(solution)/shard_map/all_to_all | solution.py:220
  117.8 3.5 %collective-permute-start.12 = (f32[4,128,128]{2,1,0:T(8,128)S(1)}, f32[4,128,128]{2,1,0:T(8,128)S(1)}, u32[]{:S(2)}, u32[]{:S(2)}) collective-permute-start(f32[4,128,128]{2,1,0:T(8,128)S(1)} %get-tuple-element.7), channel_id=1, source_target_pairs={{0,0},{1,1},{2,2},{3,3},{4,32},{5,33},{6,34},{7,35},{8,8},{9,9},{1... | collective-permute-start | bytes 786440 | tf_op jit(solution)/shard_map/ppermute | solution.py:28
  121.4 1.9 %collective-permute-start.14 = (f32[4,128,128]{2,1,0:T(8,128)S(1)}, f32[4,128,128]{2,1,0:T(8,128)S(1)}, u32[]{:S(2)}, u32[]{:S(2)}) collective-permute-start(f32[4,128,128]{2,1,0:T(8,128)S(1)} %get-tuple-element.9), channel_id=1, source_target_pairs={{0,64},{1,65},{2,66},{3,67},{4,96},{5,97},{6,98},{7,99},{8,72},{9,... | collective-permute-start | bytes 786440 | tf_op jit(solution)/shard_map/ppermute | solution.py:28
  123.3 0.7 collective-permute-start.15
  124.0 3.4 %all-to-all-done.1 = f32[128,1,128]{2,1,0:T(1,128)S(1)} async-done(((f32[128,1,128]{2,1,0:T(1,128)}), f32[128,1,128]{2,1,0:T(1,128)S(1)}, u32[]{:S(2)}, u32[]{:S(2)}) %all-to-all-start.1) | async-done | bytes 65568 | tf_op jit(solution)/shard_map/all_to_all | solution.py:220
  127.6 0.7 div.10
  128.3 1.2 collective-permute-done.13
  129.5 1.4 %collective-permute-done.14 = f32[4,128,128]{2,1,0:T(8,128)S(1)} collective-permute-done((f32[4,128,128]{2,1,0:T(8,128)S(1)}, f32[4,128,128]{2,1,0:T(8,128)S(1)}, u32[]{:S(2)}, u32[]{:S(2)}) %collective-permute-start.14) | collective-permute-done | bytes 262176 | tf_op jit(solution)/shard_map/ppermute | solution.py:28
  130.9 5.0 %collective-permute-done.15 = f32[4,128,128]{2,1,0:T(8,128)S(1)} collective-permute-done((f32[4,128,128]{2,1,0:T(8,128)S(1)}, f32[4,128,128]{2,1,0:T(8,128)S(1)}, u32[]{:S(2)}, u32[]{:S(2)}) %collective-permute-start.15) | collective-permute-done | bytes 262176 | tf_op jit(solution)/shard_map/ppermute | solution.py:28
  136.2 1.1 copy.6
  (27 shorter events, 1.0 us)
Async XLA Ops:
  0.7 1.3 copy-start.3
  2.3 13.1 %collective-permute-start.2 = (f32[8,128,128]{2,1,0:T(8,128)S(1)}, f32[8,128,128]{2,1,0:T(8,128)S(1)}, u32[]{:S(2)}, u32[]{:S(2)}) collective-permute-start(f32[8,128,128]{2,1,0:T(8,128)S(1)} %get-tuple-element.26), channel_id=1, source_target_pairs={{0,2},{1,3},{2,0},{3,1},{4,34},{5,35},{6,32},{7,33},{8,10},{9,11},... | collective-permute-start | bytes 1572872 | tf_op jit(solution)/shard_map/ppermute | solution.py:28
  8.3 13.5 %collective-permute-start.3 = (f32[8,128,128]{2,1,0:T(8,128)S(1)}, f32[8,128,128]{2,1,0:T(8,128)S(1)}, u32[]{:S(2)}, u32[]{:S(2)}) collective-permute-start(f32[8,128,128]{2,1,0:T(8,128)S(1)} %get-tuple-element.24), channel_id=1, source_target_pairs={{0,3},{1,0},{2,1},{3,2},{4,35},{5,32},{6,33},{7,34},{8,11},{9,8},{... | collective-permute-start | bytes 1572872 | tf_op jit(solution)/shard_map/ppermute | solution.py:28
  8.5 25.5 %collective-permute-start = (f32[8,128,128]{2,1,0:T(8,128)S(1)}, f32[8,128,128]{2,1,0:T(8,128)S(1)}, u32[]{:S(2)}, u32[]{:S(2)}) collective-permute-start(f32[8,128,128]{2,1,0:T(8,128)S(1)} %get-tuple-element.27), channel_id=1, source_target_pairs={{0,0},{1,1},{2,2},{3,3},{4,32},{5,33},{6,34},{7,35},{8,8},{9,9},{1... | collective-permute-start | bytes 1572872 | tf_op jit(solution)/shard_map/ppermute | solution.py:28
  12.1 22.4 %collective-permute-start.1 = (f32[8,128,128]{2,1,0:T(8,128)S(1)}, f32[8,128,128]{2,1,0:T(8,128)S(1)}, u32[]{:S(2)}, u32[]{:S(2)}) collective-permute-start(f32[8,128,128]{2,1,0:T(8,128)S(1)} %get-tuple-element.25), channel_id=1, source_target_pairs={{0,1},{1,2},{2,3},{3,0},{4,33},{5,34},{6,35},{7,32},{8,9},{9,10},{... | collective-permute-start | bytes 1572872 | tf_op jit(solution)/shard_map/ppermute | solution.py:28
  15.3 19.2 %collective-permute-start.10 = (f32[8,128,128]{2,1,0:T(8,128)S(1)}, f32[8,128,128]{2,1,0:T(8,128)S(1)}, u32[]{:S(2)}, u32[]{:S(2)}) collective-permute-start(f32[8,128,128]{2,1,0:T(8,128)S(1)} %collective-permute-done.2.refs_2_), channel_id=1, source_target_pairs={{0,56},{1,57},{2,58},{3,59},{4,60},{5,61},{6,62},{7,63},{8,32},{9,... | collective-permute-start | bytes 1572872 | tf_op jit(solution)/shard_map/ppermute | solution.py:28
  21.8 19.3 %collective-permute-start.11 = (f32[8,128,128]{2,1,0:T(8,128)S(1)}, f32[8,128,128]{2,1,0:T(8,128)S(1)}, u32[]{:S(2)}, u32[]{:S(2)}) collective-permute-start(f32[8,128,128]{2,1,0:T(8,128)S(1)} %collective-permute-done.3.refs_3_), channel_id=1, source_target_pairs={{0,56},{1,57},{2,58},{3,59},{4,60},{5,61},{6,62},{7,63},{8,32},{9,... | collective-permute-start | bytes 1572872 | tf_op jit(solution)/shard_map/ppermute | solution.py:28
  34.0 8.6 %collective-permute-start.4 = (f32[8,128,128]{2,1,0:T(8,128)S(1)}, f32[8,128,128]{2,1,0:T(8,128)S(1)}, u32[]{:S(2)}, u32[]{:S(2)}) collective-permute-start(f32[8,128,128]{2,1,0:T(8,128)S(1)} %collective-permute-done.refs_0_), channel_id=1, source_target_pairs={{0,32},{1,33},{2,34},{3,35},{4,36},{5,37},{6,38},{7,39},{8,40},{9,... | collective-permute-start | bytes 1572872 | tf_op jit(solution)/shard_map/ppermute | solution.py:28
  34.0 9.8 %collective-permute-start.6 = (f32[8,128,128]{2,1,0:T(8,128)S(1)}, f32[8,128,128]{2,1,0:T(8,128)}, u32[]{:S(2)}, u32[]{:S(2)}) collective-permute-start(f32[8,128,128]{2,1,0:T(8,128)S(1)} %collective-permute-done.2.refs_2_), channel_id=1, source_target_pairs={{0,32},{1,33},{2,34},{3,35},{4,36},{5,37},{6,38},{7,39},{8,40},{9,... | collective-permute-start | bytes 1572872 | tf_op jit(solution)/shard_map/ppermute | solution.py:28
  34.5 9.3 %collective-permute-start.7 = (f32[8,128,128]{2,1,0:T(8,128)S(1)}, f32[8,128,128]{2,1,0:T(8,128)}, u32[]{:S(2)}, u32[]{:S(2)}) collective-permute-start(f32[8,128,128]{2,1,0:T(8,128)S(1)} %collective-permute-done.3.refs_3_), channel_id=1, source_target_pairs={{0,32},{1,33},{2,34},{3,35},{4,36},{5,37},{6,38},{7,39},{8,40},{9,... | collective-permute-start | bytes 1572872 | tf_op jit(solution)/shard_map/ppermute | solution.py:28
  34.5 9.3 %collective-permute-start.5 = (f32[8,128,128]{2,1,0:T(8,128)S(1)}, f32[8,128,128]{2,1,0:T(8,128)}, u32[]{:S(2)}, u32[]{:S(2)}) collective-permute-start(f32[8,128,128]{2,1,0:T(8,128)S(1)} %collective-permute-done.1.refs_1_), channel_id=1, source_target_pairs={{0,32},{1,33},{2,34},{3,35},{4,36},{5,37},{6,38},{7,39},{8,40},{9,... | collective-permute-start | bytes 1572872 | tf_op jit(solution)/shard_map/ppermute | solution.py:28
  41.1 9.0 %collective-permute-start.8 = (f32[8,128,128]{2,1,0:T(8,128)S(1)}, f32[8,128,128]{2,1,0:T(8,128)}, u32[]{:S(2)}, u32[]{:S(2)}) collective-permute-start(f32[8,128,128]{2,1,0:T(8,128)S(1)} %collective-permute-done.refs_0_), channel_id=1, source_target_pairs={{0,56},{1,57},{2,58},{3,59},{4,60},{5,61},{6,62},{7,63},{8,32},{9,... | collective-permute-start | bytes 1572872 | tf_op jit(solution)/shard_map/ppermute | solution.py:28
  42.6 0.8 copy-start
  43.4 12.4 %collective-permute-start.9 = (f32[8,128,128]{2,1,0:T(8,128)S(1)}, f32[8,128,128]{2,1,0:T(8,128)}, u32[]{:S(2)}, u32[]{:S(2)}) collective-permute-start(f32[8,128,128]{2,1,0:T(8,128)S(1)} %collective-permute-done.1.refs_1_), channel_id=1, source_target_pairs={{0,56},{1,57},{2,58},{3,59},{4,60},{5,61},{6,62},{7,63},{8,32},{9,... | collective-permute-start | bytes 1572872 | tf_op jit(solution)/shard_map/ppermute | solution.py:28
  55.8 1.0 copy-start.1
  81.6 20.8 %all-to-all-start = ((f32[16,128,128]{2,1,0:T(8,128)}), f32[16,128,128]{2,1,0:T(8,128)S(1)}, u32[]{:S(2)}, u32[]{:S(2)}) async-start(f32[16,128,128]{2,1,0:T(8,128)} %chebyshev.1), calls=%async_computation | async-start | bytes 2097152 | tf_op jit(solution)/shard_map/all_to_all | solution.py:212
  88.0 14.5 %copy-start.2 = (f32[16,16]{1,0:T(8,128)S(1)}, f32[16,16]{1,0:T(8,128)}, u32[]{:S(2)}) copy-start(f32[16,16]{1,0:T(8,128)} %rotation.1) | copy-start | bytes 3076
  107.4 20.0 %all-to-all-start.1 = ((f32[128,1,128]{2,1,0:T(1,128)}), f32[128,1,128]{2,1,0:T(1,128)S(1)}, u32[]{:S(2)}, u32[]{:S(2)}) async-start(f32[128,1,128]{2,1,0:T(1,128)} %bitcast.11), calls=%async_computation.1 | async-start | bytes 131072 | tf_op jit(solution)/shard_map/all_to_all | solution.py:220
  117.8 10.5 %collective-permute-start.12 = (f32[4,128,128]{2,1,0:T(8,128)S(1)}, f32[4,128,128]{2,1,0:T(8,128)S(1)}, u32[]{:S(2)}, u32[]{:S(2)}) collective-permute-start(f32[4,128,128]{2,1,0:T(8,128)S(1)} %get-tuple-element.7), channel_id=1, source_target_pairs={{0,0},{1,1},{2,2},{3,3},{4,32},{5,33},{6,34},{7,35},{8,8},{9,9},{1... | collective-permute-start | bytes 786440 | tf_op jit(solution)/shard_map/ppermute | solution.py:28
  121.3 8.2 %collective-permute-start.13 = (f32[4,128,128]{2,1,0:T(8,128)S(1)}, f32[4,128,128]{2,1,0:T(8,128)S(1)}, u32[]{:S(2)}, u32[]{:S(2)}) collective-permute-start(f32[4,128,128]{2,1,0:T(8,128)S(1)} %get-tuple-element.8), channel_id=1, source_target_pairs={{0,32},{1,33},{2,34},{3,35},{4,0},{5,1},{6,2},{7,3},{8,40},{9,41},... | collective-permute-start | bytes 786440 | tf_op jit(solution)/shard_map/ppermute | solution.py:28
  121.4 9.5 %collective-permute-start.14 = (f32[4,128,128]{2,1,0:T(8,128)S(1)}, f32[4,128,128]{2,1,0:T(8,128)S(1)}, u32[]{:S(2)}, u32[]{:S(2)}) collective-permute-start(f32[4,128,128]{2,1,0:T(8,128)S(1)} %get-tuple-element.9), channel_id=1, source_target_pairs={{0,64},{1,65},{2,66},{3,67},{4,96},{5,97},{6,98},{7,99},{8,72},{9,... | collective-permute-start | bytes 786440 | tf_op jit(solution)/shard_map/ppermute | solution.py:28
  123.3 12.7 %collective-permute-start.15 = (f32[4,128,128]{2,1,0:T(8,128)S(1)}, f32[4,128,128]{2,1,0:T(8,128)S(1)}, u32[]{:S(2)}, u32[]{:S(2)}) collective-permute-start(f32[4,128,128]{2,1,0:T(8,128)S(1)} %get-tuple-element.10), channel_id=1, source_target_pairs={{0,96},{1,97},{2,98},{3,99},{4,64},{5,65},{6,66},{7,67},{8,104},{9... | collective-permute-start | bytes 786440 | tf_op jit(solution)/shard_map/ppermute | solution.py:28
where the time goes:
time: 138 us; the launch traced here: 137 us
  starting transfers between devices  54.9 us (40%)
  waiting for transfers between devices  46.2 us (33%)
  Pallas kernels  29 us (21%)
  local copies, waits for them, and re-layouts  5.62 us (4%)
    ppermute x16, starting transfers between devices, moved(): return lax.ppermute(array, AXES, pairs)  38.3 us
    ppermute x16, waiting for transfers between devices, moved(): return lax.ppermute(array, AXES, pairs)  28.3 us
    pallas_call x1, Pallas kernels, filtered(): pl.pallas_call(filter_kernel, out_shape=jax.ShapeDtypeStruct((OWN, N, N),...  24.8 us
    all_to_all x1, waiting for transfers between devices, local(): planes = lax.all_to_all(mine, ('x_hi', 'x_lo', 'z'), 0, 0, tiled=True)  14.5 us
    all_to_all x1, starting transfers between devices, local(): rows = lax.all_to_all(rows, AXES, 0, 0, tiled=True)  10.3 us
    all_to_all x1, starting transfers between devices, local(): planes = lax.all_to_all(mine, ('x_hi', 'x_lo', 'z'), 0, 0, tiled=True)  6.31 us
    pallas_call x1, Pallas kernels, rotated_parts(): pl.pallas_call(rotate_kernel, out_shape=[part] * 4 + [jax.ShapeDtypeStruc...  4.15 us
    all_to_all x1, waiting for transfers between devices, local(): rows = lax.all_to_all(rows, AXES, 0, 0, tiled=True)  3.42 us
  transfers between devices with their start and end apart: 18, of which 9 were waited for; matrix products, arithmetic and copies ran while one was open for 1% of the time, Pallas kernels for 0%

commit v1 on v0

v1 whole, which is shorter than its diff:
```python
import jax
import jax.numpy as jnp
import numpy as np
from jax import lax
from jax.experimental import pallas as pl
from jax.experimental.pallas import tpu as pltpu
from jax.sharding import Mesh, PartitionSpec as P

DEGREE = 8
CENTER = 4.5
HALF_WIDTH = 5.0
AXES = ("x_hi", "core", "y", "x_lo", "z")
SIZES = (2, 2, 4, 2, 4)
N = 128
PAD = 8
ROWS = N + 2 * PAD
OWN = 16


def moved(array, where):
    pairs = []
    for i in range(int(np.prod(SIZES))):
        c = dict(zip(AXES, (int(k) for k in np.unravel_index(i, SIZES))))
        d = where(c)
        j = int(np.ravel_multi_index([d[a] % s for a, s in zip(AXES, SIZES)], SIZES))
        pairs.append((i, j))
    return lax.ppermute(array, AXES, pairs)


def to_orbital(shift):
    return lambda c: {**c, "core": c["x_lo"], "x_lo": c["core"], "z": c["z"] + shift}


def to_outer(c):
    return {**c, "core": 1 - c["core"], "y": c["y"] + (1 if c["core"] == 1 else -1)}


def to_sibling(c):
    return {**c, "core": 1 - c["core"]}


def to_home(a, e):
    return lambda c: {
        **c,
        "x_hi": c["x_hi"] ^ a,
        "core": c["x_lo"] ^ e,
        "x_lo": c["core"],
    }


FACTOR = 2.0 / HALF_WIDTH
DIAG = FACTOR * (0.5 * 7.5 - CENTER)
NEAR = FACTOR * (-0.5 * 4.0 / 3.0)
UNIT = NEAR / 16.0


def stencil_matrix():
    m = np.zeros((N, N), np.float32)
    for i in range(N):
        for d, c in ((1, 16.0), (-1, 16.0), (2, -1.0), (-2, -1.0)):
            m[i, (i + d) % N] += c
    return jnp.asarray(np.concatenate([m, m], axis=0), jnp.bfloat16)


def place_blocks(ref, target, first, z, sems, copies):
    for shift in range(4):
        where = first + 4 * lax.rem(z + 4 - shift, 4)
        copies.append(
            pltpu.make_async_copy(
                ref.at[pl.ds(4 * shift, 4)],
                target.at[pl.ds(where, 4), pl.ds(PAD, N), :],
                sems.at[len(copies)],
            )
        )


def wrap_rows(ref, p):
    ref[p, 0:PAD, :] = ref[p, N : N + PAD, :]
    ref[p, N + PAD : ROWS, :] = ref[p, PAD : 2 * PAD, :]


def four_planes(src, dst, pot, along, matrix, p, first_step):
    for k in range(4):
        v = src[p + k, PAD : PAD + N, :]
        high = v.astype(jnp.bfloat16)
        low = (v - high.astype(jnp.float32)).astype(jnp.bfloat16)
        along[k] = jnp.dot(
            jnp.concatenate([high, low], axis=1),
            matrix[...],
            preferred_element_type=jnp.float32,
        )
    for t in range(N // 8):
        r = PAD + 8 * t
        column = [src[p + k - 2, r : r + 8, :] for k in range(8)]
        for k in range(4):
            near = column[k + 1] + column[k + 3]
            far = column[k] + column[k + 4]
            near = near + (src[p + k, r - 1 : r + 7, :] + src[p + k, r + 1 : r + 9, :])
            far = far + (src[p + k, r - 2 : r + 6, :] + src[p + k, r + 2 : r + 10, :])
            sums = (16.0 * near - far) + along[k, 8 * t : 8 * t + 8, :]
            res = pot[p + k, r : r + 8, :] * column[k + 2] + UNIT * sums
            if first_step:
                res = 0.5 * res
            else:
                res = res - dst[p + k, r : r + 8, :]
            dst[p + k, r : r + 8, :] = res
            if t == 0:
                dst[p + k, N + PAD : ROWS, :] = res
            if t == N // 8 - 1:
                dst[p + k, 0:PAD, :] = res


def inner_kernel(
    place, own, sibling, own_pot, sibling_pot, matrix, edges, one, two, pot, along, keep, sems, out_sems
):
    core, z = place[0], place[1]
    copies = []
    place_blocks(own, one, OWN * core, z, sems, copies)
    place_blocks(own_pot, pot, OWN * core, z, sems, copies)
    place_blocks(sibling, one, OWN * (1 - core), z, sems, copies)
    place_blocks(sibling_pot, pot, OWN * (1 - core), z, sems, copies)
    for copy in copies:
        copy.start()
    for copy in copies:
        copy.wait()

    @pl.loop(0, 2 * OWN)
    def _(p):
        wrap_rows(one, p)
        pot[p, PAD : PAD + N, :] = FACTOR * pot[p, PAD : PAD + N, :] + DIAG

    sent = []
    for step in range(DEGREE):
        src, dst = (one, two) if step % 2 == 1 else (two, one)
        if step > 0:

            @pl.loop(0, (2 * OWN - 4 * step) // 4)
            def _(group):
                four_planes(src, dst, pot, along, matrix, 2 * step + 4 * group, step == 1)

        base = 2 * step + core * (28 - 4 * step)

        @pl.loop(0, 4)
        def _(k):
            keep[4 * step + k] = dst[base + k]

        copy = pltpu.make_async_copy(
            keep.at[pl.ds(4 * step, 4)], edges.at[pl.ds(4 * step, 4)], out_sems.at[step]
        )
        copy.start()
        sent.append(copy)
    for copy in sent:
        copy.wait()


def outer_kernel(
    place, outer, outer_pot, own_pot, edges, matrix, out, one, two, pot, along, keep, sems, out_sems
):
    core, z = place[0], place[1]
    copies = []
    place_blocks(outer, one, 18 * core, z, sems, copies)
    place_blocks(outer_pot, pot, 18 * core, z, sems, copies)
    place_blocks(own_pot, pot, 16 - 14 * core, z, sems, copies)
    copies.append(pltpu.make_async_copy(edges, keep, sems.at[len(copies)]))
    for copy in copies:
        copy.start()
    for copy in copies:
        copy.wait()

    @pl.loop(0, OWN)
    def _(p):
        wrap_rows(one, p + 18 * core)

    @pl.loop(2, 2 * OWN)
    def _(p):
        pot[p, PAD : PAD + N, :] = FACTOR * pot[p, PAD : PAD + N, :] + DIAG

    for step in range(1, DEGREE + 1):
        src, dst = (one, two) if step % 2 == 1 else (two, one)
        before = step - 1
        base = 16 + 2 * before - core * (2 + 4 * before)

        @pl.loop(0, 4)
        def _(k):
            src[base + k] = keep[4 * before + k]

        first = 2 * step + core * (18 - 4 * step)

        @pl.loop(0, OWN // 4)
        def _(group):
            four_planes(src, dst, pot, along, matrix, first + 4 * group, step == 1)

    last = one if DEGREE % 2 == 0 else two
    copies = []
    for n in range(OWN):
        q = 4 * (n % 4) + n // 4
        copies.append(
            pltpu.make_async_copy(
                last.at[16 - 14 * core + q, pl.ds(PAD, N), :], out.at[n], out_sems.at[n]
            )
        )
    for copy in copies:
        copy.start()
    for copy in copies:
        copy.wait()


def filter_call(kernel, name, planes, n_in, shape, updates, args):
    anywhere = pl.BlockSpec(memory_space=pl.ANY)
    return pl.pallas_call(
        kernel,
        out_shape=jax.ShapeDtypeStruct(shape, jnp.float32),
        in_specs=[pl.BlockSpec(memory_space=pltpu.SMEM)]
        + [anywhere] * n_in
        + [pl.BlockSpec(memory_space=pltpu.VMEM)],
        out_specs=anywhere,
        scratch_shapes=[pltpu.VMEM((planes, ROWS, N), jnp.float32)] * 3
        + [
            pltpu.VMEM((4, N, N), jnp.float32),
            pltpu.VMEM((4 * DEGREE, ROWS, N), jnp.float32),
            pltpu.SemaphoreType.DMA((16,)),
            pltpu.SemaphoreType.DMA((16,)),
        ],
        compiler_params=pltpu.CompilerParams(vmem_limit_bytes=40 << 20),
        cost_estimate=pl.CostEstimate(flops=updates, bytes_accessed=0, transcendentals=0),
        name=name,
    )(*args, stencil_matrix())


def filtered(place, own, sibling, outer, own_pot, sibling_pot, outer_pot):
    edges = filter_call(
        inner_kernel, "inner", 2 * OWN, 4, (4 * DEGREE, ROWS, N), 112,
        (place, own, sibling, own_pot, sibling_pot),
    )
    return filter_call(
        outer_kernel, "outer", 2 * OWN + 2, 4, (OWN, N, N), 128,
        (place, outer, outer_pot, own_pot, edges),
    )


def rotate_kernel(place, rotation, x, o0, o1, o2, o3):
    outs = (o0, o1, o2, o3)
    for rel in range(4):
        b = place[0] ^ rel

        @pl.loop(0, 4)
        def _(j, rel=rel, b=b):
            coeffs = [rotation[i, 4 * b + j] for i in range(16)]

            @pl.loop(0, 2)
            def _(half):
                rows = [pl.ds(pl.multiple_of(64 * half + 8 * u, 8), 8) for u in range(8)]
                totals = [coeffs[0] * x[0, r, :] for r in rows]
                for i in range(1, 16):
                    totals = [a + coeffs[i] * x[i, r, :] for a, r in zip(totals, rows)]
                for a, r in zip(totals, rows):
                    outs[rel][j, r, :] = a


def rotated_parts(place, rotation, planes):
    vmem = pl.BlockSpec(memory_space=pltpu.VMEM)
    smem = pl.BlockSpec(memory_space=pltpu.SMEM)
    return pl.pallas_call(
        rotate_kernel,
        out_shape=[jax.ShapeDtypeStruct((4, N, N), jnp.float32)] * 4,
        in_specs=[smem, smem, vmem],
        out_specs=[vmem] * 4,
        compiler_params=pltpu.CompilerParams(vmem_limit_bytes=32 << 20),
        name="rotate",
    )(place, rotation, planes)


def gram_kernel(place, o0, o1, o2, o3, out, sums):
    parts = (o0, o1, o2, o3)
    sums[...] = jnp.zeros_like(sums)
    for rel in range(4):
        for j in range(4):
            row = 16 * (4 * (place[0] ^ rel) + j)
            for other in range(rel + 1):
                totals = [jnp.zeros((8, N), jnp.float32) for _ in range(4)]
                for t in range(N // 8):
                    a = parts[rel][j, 8 * t : 8 * t + 8, :]
                    totals = [
                        s + a * parts[other][k, 8 * t : 8 * t + 8, :]
                        for k, s in enumerate(totals)
                    ]
                for k in range(4):
                    total = jnp.sum(totals[k], axis=0, keepdims=True)
                    column = 4 * (place[0] ^ other) + k
                    sums[pl.ds(row + column, 1), :] = total
                    if other < rel:
                        back = 16 * column + 4 * (place[0] ^ rel) + j
                        sums[pl.ds(back, 1), :] = total
    out[...] = lax.dot_general(
        jnp.ones((N, N), jnp.float32),
        sums[...],
        (((1,), (1,)), ((), ())),
        precision=lax.Precision.HIGHEST,
        preferred_element_type=jnp.float32,
    )


def gram_rows(place, parts):
    vmem = pl.BlockSpec(memory_space=pltpu.VMEM)
    smem = pl.BlockSpec(memory_space=pltpu.SMEM)
    return pl.pallas_call(
        gram_kernel,
        out_shape=jax.ShapeDtypeStruct((N, 256), jnp.float32),
        in_specs=[smem] + [vmem] * 4,
        out_specs=vmem,
        scratch_shapes=[pltpu.VMEM((256, N), jnp.float32)],
        compiler_params=pltpu.CompilerParams(vmem_limit_bytes=32 << 20),
        cost_estimate=pl.CostEstimate(
            flops=N * N * 256 * 200, bytes_accessed=2 << 20, transcendentals=0
        ),
        name="gram",
    )(place, *parts)


def local(orbitals, potential, rotation):
    x_hi = lax.axis_index("x_hi")
    core = lax.axis_index("core")
    x_lo = lax.axis_index("x_lo")
    z = lax.axis_index("z")
    place = jnp.stack([core, z]).astype(jnp.int32)
    pots = [moved(potential, to_orbital(s)) for s in range(4)]
    orbs = [
        moved(
            lax.dynamic_index_in_dim(orbitals, (z + s) % 4, 0, keepdims=False), to_orbital(s)
        )
        for s in range(4)
    ]
    own_pot = jnp.concatenate(pots, axis=0)
    own = jnp.concatenate(orbs, axis=0)
    mine = filtered(
        place,
        own,
        moved(own, to_sibling),
        moved(own, to_outer),
        own_pot,
        moved(own_pot, to_sibling),
        moved(own_pot, to_outer),
    )
    planes = lax.all_to_all(mine, ("x_hi", "x_lo", "z"), 0, 0, tiled=True)
    base = jnp.stack([2 * x_hi + x_lo]).astype(jnp.int32)
    parts = rotated_parts(base, rotation, planes)
    home = [moved(parts[2 * a + e], to_home(a, e)) for a in range(2) for e in range(2)]
    parts, home[0] = lax.optimization_barrier((parts, home[0]))
    rows = lax.all_to_all(gram_rows(base, parts), AXES, 0, 0, tiled=True)
    total = jnp.sum(rows, axis=0).reshape(16, 16) / (N * N * N)
    correlation = lax.dynamic_slice_in_dim(total, 4 * (2 * x_hi + core), 4, 0)
    band = 2 * x_hi + core
    pieces = []
    for p in range(4):
        rel = band ^ p
        piece = jnp.where(
            rel < 2,
            jnp.where(rel == 0, home[0], home[1]),
            jnp.where(rel == 2, home[2], home[3]),
        )
        pieces.append(piece)
    return jnp.stack(pieces, axis=1), correlation


def solution(mesh):
    fine = Mesh(mesh.devices.reshape(SIZES), AXES)
    band, dom = ("x_hi", "core"), ("y", "x_lo", "z")
    return jax.shard_map(
        local,
        mesh=fine,
        in_specs=(P(band, dom, None, None), P(dom, None, None), P()),
        out_specs=(P(band, dom, None, None), P(band, None)),
        check_vma=False,
    )
```

time: 138 us -> 129 us (0.935)
  starting transfers between devices: 54.9 us -> 45.4 us
  waiting for transfers between devices: 46.2 us -> 52.4 us
  Pallas kernels: 29 us -> 25 us
  local copies, waits for them, and re-layouts: 5.62 us -> 3.99 us
    ppermute x16, starting transfers between devices: 38.3 us -> 30.5 us  [moved(): return lax.ppermute(array, AXES, pairs)]
    all_to_all x1, waiting for transfers between devices: 3.42 us -> 8.63 us  [local(): rows = lax.all_to_all(gram_rows(base, parts), AXES, 0, 0, tiled=True)]
    pallas_call x2 -> x4, Pallas kernels: 29 us -> 25 us  [the longest x2 21.6 us: filter_call(): pl.pallas_call(kernel, out_shape=jax.ShapeDtypeStruct(shape, jnp.float32)...]
    unnamed x9 -> x13, local copies, waits for them, and re-layouts: 2.91 us -> 1.2 us
    all_to_all x1, starting transfers between devices: 10.3 us -> 8.82 us  [local(): rows = lax.all_to_all(gram_rows(base, parts), AXES, 0, 0, tiled=True)]
  transfers between devices with their start and end apart: 18 -> 18, of which waited for: 9 -> 10; matrix products, arithmetic and copies ran while one was open for 1% -> 2% of each run, Pallas kernels for 0% -> 9%
where the time goes in v1:
time: 129 us; the launch traced here: 128 us
  waiting for transfers between devices  52.4 us (41%)
  starting transfers between devices  45.4 us (35%)
  Pallas kernels  25 us (19%)
  local copies, waits for them, and re-layouts  3.99 us (3%)
    ppermute x16, starting transfers between devices, moved(): return lax.ppermute(array, AXES, pairs)  30.5 us
    ppermute x16, waiting for transfers between devices, moved(): return lax.ppermute(array, AXES, pairs)  28.5 us
    pallas_call x2, Pallas kernels, filter_call(): pl.pallas_call(kernel, out_shape=jax.ShapeDtypeStruct(shape, jnp.float32)...  21.6 us
    all_to_all x1, waiting for transfers between devices, local(): planes = lax.all_to_all(mine, ('x_hi', 'x_lo', 'z'), 0, 0, tiled=True)  15.2 us
    all_to_all x1, starting transfers between devices, local(): rows = lax.all_to_all(gram_rows(base, parts), AXES, 0, 0, tiled=True)  8.82 us
    all_to_all x1, waiting for transfers between devices, local(): rows = lax.all_to_all(gram_rows(base, parts), AXES, 0, 0, tiled=True)  8.63 us
    all_to_all x1, starting transfers between devices, local(): planes = lax.all_to_all(mine, ('x_hi', 'x_lo', 'z'), 0, 0, tiled=True)  6.04 us
  transfers between devices with their start and end apart: 18, of which 10 were waited for; matrix products, arithmetic and copies ran while one was open for 2% of the time, Pallas kernels for 9%

profile of v1, /device:TPU:1, one launch (start us, length us, event | category | flops | bytes accessed | tf_op | source)
XLA Modules:
  0.0 128.2 jit_solution(14318404039441136411)
XLA Ops:
  0.7 1.3 %dynamic-slice_bitcast_fusion = (f32[4,128,128]{2,1,0:T(8,128)S(1)}, f32[4,128,128]{2,1,0:T(8,128)S(1)}, f32[4,128,128]{2,1,0:T(8,128)S(1)}, f32[4,128,128]{2,1,0:T(8,128)S(1)}) fusion(f32[4,4,128,128]{3,2,1,0:T(8,128)} %param.5, s32[]{:T(128)S(6)} %select_n.118, s32[]{:T(128)S(6)} %select_n.114, s32[]{:T(128)S(6)} %select_n.112, s32[]{:T(128)S(6)} %select_n.116), kind=kLoop, calls=%fused_computation.5 | loop fusion | bytes 2097168 | tf_op jit(solution)/shard_map/jit(dynamic_index_in_dim)/squeeze | solution.py:329
  2.0 4.6 %collective-permute-start = (f32[4,128,128]{2,1,0:T(8,128)S(1)}, f32[4,128,128]{2,1,0:T(8,128)S(1)}, u32[]{:S(2)}, u32[]{:S(2)}) collective-permute-start(f32[4,128,128]{2,1,0:T(8,128)S(1)} %get-tuple-element.30), channel_id=1, source_target_pairs={{0,0},{1,1},{2,2},{3,3},{4,32},{5,33},{6,34},{7,35},{8,8},{9,9},{1... | collective-permute-start | bytes 786440 | tf_op jit(solution)/shard_map/ppermute | solution.py:27
  6.7 1.4 %collective-permute-start.1 = (f32[4,128,128]{2,1,0:T(8,128)S(1)}, f32[4,128,128]{2,1,0:T(8,128)S(1)}, u32[]{:S(2)}, u32[]{:S(2)}) collective-permute-start(f32[4,128,128]{2,1,0:T(8,128)S(1)} %get-tuple-element.29), channel_id=1, source_target_pairs={{0,1},{1,2},{2,3},{3,0},{4,33},{5,34},{6,35},{7,32},{8,9},{9,10},{... | collective-permute-start | bytes 786440 | tf_op jit(solution)/shard_map/ppermute | solution.py:27
  8.1 4.8 %collective-permute-start.2 = (f32[4,128,128]{2,1,0:T(8,128)S(1)}, f32[4,128,128]{2,1,0:T(8,128)S(1)}, u32[]{:S(2)}, u32[]{:S(2)}) collective-permute-start(f32[4,128,128]{2,1,0:T(8,128)S(1)} %get-tuple-element.31), channel_id=1, source_target_pairs={{0,2},{1,3},{2,0},{3,1},{4,34},{5,35},{6,32},{7,33},{8,10},{9,11},... | collective-permute-start | bytes 786440 | tf_op jit(solution)/shard_map/ppermute | solution.py:27
  12.8 1.9 %collective-permute-start.5 = (f32[4,128,128]{2,1,0:T(8,128)}, f32[4,128,128]{2,1,0:T(8,128)S(1)}, u32[]{:S(2)}, u32[]{:S(2)}) collective-permute-start(f32[4,128,128]{2,1,0:T(8,128)} %param.6), channel_id=1, source_target_pairs={{0,0},{1,1},{2,2},{3,3},{4,32},{5,33},{6,34},{7,35},{8,8},{9,9},{1... | collective-permute-start | bytes 786440 | tf_op jit(solution)/shard_map/ppermute | solution.py:27
  14.9 3.8 %collective-permute-start.3 = (f32[4,128,128]{2,1,0:T(8,128)S(1)}, f32[4,128,128]{2,1,0:T(8,128)S(1)}, u32[]{:S(2)}, u32[]{:S(2)}) collective-permute-start(f32[4,128,128]{2,1,0:T(8,128)S(1)} %get-tuple-element.28), channel_id=1, source_target_pairs={{0,3},{1,0},{2,1},{3,2},{4,35},{5,32},{6,33},{7,34},{8,11},{9,8},{... | collective-permute-start | bytes 786440 | tf_op jit(solution)/shard_map/ppermute | solution.py:27
  18.9 1.1 collective-permute-done.2
  19.9 1.8 %collective-permute-start.8 = (f32[4,128,128]{2,1,0:T(8,128)S(1)}, f32[4,128,128]{2,1,0:T(8,128)S(1)}, u32[]{:S(2)}, u32[]{:S(2)}) collective-permute-start(f32[4,128,128]{2,1,0:T(8,128)S(1)} %copy-done.2), channel_id=1, source_target_pairs={{0,3},{1,0},{2,1},{3,2},{4,35},{5,32},{6,33},{7,34},{8,11},{9,8},{... | collective-permute-start | bytes 786440 | tf_op jit(solution)/shard_map/ppermute | solution.py:27
  21.7 5.2 %collective-permute-done.3 = f32[4,128,128]{2,1,0:T(8,128)S(1)} collective-permute-done((f32[4,128,128]{2,1,0:T(8,128)S(1)}, f32[4,128,128]{2,1,0:T(8,128)S(1)}, u32[]{:S(2)}, u32[]{:S(2)}) %collective-permute-start.3) | collective-permute-done | bytes 262176 | tf_op jit(solution)/shard_map/ppermute | solution.py:27
  27.1 4.1 %collective-permute-done.7 = f32[4,128,128]{2,1,0:T(8,128)S(1)} collective-permute-done((f32[4,128,128]{2,1,0:T(8,128)S(1)}, f32[4,128,128]{2,1,0:T(8,128)S(1)}, u32[]{:S(2)}, u32[]{:S(2)}) %collective-permute-start.7) | collective-permute-done | bytes 262176 | tf_op jit(solution)/shard_map/ppermute | solution.py:27
  31.3 1.3 %collective-permute-done.8 = f32[4,128,128]{2,1,0:T(8,128)S(1)} collective-permute-done((f32[4,128,128]{2,1,0:T(8,128)S(1)}, f32[4,128,128]{2,1,0:T(8,128)S(1)}, u32[]{:S(2)}, u32[]{:S(2)}) %collective-permute-start.8) | collective-permute-done | bytes 262176 | tf_op jit(solution)/shard_map/ppermute | solution.py:27
  32.6 3.2 %collective-permute-start.11 = (f32[16,128,128]{2,1,0:T(8,128)S(1)}, f32[16,128,128]{2,1,0:T(8,128)}, u32[]{:S(2)}, u32[]{:S(2)}) collective-permute-start(f32[16,128,128]{2,1,0:T(8,128)S(1)} %constant_dynamic-update-slice_fusion.4.own_pot), channel_id=1, source_target_pairs={{0,32},{1,33},{2,34},{3,35},{4,36},{5,37},{6,38},{7,39},{8,40},{9,... | collective-permute-start | bytes 3145736 | tf_op jit(solution)/shard_map/ppermute | solution.py:27
  35.9 1.3 collective-permute-start.4
  37.1 0.5 collective-permute-start.9
  37.7 0.6 collective-permute-done.11.sibling_pot
  38.3 10.0 %inner.1.edges = f32[32,144,128]{2,1,0:T(8,128)S(1)} custom-call(s32[2]{0:T(128)S(1)} %pad_add_fusion.place, f32[16,128,128]{2,1,0:T(8,128)S(1)} %constant_dynamic-update-slice_fusion.own, f32[16,128,128]{2,1,0:T(8,128)S(1)} %collective-permute-done.10.sibling, f32[16,128,128]{2,1,0:T(8,128)S(1)} %constant_dynamic-update-slice_fusion.4.own_pot, ...), custom_call_target="tpu_custom_call" | custom-call | flops 112 | tf_op jit(solution)/shard_map/inner/pallas_call | solution.py:210
  48.3 2.2 %collective-permute-done.4.outer = f32[16,128,128]{2,1,0:T(8,128)} collective-permute-done((f32[16,128,128]{2,1,0:T(8,128)S(1)}, f32[16,128,128]{2,1,0:T(8,128)}, u32[]{:S(2)}, u32[]{:S(2)}) %collective-permute-start.4) | collective-permute-done | bytes 1048608 | tf_op jit(solution)/shard_map/ppermute | solution.py:27
  50.5 11.2 %collective-permute-done.9.outer_pot = f32[16,128,128]{2,1,0:T(8,128)} collective-permute-done((f32[16,128,128]{2,1,0:T(8,128)S(1)}, f32[16,128,128]{2,1,0:T(8,128)}, u32[]{:S(2)}, u32[]{:S(2)}) %collective-permute-start.9) | collective-permute-done | bytes 1048608 | tf_op jit(solution)/shard_map/ppermute | solution.py:27
  61.7 11.5 %outer.1 = f32[16,128,128]{2,1,0:T(8,128)} custom-call(s32[2]{0:T(128)S(1)} %pad_add_fusion.place, f32[16,128,128]{2,1,0:T(8,128)} %collective-permute-done.4.outer, f32[16,128,128]{2,1,0:T(8,128)} %collective-permute-done.9.outer_pot, f32[16,128,128]{2,1,0:T(8,128)S(1)} %constant_dynamic-update-slice_fusion.4.own_pot, f32[32,144,128]{2,1,0:T(8,128)S(1)} %inner.1.edges, ...), custom_call_target="tpu_custom_call" | custom-call | flops 128 | tf_op jit(solution)/shard_map/outer/pallas_call | solution.py:210
  73.3 6.0 %all-to-all-start = ((f32[16,128,128]{2,1,0:T(8,128)}), f32[16,128,128]{2,1,0:T(8,128)S(1)}, u32[]{:S(2)}, u32[]{:S(2)}) async-start(f32[16,128,128]{2,1,0:T(8,128)} %outer.1), calls=%async_computation | async-start | bytes 2097152 | tf_op jit(solution)/shard_map/all_to_all | solution.py:344
  79.3 15.2 %all-to-all-done.x = f32[16,128,128]{2,1,0:T(8,128)S(1)} async-done(((f32[16,128,128]{2,1,0:T(8,128)}), f32[16,128,128]{2,1,0:T(8,128)S(1)}, u32[]{:S(2)}, u32[]{:S(2)}) %all-to-all-start) | async-done | bytes 1048608 | tf_op jit(solution)/shard_map/all_to_all | solution.py:344
  94.5 2.4 %rotate.1 = (f32[4,128,128]{2,1,0:T(8,128)S(1)}, f32[4,128,128]{2,1,0:T(8,128)S(1)}, f32[4,128,128]{2,1,0:T(8,128)S(1)}, f32[4,128,128]{2,1,0:T(8,128)S(1)}) custom-call(s32[1]{0:T(128)} %bitcast.place, f32[16,16]{1,0:T(8,128)S(1)} %copy-done.1, f32[16,128,128]{2,1,0:T(8,128)S(1)} %all-to-all-done.x), custom_call_target="tpu_custom_call" | custom-call | tf_op jit(solution)/shard_map/rotate/pallas_call | solution.py:263
  97.0 4.4 %collective-permute-start.12 = (f32[4,128,128]{2,1,0:T(8,128)S(1)}, f32[4,128,128]{2,1,0:T(8,128)S(1)}, u32[]{:S(2)}, u32[]{:S(2)}) collective-permute-start(f32[4,128,128]{2,1,0:T(8,128)S(1)} %get-tuple-element.16.o0), channel_id=1, source_target_pairs={{0,0},{1,1},{2,2},{3,3},{4,32},{5,33},{6,34},{7,35},{8,8},{9,9},{1... | collective-permute-start | bytes 786440 | tf_op jit(solution)/shard_map/ppermute | solution.py:27
  101.5 1.3 %collective-permute-start.14 = (f32[4,128,128]{2,1,0:T(8,128)S(1)}, f32[4,128,128]{2,1,0:T(8,128)S(1)}, u32[]{:S(2)}, u32[]{:S(2)}) collective-permute-start(f32[4,128,128]{2,1,0:T(8,128)S(1)} %get-tuple-element.18.o2), channel_id=1, source_target_pairs={{0,64},{1,65},{2,66},{3,67},{4,96},{5,97},{6,98},{7,99},{8,72},{9,... | collective-permute-start | bytes 786440 | tf_op jit(solution)/shard_map/ppermute | solution.py:27
  102.8 1.2 collective-permute-start.15
  104.0 2.8 %collective-permute-done.12 = f32[4,128,128]{2,1,0:T(8,128)S(1)} collective-permute-done((f32[4,128,128]{2,1,0:T(8,128)S(1)}, f32[4,128,128]{2,1,0:T(8,128)S(1)}, u32[]{:S(2)}, u32[]{:S(2)}) %collective-permute-start.12) | collective-permute-done | bytes 262176 | tf_op jit(solution)/shard_map/ppermute | solution.py:27
  106.7 1.1 gram.1
  107.8 0.8 copy.8
  108.6 8.8 %all-to-all-start.1 = ((f32[128,1,256]{2,1,0:T(1,128)}), f32[128,1,256]{2,1,0:T(1,128)S(1)}, u32[]{:S(2)}, u32[]{:S(2)}) async-start(f32[128,1,256]{2,1,0:T(1,128)} %copy.8), calls=%async_computation.1 | async-start | bytes 262144 | tf_op jit(solution)/shard_map/all_to_all | solution.py:349
  117.7 1.1 copy.9
  118.8 8.6 %all-to-all-done.1 = f32[128,1,256]{2,1,0:T(1,128)S(1)} async-done(((f32[128,1,256]{2,1,0:T(1,128)}), f32[128,1,256]{2,1,0:T(1,128)S(1)}, u32[]{:S(2)}, u32[]{:S(2)}) %all-to-all-start.1) | async-done | bytes 131104 | tf_op jit(solution)/shard_map/all_to_all | solution.py:349
  127.7 0.6 constant_dynamic-slice_fusion
  (32 shorter events, 1.1 us)
Async XLA Ops:
  0.6 18.1 %copy-start.2 = (f32[4,128,128]{2,1,0:T(8,128)S(1)}, f32[4,128,128]{2,1,0:T(8,128)}, u32[]{:S(2)}) copy-start(f32[4,128,128]{2,1,0:T(8,128)} %param.6) | copy-start | bytes 786436
  2.0 36.3 %copy-start = (bf16[256,128]{1,0:T(8,128)(2,1)S(1)}, bf16[256,128]{1,0:T(8,128)(2,1)}, u32[]{:S(2)}) copy-start(bf16[256,128]{1,0:T(8,128)(2,1)} %constant.67.clone.matrix) | copy-start | bytes 196612
  2.0 12.8 %collective-permute-start = (f32[4,128,128]{2,1,0:T(8,128)S(1)}, f32[4,128,128]{2,1,0:T(8,128)S(1)}, u32[]{:S(2)}, u32[]{:S(2)}) collective-permute-start(f32[4,128,128]{2,1,0:T(8,128)S(1)} %get-tuple-element.30), channel_id=1, source_target_pairs={{0,0},{1,1},{2,2},{3,3},{4,32},{5,33},{6,34},{7,35},{8,8},{9,9},{1... | collective-permute-start | bytes 786440 | tf_op jit(solution)/shard_map/ppermute | solution.py:27
  6.7 12.1 %collective-permute-start.1 = (f32[4,128,128]{2,1,0:T(8,128)S(1)}, f32[4,128,128]{2,1,0:T(8,128)S(1)}, u32[]{:S(2)}, u32[]{:S(2)}) collective-permute-start(f32[4,128,128]{2,1,0:T(8,128)S(1)} %get-tuple-element.29), channel_id=1, source_target_pairs={{0,1},{1,2},{2,3},{3,0},{4,33},{5,34},{6,35},{7,32},{8,9},{9,10},{... | collective-permute-start | bytes 786440 | tf_op jit(solution)/shard_map/ppermute | solution.py:27
  8.1 11.8 %collective-permute-start.2 = (f32[4,128,128]{2,1,0:T(8,128)S(1)}, f32[4,128,128]{2,1,0:T(8,128)S(1)}, u32[]{:S(2)}, u32[]{:S(2)}) collective-permute-start(f32[4,128,128]{2,1,0:T(8,128)S(1)} %get-tuple-element.31), channel_id=1, source_target_pairs={{0,2},{1,3},{2,0},{3,1},{4,34},{5,35},{6,32},{7,33},{8,10},{9,11},... | collective-permute-start | bytes 786440 | tf_op jit(solution)/shard_map/ppermute | solution.py:27
  12.8 14.2 %collective-permute-start.5 = (f32[4,128,128]{2,1,0:T(8,128)}, f32[4,128,128]{2,1,0:T(8,128)S(1)}, u32[]{:S(2)}, u32[]{:S(2)}) collective-permute-start(f32[4,128,128]{2,1,0:T(8,128)} %param.6), channel_id=1, source_target_pairs={{0,0},{1,1},{2,2},{3,3},{4,32},{5,33},{6,34},{7,35},{8,8},{9,9},{1... | collective-permute-start | bytes 786440 | tf_op jit(solution)/shard_map/ppermute | solution.py:27
  14.8 12.3 %collective-permute-start.6 = (f32[4,128,128]{2,1,0:T(8,128)}, f32[4,128,128]{2,1,0:T(8,128)S(1)}, u32[]{:S(2)}, u32[]{:S(2)}) collective-permute-start(f32[4,128,128]{2,1,0:T(8,128)} %param.6), channel_id=1, source_target_pairs={{0,1},{1,2},{2,3},{3,0},{4,33},{5,34},{6,35},{7,32},{8,9},{9,10},{... | collective-permute-start | bytes 786440 | tf_op jit(solution)/shard_map/ppermute | solution.py:27
  14.9 12.1 %collective-permute-start.3 = (f32[4,128,128]{2,1,0:T(8,128)S(1)}, f32[4,128,128]{2,1,0:T(8,128)S(1)}, u32[]{:S(2)}, u32[]{:S(2)}) collective-permute-start(f32[4,128,128]{2,1,0:T(8,128)S(1)} %get-tuple-element.28), channel_id=1, source_target_pairs={{0,3},{1,0},{2,1},{3,2},{4,35},{5,32},{6,33},{7,34},{8,11},{9,8},{... | collective-permute-start | bytes 786440 | tf_op jit(solution)/shard_map/ppermute | solution.py:27
  18.7 12.5 %collective-permute-start.7 = (f32[4,128,128]{2,1,0:T(8,128)S(1)}, f32[4,128,128]{2,1,0:T(8,128)S(1)}, u32[]{:S(2)}, u32[]{:S(2)}) collective-permute-start(f32[4,128,128]{2,1,0:T(8,128)S(1)} %copy-done.2), channel_id=1, source_target_pairs={{0,2},{1,3},{2,0},{3,1},{4,34},{5,35},{6,32},{7,33},{8,10},{9,11},... | collective-permute-start | bytes 786440 | tf_op jit(solution)/shard_map/ppermute | solution.py:27
  19.9 12.7 %collective-permute-start.8 = (f32[4,128,128]{2,1,0:T(8,128)S(1)}, f32[4,128,128]{2,1,0:T(8,128)S(1)}, u32[]{:S(2)}, u32[]{:S(2)}) collective-permute-start(f32[4,128,128]{2,1,0:T(8,128)S(1)} %copy-done.2), channel_id=1, source_target_pairs={{0,3},{1,0},{2,1},{3,2},{4,35},{5,32},{6,33},{7,34},{8,11},{9,8},{... | collective-permute-start | bytes 786440 | tf_op jit(solution)/shard_map/ppermute | solution.py:27
  27.0 10.7 %collective-permute-start.10 = (f32[16,128,128]{2,1,0:T(8,128)S(1)}, f32[16,128,128]{2,1,0:T(8,128)S(1)}, u32[]{:S(2)}, u32[]{:S(2)}) collective-permute-start(f32[16,128,128]{2,1,0:T(8,128)S(1)} %constant_dynamic-update-slice_fusion.own), channel_id=1, source_target_pairs={{0,32},{1,33},{2,34},{3,35},{4,36},{5,37},{6,38},{7,39},{8,40},{9,... | collective-permute-start | bytes 3145736 | tf_op jit(solution)/shard_map/ppermute | solution.py:27
  32.6 5.7 %collective-permute-start.11 = (f32[16,128,128]{2,1,0:T(8,128)S(1)}, f32[16,128,128]{2,1,0:T(8,128)}, u32[]{:S(2)}, u32[]{:S(2)}) collective-permute-start(f32[16,128,128]{2,1,0:T(8,128)S(1)} %constant_dynamic-update-slice_fusion.4.own_pot), channel_id=1, source_target_pairs={{0,32},{1,33},{2,34},{3,35},{4,36},{5,37},{6,38},{7,39},{8,40},{9,... | collective-permute-start | bytes 3145736 | tf_op jit(solution)/shard_map/ppermute | solution.py:27
  35.9 14.6 %collective-permute-start.4 = (f32[16,128,128]{2,1,0:T(8,128)S(1)}, f32[16,128,128]{2,1,0:T(8,128)}, u32[]{:S(2)}, u32[]{:S(2)}) collective-permute-start(f32[16,128,128]{2,1,0:T(8,128)S(1)} %constant_dynamic-update-slice_fusion.own), channel_id=1, source_target_pairs={{0,56},{1,57},{2,58},{3,59},{4,60},{5,61},{6,62},{7,63},{8,32},{9,... | collective-permute-start | bytes 3145736 | tf_op jit(solution)/shard_map/ppermute | solution.py:27
  37.1 24.6 %collective-permute-start.9 = (f32[16,128,128]{2,1,0:T(8,128)S(1)}, f32[16,128,128]{2,1,0:T(8,128)}, u32[]{:S(2)}, u32[]{:S(2)}) collective-permute-start(f32[16,128,128]{2,1,0:T(8,128)S(1)} %constant_dynamic-update-slice_fusion.4.own_pot), channel_id=1, source_target_pairs={{0,56},{1,57},{2,58},{3,59},{4,60},{5,61},{6,62},{7,63},{8,32},{9,... | collective-permute-start | bytes 3145736 | tf_op jit(solution)/shard_map/ppermute | solution.py:27
  48.3 46.2 %copy-start.1 = (f32[16,16]{1,0:T(8,128)S(1)}, f32[16,16]{1,0:T(8,128)}, u32[]{:S(2)}) copy-start(f32[16,16]{1,0:T(8,128)} %rotation.1) | copy-start | bytes 3076
  73.3 21.3 %all-to-all-start = ((f32[16,128,128]{2,1,0:T(8,128)}), f32[16,128,128]{2,1,0:T(8,128)S(1)}, u32[]{:S(2)}, u32[]{:S(2)}) async-start(f32[16,128,128]{2,1,0:T(8,128)} %outer.1), calls=%async_computation | async-start | bytes 2097152 | tf_op jit(solution)/shard_map/all_to_all | solution.py:344
  97.0 9.8 %collective-permute-start.12 = (f32[4,128,128]{2,1,0:T(8,128)S(1)}, f32[4,128,128]{2,1,0:T(8,128)S(1)}, u32[]{:S(2)}, u32[]{:S(2)}) collective-permute-start(f32[4,128,128]{2,1,0:T(8,128)S(1)} %get-tuple-element.16.o0), channel_id=1, source_target_pairs={{0,0},{1,1},{2,2},{3,3},{4,32},{5,33},{6,34},{7,35},{8,8},{9,9},{1... | collective-permute-start | bytes 786440 | tf_op jit(solution)/shard_map/ppermute | solution.py:27
  101.4 16.0 %collective-permute-start.13 = (f32[4,128,128]{2,1,0:T(8,128)S(1)}, f32[4,128,128]{2,1,0:T(8,128)S(1)}, u32[]{:S(2)}, u32[]{:S(2)}) collective-permute-start(f32[4,128,128]{2,1,0:T(8,128)S(1)} %get-tuple-element.17.o1), channel_id=1, source_target_pairs={{0,32},{1,33},{2,34},{3,35},{4,0},{5,1},{6,2},{7,3},{8,40},{9,41},... | collective-permute-start | bytes 786440 | tf_op jit(solution)/shard_map/ppermute | solution.py:27
  101.5 16.0 %collective-permute-start.14 = (f32[4,128,128]{2,1,0:T(8,128)S(1)}, f32[4,128,128]{2,1,0:T(8,128)S(1)}, u32[]{:S(2)}, u32[]{:S(2)}) collective-permute-start(f32[4,128,128]{2,1,0:T(8,128)S(1)} %get-tuple-element.18.o2), channel_id=1, source_target_pairs={{0,64},{1,65},{2,66},{3,67},{4,96},{5,97},{6,98},{7,99},{8,72},{9,... | collective-permute-start | bytes 786440 | tf_op jit(solution)/shard_map/ppermute | solution.py:27
  102.8 14.7 %collective-permute-start.15 = (f32[4,128,128]{2,1,0:T(8,128)S(1)}, f32[4,128,128]{2,1,0:T(8,128)S(1)}, u32[]{:S(2)}, u32[]{:S(2)}) collective-permute-start(f32[4,128,128]{2,1,0:T(8,128)S(1)} %get-tuple-element.19.o3), channel_id=1, source_target_pairs={{0,96},{1,97},{2,98},{3,99},{4,64},{5,65},{6,66},{7,67},{8,104},{9... | collective-permute-start | bytes 786440 | tf_op jit(solution)/shard_map/ppermute | solution.py:27
  108.6 18.8 %all-to-all-start.1 = ((f32[128,1,256]{2,1,0:T(1,128)}), f32[128,1,256]{2,1,0:T(1,128)S(1)}, u32[]{:S(2)}, u32[]{:S(2)}) async-start(f32[128,1,256]{2,1,0:T(1,128)} %copy.8), calls=%async_computation.1 | async-start | bytes 262144 | tf_op jit(solution)/shard_map/all_to_all | solution.py:349

commit v2 on v1

--- a/solution.py
+++ b/solution.py
@@ -1,3 +1,5 @@
+import functools
+
 import jax
 import jax.numpy as jnp
 import numpy as np
@@ -111,7 +113,7 @@
 
 
 def inner_kernel(
-    place, own, sibling, own_pot, sibling_pot, matrix, edges, one, two, pot, along, keep, sems, out_sems
+    place, own, sibling, own_pot, sibling_pot, matrix, edges, one, two, pot, along, sems
 ):
     core, z = place[0], place[1]
     copies = []
@@ -127,9 +129,7 @@
     @pl.loop(0, 2 * OWN)
     def _(p):
         wrap_rows(one, p)
-        pot[p, PAD : PAD + N, :] = FACTOR * pot[p, PAD : PAD + N, :] + DIAG
-
-    sent = []
+
     for step in range(DEGREE):
         src, dst = (one, two) if step % 2 == 1 else (two, one)
         if step > 0:
@@ -142,26 +142,17 @@
 
         @pl.loop(0, 4)
         def _(k):
-            keep[4 * step + k] = dst[base + k]
-
-        copy = pltpu.make_async_copy(
-            keep.at[pl.ds(4 * step, 4)], edges.at[pl.ds(4 * step, 4)], out_sems.at[step]
-        )
-        copy.start()
-        sent.append(copy)
-    for copy in sent:
-        copy.wait()
+            edges[4 * step + k] = dst[base + k]
 
 
 def outer_kernel(
-    place, outer, outer_pot, own_pot, edges, matrix, out, one, two, pot, along, keep, sems, out_sems
+    place, outer, outer_pot, own_pot, edges, matrix, out, one, two, pot, along, sems
 ):
     core, z = place[0], place[1]
     copies = []
     place_blocks(outer, one, 18 * core, z, sems, copies)
     place_blocks(outer_pot, pot, 18 * core, z, sems, copies)
     place_blocks(own_pot, pot, 16 - 14 * core, z, sems, copies)
-    copies.append(pltpu.make_async_copy(edges, keep, sems.at[len(copies)]))
     for copy in copies:
         copy.start()
     for copy in copies:
@@ -170,10 +161,6 @@
     @pl.loop(0, OWN)
     def _(p):
         wrap_rows(one, p + 18 * core)
-
-    @pl.loop(2, 2 * OWN)
-    def _(p):
-        pot[p, PAD : PAD + N, :] = FACTOR * pot[p, PAD : PAD + N, :] + DIAG
 
     for step in range(1, DEGREE + 1):
         src, dst = (one, two) if step % 2 == 1 else (two, one)
@@ -182,7 +169,7 @@
 
         @pl.loop(0, 4)
         def _(k):
-            src[base + k] = keep[4 * before + k]
+            src[base + k] = edges[4 * before + k]
 
         first = 2 * step + core * (18 - 4 * step)
 
@@ -196,7 +183,7 @@
         q = 4 * (n % 4) + n // 4
         copies.append(
             pltpu.make_async_copy(
-                last.at[16 - 14 * core + q, pl.ds(PAD, N), :], out.at[n], out_sems.at[n]
+                last.at[16 - 14 * core + q, pl.ds(PAD, N), :], out.at[n], sems.at[n]
             )
         )
     for copy in copies:
@@ -205,46 +192,39 @@
         copy.wait()
 
 
-def filter_call(kernel, name, planes, n_in, shape, updates, args):
-    anywhere = pl.BlockSpec(memory_space=pl.ANY)
+def filter_call(kernel, name, planes, places, shape, place_out, args):
     return pl.pallas_call(
         kernel,
         out_shape=jax.ShapeDtypeStruct(shape, jnp.float32),
         in_specs=[pl.BlockSpec(memory_space=pltpu.SMEM)]
-        + [anywhere] * n_in
+        + [pl.BlockSpec(memory_space=m) for m in places]
         + [pl.BlockSpec(memory_space=pltpu.VMEM)],
-        out_specs=anywhere,
+        out_specs=pl.BlockSpec(memory_space=place_out),
         scratch_shapes=[pltpu.VMEM((planes, ROWS, N), jnp.float32)] * 3
-        + [
-            pltpu.VMEM((4, N, N), jnp.float32),
-            pltpu.VMEM((4 * DEGREE, ROWS, N), jnp.float32),
-            pltpu.SemaphoreType.DMA((16,)),
-            pltpu.SemaphoreType.DMA((16,)),
-        ],
+        + [pltpu.VMEM((4, N, N), jnp.float32), pltpu.SemaphoreType.DMA((16,))],
         compiler_params=pltpu.CompilerParams(vmem_limit_bytes=40 << 20),
-        cost_estimate=pl.CostEstimate(flops=updates, bytes_accessed=0, transcendentals=0),
+        cost_estimate=pl.CostEstimate(flops=1000, bytes_accessed=0, transcendentals=0),
         name=name,
     )(*args, stencil_matrix())
 
 
 def filtered(place, own, sibling, outer, own_pot, sibling_pot, outer_pot):
     edges = filter_call(
-        inner_kernel, "inner", 2 * OWN, 4, (4 * DEGREE, ROWS, N), 112,
+        inner_kernel, "inner", 2 * OWN, [pl.ANY] * 4, (4 * DEGREE, ROWS, N), pltpu.VMEM,
         (place, own, sibling, own_pot, sibling_pot),
     )
     return filter_call(
-        outer_kernel, "outer", 2 * OWN + 2, 4, (OWN, N, N), 128,
+        outer_kernel, "outer", 2 * OWN + 2, [pl.ANY] * 3 + [pltpu.VMEM], (OWN, N, N), pl.ANY,
         (place, outer, outer_pot, own_pot, edges),
     )
 
 
-def rotate_kernel(place, rotation, x, o0, o1, o2, o3):
-    outs = (o0, o1, o2, o3)
-    for rel in range(4):
-        b = place[0] ^ rel
+def rotate_kernel(first, place, rotation, x, *outs):
+    for n, out in enumerate(outs):
+        b = place[0] ^ (first + n)
 
         @pl.loop(0, 4)
-        def _(j, rel=rel, b=b):
+        def _(j, out=out, b=b):
             coeffs = [rotation[i, 4 * b + j] for i in range(16)]
 
             @pl.loop(0, 2)
@@ -254,17 +234,17 @@
                 for i in range(1, 16):
                     totals = [a + coeffs[i] * x[i, r, :] for a, r in zip(totals, rows)]
                 for a, r in zip(totals, rows):
-                    outs[rel][j, r, :] = a
-
-
-def rotated_parts(place, rotation, planes):
+                    out[j, r, :] = a
+
+
+def rotated_parts(first, place, rotation, planes):
     vmem = pl.BlockSpec(memory_space=pltpu.VMEM)
     smem = pl.BlockSpec(memory_space=pltpu.SMEM)
     return pl.pallas_call(
-        rotate_kernel,
-        out_shape=[jax.ShapeDtypeStruct((4, N, N), jnp.float32)] * 4,
+        functools.partial(rotate_kernel, first),
+        out_shape=[jax.ShapeDtypeStruct((4, N, N), jnp.float32)] * 2,
         in_specs=[smem, smem, vmem],
-        out_specs=[vmem] * 4,
+        out_specs=[vmem] * 2,
         compiler_params=pltpu.CompilerParams(vmem_limit_bytes=32 << 20),
         name="rotate",
     )(place, rotation, planes)
@@ -292,7 +272,7 @@
                         back = 16 * column + 4 * (place[0] ^ rel) + j
                         sums[pl.ds(back, 1), :] = total
     out[...] = lax.dot_general(
-        jnp.ones((N, N), jnp.float32),
+        jnp.ones((8, N), jnp.float32),
         sums[...],
         (((1,), (1,)), ((), ())),
         precision=lax.Precision.HIGHEST,
@@ -305,14 +285,11 @@
     smem = pl.BlockSpec(memory_space=pltpu.SMEM)
     return pl.pallas_call(
         gram_kernel,
-        out_shape=jax.ShapeDtypeStruct((N, 256), jnp.float32),
+        out_shape=jax.ShapeDtypeStruct((8, 256), jnp.float32),
         in_specs=[smem] + [vmem] * 4,
         out_specs=vmem,
         scratch_shapes=[pltpu.VMEM((256, N), jnp.float32)],
         compiler_params=pltpu.CompilerParams(vmem_limit_bytes=32 << 20),
-        cost_estimate=pl.CostEstimate(
-            flops=N * N * 256 * 200, bytes_accessed=2 << 20, transcendentals=0
-        ),
         name="gram",
     )(place, *parts)
 
@@ -323,31 +300,33 @@
     x_lo = lax.axis_index("x_lo")
     z = lax.axis_index("z")
     place = jnp.stack([core, z]).astype(jnp.int32)
-    pots = [moved(potential, to_orbital(s)) for s in range(4)]
     orbs = [
         moved(
             lax.dynamic_index_in_dim(orbitals, (z + s) % 4, 0, keepdims=False), to_orbital(s)
         )
         for s in range(4)
     ]
+    diagonal = FACTOR * potential + DIAG
+    pots = [moved(diagonal, to_orbital(s)) for s in range(4)]
+    own = jnp.concatenate(orbs, axis=0)
     own_pot = jnp.concatenate(pots, axis=0)
-    own = jnp.concatenate(orbs, axis=0)
-    mine = filtered(
-        place,
-        own,
-        moved(own, to_sibling),
-        moved(own, to_outer),
-        own_pot,
-        moved(own_pot, to_sibling),
-        moved(own_pot, to_outer),
-    )
+    outer = moved(own, to_outer)
+    sibling = moved(own, to_sibling)
+    outer_pot = moved(own_pot, to_outer)
+    sibling_pot = moved(own_pot, to_sibling)
+    sibling, outer = lax.optimization_barrier((sibling, outer))
+    mine = filtered(place, own, sibling, outer, own_pot, sibling_pot, outer_pot)
     planes = lax.all_to_all(mine, ("x_hi", "x_lo", "z"), 0, 0, tiled=True)
     base = jnp.stack([2 * x_hi + x_lo]).astype(jnp.int32)
-    parts = rotated_parts(base, rotation, planes)
-    home = [moved(parts[2 * a + e], to_home(a, e)) for a in range(2) for e in range(2)]
-    parts, home[0] = lax.optimization_barrier((parts, home[0]))
-    rows = lax.all_to_all(gram_rows(base, parts), AXES, 0, 0, tiled=True)
-    total = jnp.sum(rows, axis=0).reshape(16, 16) / (N * N * N)
+    far = rotated_parts(2, base, rotation, planes)
+    near = rotated_parts(0, base, rotation, planes)
+    home = [None] * 4
+    home[2], home[3] = moved(far[0], to_home(1, 0)), moved(far[1], to_home(1, 1))
+    home[0], home[1] = moved(near[0], to_home(0, 0)), moved(near[1], to_home(0, 1))
+    total = gram_rows(base, [*near, *far])
+    for axis, bit in (("z", 1), ("z", 2), ("y", 1), ("y", 2), ("core", 1), ("x_lo", 1), ("x_hi", 1)):
+        total = total + moved(total, lambda c: {**c, axis: c[axis] ^ bit})
+    total = total[0].reshape(16, 16) / (N * N * N)
     correlation = lax.dynamic_slice_in_dim(total, 4 * (2 * x_hi + core), 4, 0)
     band = 2 * x_hi + core
     pieces = []

time: 129 us -> 126 us (0.977)
  waiting for transfers between devices: 52.4 us -> 43.7 us
  starting transfers between devices: 45.4 us -> 51.8 us
    ppermute x16 -> x23, starting transfers between devices: 30.5 us -> 45.1 us  [moved(): return lax.ppermute(array, AXES, pairs)]
    all_to_all x1 -> x0, starting transfers between devices: 8.82 us -> none  [local(): rows = lax.all_to_all(gram_rows(base, parts), AXES, 0, 0, tiled=True)]
    all_to_all x1 -> x0, waiting for transfers between devices: 8.63 us -> none  [local(): rows = lax.all_to_all(gram_rows(base, parts), AXES, 0, 0, tiled=True)]
    pallas_call x2, Pallas kernels: 21.6 us -> 20.2 us  [filter_call(): pl.pallas_call(kernel, out_shape=jax.ShapeDtypeStruct(shape, jnp.float32)...]
    pallas_call x2 -> x3, Pallas kernels: 3.48 us -> 4.07 us  [the longest x2 3.1 us: rotated_parts(): pl.pallas_call(functools.partial(rotate_kernel, first), out_shape=[jax.Sh...]
    ppermute x16 -> x23, waiting for transfers between devices: 28.5 us -> 28.5 us  [moved(): return lax.ppermute(array, AXES, pairs)]
  transfers between devices with their start and end apart: 18 -> 24, of which waited for: 10 -> 13; matrix products, arithmetic and copies ran while one was open for 2% -> 1% of each run, Pallas kernels for 9% -> 7%
where the time goes in v2:
time: 126 us; the launch traced here: 124 us
  starting transfers between devices  51.8 us (41%)
  waiting for transfers between devices  43.7 us (35%)
  Pallas kernels  24.2 us (19%)
  local copies, waits for them, and re-layouts  3.2 us (3%)
    ppermute x23, starting transfers between devices, moved(): return lax.ppermute(array, AXES, pairs)  45.1 us
    ppermute x23, waiting for transfers between devices, moved(): return lax.ppermute(array, AXES, pairs)  28.5 us
    pallas_call x2, Pallas kernels, filter_call(): pl.pallas_call(kernel, out_shape=jax.ShapeDtypeStruct(shape, jnp.float32)...  20.2 us
    all_to_all x1, waiting for transfers between devices, local(): planes = lax.all_to_all(mine, ('x_hi', 'x_lo', 'z'), 0, 0, tiled=True)  15.2 us
    all_to_all x1, starting transfers between devices, local(): planes = lax.all_to_all(mine, ('x_hi', 'x_lo', 'z'), 0, 0, tiled=True)  6.71 us
    pallas_call x2, Pallas kernels, rotated_parts(): pl.pallas_call(functools.partial(rotate_kernel, first), out_shape=[jax.Sh...  3.1 us
  transfers between devices with their start and end apart: 24, of which 13 were waited for; matrix products, arithmetic and copies ran while one was open for 1% of the time, Pallas kernels for 7%

profile of v2, /device:TPU:1, one launch (start us, length us, event | category | flops | bytes accessed | tf_op | source)
XLA Modules:
  0.0 124.3 jit_solution(4445052119624114380)
XLA Ops:
  0.7 1.3 %dynamic-slice_bitcast_fusion = (f32[4,128,128]{2,1,0:T(8,128)S(1)}, f32[4,128,128]{2,1,0:T(8,128)S(1)}, f32[4,128,128]{2,1,0:T(8,128)S(1)}, f32[4,128,128]{2,1,0:T(8,128)S(1)}) fusion(f32[4,4,128,128]{3,2,1,0:T(8,128)} %param.5, s32[]{:T(128)S(6)} %select_n.118, s32[]{:T(128)S(6)} %select_n.114, s32[]{:T(128)S(6)} %select_n.112, s32[]{:T(128)S(6)} %select_n.116), kind=kLoop, calls=%fused_computation.6 | loop fusion | bytes 2097168 | tf_op jit(solution)/shard_map/jit(dynamic_index_in_dim)/squeeze | solution.py:305
  2.0 4.5 %collective-permute-start = (f32[4,128,128]{2,1,0:T(8,128)S(1)}, f32[4,128,128]{2,1,0:T(8,128)S(1)}, u32[]{:S(2)}, u32[]{:S(2)}) collective-permute-start(f32[4,128,128]{2,1,0:T(8,128)S(1)} %get-tuple-element.22), channel_id=1, source_target_pairs={{0,0},{1,1},{2,2},{3,3},{4,32},{5,33},{6,34},{7,35},{8,8},{9,9},{1... | collective-permute-start | bytes 786440 | tf_op jit(solution)/shard_map/ppermute | solution.py:29
  6.5 1.4 %collective-permute-start.1 = (f32[4,128,128]{2,1,0:T(8,128)S(1)}, f32[4,128,128]{2,1,0:T(8,128)S(1)}, u32[]{:S(2)}, u32[]{:S(2)}) collective-permute-start(f32[4,128,128]{2,1,0:T(8,128)S(1)} %get-tuple-element.21), channel_id=1, source_target_pairs={{0,1},{1,2},{2,3},{3,0},{4,33},{5,34},{6,35},{7,32},{8,9},{9,10},{... | collective-permute-start | bytes 786440 | tf_op jit(solution)/shard_map/ppermute | solution.py:29
  8.0 4.8 %collective-permute-start.2 = (f32[4,128,128]{2,1,0:T(8,128)S(1)}, f32[4,128,128]{2,1,0:T(8,128)S(1)}, u32[]{:S(2)}, u32[]{:S(2)}) collective-permute-start(f32[4,128,128]{2,1,0:T(8,128)S(1)} %get-tuple-element.23), channel_id=1, source_target_pairs={{0,2},{1,3},{2,0},{3,1},{4,34},{5,35},{6,32},{7,33},{8,10},{9,11},... | collective-permute-start | bytes 786440 | tf_op jit(solution)/shard_map/ppermute | solution.py:29
  12.7 1.9 %collective-permute-start.6 = (f32[4,128,128]{2,1,0:T(8,128)S(1)}, f32[4,128,128]{2,1,0:T(8,128)S(1)}, u32[]{:S(2)}, u32[]{:S(2)}) collective-permute-start(f32[4,128,128]{2,1,0:T(8,128)S(1)} %multiply_add_fusion), channel_id=1, source_target_pairs={{0,0},{1,1},{2,2},{3,3},{4,32},{5,33},{6,34},{7,35},{8,8},{9,9},{1... | collective-permute-start | bytes 786440 | tf_op jit(solution)/shard_map/ppermute | solution.py:29
  14.8 3.8 %collective-permute-start.3 = (f32[4,128,128]{2,1,0:T(8,128)S(1)}, f32[4,128,128]{2,1,0:T(8,128)S(1)}, u32[]{:S(2)}, u32[]{:S(2)}) collective-permute-start(f32[4,128,128]{2,1,0:T(8,128)S(1)} %get-tuple-element.20), channel_id=1, source_target_pairs={{0,3},{1,0},{2,1},{3,2},{4,35},{5,32},{6,33},{7,34},{8,11},{9,8},{... | collective-permute-start | bytes 786440 | tf_op jit(solution)/shard_map/ppermute | solution.py:29
  19.8 1.8 %collective-permute-start.9 = (f32[4,128,128]{2,1,0:T(8,128)S(1)}, f32[4,128,128]{2,1,0:T(8,128)S(1)}, u32[]{:S(2)}, u32[]{:S(2)}) collective-permute-start(f32[4,128,128]{2,1,0:T(8,128)S(1)} %multiply_add_fusion), channel_id=1, source_target_pairs={{0,3},{1,0},{2,1},{3,2},{4,35},{5,32},{6,33},{7,34},{8,11},{9,8},{... | collective-permute-start | bytes 786440 | tf_op jit(solution)/shard_map/ppermute | solution.py:29
  21.6 5.2 %collective-permute-done.3 = f32[4,128,128]{2,1,0:T(8,128)S(1)} collective-permute-done((f32[4,128,128]{2,1,0:T(8,128)S(1)}, f32[4,128,128]{2,1,0:T(8,128)S(1)}, u32[]{:S(2)}, u32[]{:S(2)}) %collective-permute-start.3) | collective-permute-done | bytes 262176 | tf_op jit(solution)/shard_map/ppermute | solution.py:29
  26.9 1.7 %collective-permute-start.5 = (f32[16,128,128]{2,1,0:T(8,128)S(1)}, f32[16,128,128]{2,1,0:T(8,128)}, u32[]{:S(2)}, u32[]{:S(2)}) collective-permute-start(f32[16,128,128]{2,1,0:T(8,128)S(1)} %constant_dynamic-update-slice_fusion.own), channel_id=1, source_target_pairs={{0,56},{1,57},{2,58},{3,59},{4,60},{5,61},{6,62},{7,63},{8,32},{9,... | collective-permute-start | bytes 3145736 | tf_op jit(solution)/shard_map/ppermute | solution.py:29
  28.7 2.4 %collective-permute-done.8 = f32[4,128,128]{2,1,0:T(8,128)S(1)} collective-permute-done((f32[4,128,128]{2,1,0:T(8,128)S(1)}, f32[4,128,128]{2,1,0:T(8,128)S(1)}, u32[]{:S(2)}, u32[]{:S(2)}) %collective-permute-start.8) | collective-permute-done | bytes 262176 | tf_op jit(solution)/shard_map/ppermute | solution.py:29
  31.1 1.4 %collective-permute-done.9 = f32[4,128,128]{2,1,0:T(8,128)S(1)} collective-permute-done((f32[4,128,128]{2,1,0:T(8,128)S(1)}, f32[4,128,128]{2,1,0:T(8,128)S(1)}, u32[]{:S(2)}, u32[]{:S(2)}) %collective-permute-start.9) | collective-permute-done | bytes 262176 | tf_op jit(solution)/shard_map/ppermute | solution.py:29
  32.6 3.1 %collective-permute-start.11 = (f32[16,128,128]{2,1,0:T(8,128)S(1)}, f32[16,128,128]{2,1,0:T(8,128)}, u32[]{:S(2)}, u32[]{:S(2)}) collective-permute-start(f32[16,128,128]{2,1,0:T(8,128)S(1)} %constant_dynamic-update-slice_fusion.4.own_pot), channel_id=1, source_target_pairs={{0,32},{1,33},{2,34},{3,35},{4,36},{5,37},{6,38},{7,39},{8,40},{9,... | collective-permute-start | bytes 3145736 | tf_op jit(solution)/shard_map/ppermute | solution.py:29
  35.7 1.3 %collective-permute-start.10 = (f32[16,128,128]{2,1,0:T(8,128)S(1)}, f32[16,128,128]{2,1,0:T(8,128)}, u32[]{:S(2)}, u32[]{:S(2)}) collective-permute-start(f32[16,128,128]{2,1,0:T(8,128)S(1)} %constant_dynamic-update-slice_fusion.4.own_pot), channel_id=1, source_target_pairs={{0,56},{1,57},{2,58},{3,59},{4,60},{5,61},{6,62},{7,63},{8,32},{9,... | collective-permute-start | bytes 3145736 | tf_op jit(solution)/shard_map/ppermute | solution.py:29
  37.1 4.6 %collective-permute-done.5.outer = f32[16,128,128]{2,1,0:T(8,128)} collective-permute-done((f32[16,128,128]{2,1,0:T(8,128)S(1)}, f32[16,128,128]{2,1,0:T(8,128)}, u32[]{:S(2)}, u32[]{:S(2)}) %collective-permute-start.5) | collective-permute-done | bytes 1048608 | tf_op jit(solution)/shard_map/ppermute | solution.py:29
  41.6 9.1 %inner.1.edges = f32[32,144,128]{2,1,0:T(8,128)S(1)} custom-call(s32[2]{0:T(128)S(1)} %pad_add_fusion.place, f32[16,128,128]{2,1,0:T(8,128)S(1)} %constant_dynamic-update-slice_fusion.own, f32[16,128,128]{2,1,0:T(8,128)S(1)} %collective-permute-done.4.sibling, f32[16,128,128]{2,1,0:T(8,128)S(1)} %constant_dynamic-update-slice_fusion.4.own_pot, ...), custom_call_target="tpu_custom_call" | custom-call | flops 1000 | tf_op jit(solution)/shard_map/inner/pallas_call | solution.py:196
  50.8 2.1 %collective-permute-done.10.outer_pot = f32[16,128,128]{2,1,0:T(8,128)} collective-permute-done((f32[16,128,128]{2,1,0:T(8,128)S(1)}, f32[16,128,128]{2,1,0:T(8,128)}, u32[]{:S(2)}, u32[]{:S(2)}) %collective-permute-start.10) | collective-permute-done | bytes 1048608 | tf_op jit(solution)/shard_map/ppermute | solution.py:29
  52.9 11.1 %outer.1 = f32[16,128,128]{2,1,0:T(8,128)} custom-call(s32[2]{0:T(128)S(1)} %pad_add_fusion.place, f32[16,128,128]{2,1,0:T(8,128)} %collective-permute-done.5.outer, f32[16,128,128]{2,1,0:T(8,128)} %collective-permute-done.10.outer_pot, f32[16,128,128]{2,1,0:T(8,128)S(1)} %constant_dynamic-update-slice_fusion.4.own_pot, f32[32,144,128]{2,1,0:T(8,128)S(1)} %inner.1.edges, ...), custom_call_target="tpu_custom_call" | custom-call | flops 1000 | tf_op jit(solution)/shard_map/outer/pallas_call | solution.py:196
  63.9 6.7 %all-to-all-start = ((f32[16,128,128]{2,1,0:T(8,128)}), f32[16,128,128]{2,1,0:T(8,128)S(1)}, u32[]{:S(2)}, u32[]{:S(2)}) async-start(f32[16,128,128]{2,1,0:T(8,128)} %outer.1), calls=%async_computation | async-start | bytes 2097152 | tf_op jit(solution)/shard_map/all_to_all | solution.py:319
  70.7 15.2 %all-to-all-done.x = f32[16,128,128]{2,1,0:T(8,128)S(1)} async-done(((f32[16,128,128]{2,1,0:T(8,128)}), f32[16,128,128]{2,1,0:T(8,128)S(1)}, u32[]{:S(2)}, u32[]{:S(2)}) %all-to-all-start) | async-done | bytes 1048608 | tf_op jit(solution)/shard_map/all_to_all | solution.py:319
  85.9 1.5 %rotate.2 = (f32[4,128,128]{2,1,0:T(8,128)S(1)}, f32[4,128,128]{2,1,0:T(8,128)S(1)}) custom-call(s32[1]{0:T(128)} %bitcast.place, f32[16,16]{1,0:T(8,128)S(1)} %copy-done.1, f32[16,128,128]{2,1,0:T(8,128)S(1)} %all-to-all-done.x), custom_call_target="tpu_custom_call" | custom-call | tf_op jit(solution)/shard_map/rotate/pallas_call | solution.py:243
  87.4 1.6 %rotate.3 = (f32[4,128,128]{2,1,0:T(8,128)S(1)}, f32[4,128,128]{2,1,0:T(8,128)S(1)}) custom-call(s32[1]{0:T(128)} %bitcast.place, f32[16,16]{1,0:T(8,128)S(1)} %copy-done.1, f32[16,128,128]{2,1,0:T(8,128)S(1)} %all-to-all-done.x), custom_call_target="tpu_custom_call" | custom-call | tf_op jit(solution)/shard_map/rotate/pallas_call | solution.py:243
  90.3 2.2 %collective-permute-done.16 = f32[8,256]{1,0:T(8,128)S(1)} collective-permute-done((f32[8,256]{1,0:T(8,128)S(1)}, f32[8,256]{1,0:T(8,128)S(1)}, u32[]{:S(2)}, u32[]{:S(2)}) %collective-permute-start.16) | collective-permute-done | bytes 8224 | tf_op jit(solution)/shard_map/ppermute | solution.py:29
  93.3 3.2 %collective-permute-done.17 = f32[8,256]{1,0:T(8,128)S(1)} collective-permute-done((f32[8,256]{1,0:T(8,128)S(1)}, f32[8,256]{1,0:T(8,128)S(1)}, u32[]{:S(2)}, u32[]{:S(2)}) %collective-permute-start.17) | collective-permute-done | bytes 8224 | tf_op jit(solution)/shard_map/ppermute | solution.py:29
  97.3 6.9 %collective-permute-start.12 = (f32[4,128,128]{2,1,0:T(8,128)S(1)}, f32[4,128,128]{2,1,0:T(8,128)S(1)}, u32[]{:S(2)}, u32[]{:S(2)}) collective-permute-start(f32[4,128,128]{2,1,0:T(8,128)S(1)} %get-tuple-element.10.o0), channel_id=1, source_target_pairs={{0,0},{1,1},{2,2},{3,3},{4,32},{5,33},{6,34},{7,35},{8,8},{9,9},{1... | collective-permute-start | bytes 786440 | tf_op jit(solution)/shard_map/ppermute | solution.py:29
  104.4 1.7 %collective-permute-start.14 = (f32[4,128,128]{2,1,0:T(8,128)S(1)}, f32[4,128,128]{2,1,0:T(8,128)S(1)}, u32[]{:S(2)}, u32[]{:S(2)}) collective-permute-start(f32[4,128,128]{2,1,0:T(8,128)S(1)} %get-tuple-element.12.o2), channel_id=1, source_target_pairs={{0,64},{1,65},{2,66},{3,67},{4,96},{5,97},{6,98},{7,99},{8,72},{9,... | collective-permute-start | bytes 786440 | tf_op jit(solution)/shard_map/ppermute | solution.py:29
  106.9 4.4 %collective-permute-start.19 = (f32[8,256]{1,0:T(8,128)S(1)}, f32[8,256]{1,0:T(8,128)S(1)}, u32[]{:S(2)}, u32[]{:S(2)}) collective-permute-start(f32[8,256]{1,0:T(8,128)S(1)} %add.89), channel_id=1, source_target_pairs={{0,16},{1,17},{2,18},{3,19},{4,20},{5,21},{6,22},{7,23},{8,24},{9,... | collective-permute-start | bytes 24584 | tf_op jit(solution)/shard_map/ppermute | solution.py:29
  111.3 1.3 %collective-permute-done.19 = f32[8,256]{1,0:T(8,128)S(1)} collective-permute-done((f32[8,256]{1,0:T(8,128)S(1)}, f32[8,256]{1,0:T(8,128)S(1)}, u32[]{:S(2)}, u32[]{:S(2)}) %collective-permute-start.19) | collective-permute-done | bytes 8224 | tf_op jit(solution)/shard_map/ppermute | solution.py:29
  112.6 2.0 %collective-permute-start.20 = (f32[8,256]{1,0:T(8,128)S(1)}, f32[8,256]{1,0:T(8,128)S(1)}, u32[]{:S(2)}, u32[]{:S(2)}) collective-permute-start(f32[8,256]{1,0:T(8,128)S(1)} %add.90), channel_id=1, source_target_pairs={{0,32},{1,33},{2,34},{3,35},{4,36},{5,37},{6,38},{7,39},{8,40},{9,... | collective-permute-start | bytes 24584 | tf_op jit(solution)/shard_map/ppermute | solution.py:29
  115.5 2.8 %collective-permute-done.21 = f32[8,256]{1,0:T(8,128)S(1)} collective-permute-done((f32[8,256]{1,0:T(8,128)S(1)}, f32[8,256]{1,0:T(8,128)S(1)}, u32[]{:S(2)}, u32[]{:S(2)}) %collective-permute-start.21) | collective-permute-done | bytes 8224 | tf_op jit(solution)/shard_map/ppermute | solution.py:29
  118.3 2.6 %collective-permute-start.22 = (f32[8,256]{1,0:T(8,128)S(1)}, f32[8,256]{1,0:T(8,128)S(1)}, u32[]{:S(2)}, u32[]{:S(2)}) collective-permute-start(f32[8,256]{1,0:T(8,128)S(1)} %add.92), channel_id=1, source_target_pairs={{0,64},{1,65},{2,66},{3,67},{4,68},{5,69},{6,70},{7,71},{8,72},{9,... | collective-permute-start | bytes 24584 | tf_op jit(solution)/shard_map/ppermute | solution.py:29
  120.9 1.4 %collective-permute-done.22 = f32[8,256]{1,0:T(8,128)S(1)} collective-permute-done((f32[8,256]{1,0:T(8,128)S(1)}, f32[8,256]{1,0:T(8,128)S(1)}, u32[]{:S(2)}, u32[]{:S(2)}) %collective-permute-start.22) | collective-permute-done | bytes 8224 | tf_op jit(solution)/shard_map/ppermute | solution.py:29
  123.2 1.1 copy.7
  (50 shorter events, 7.3 us)
Async XLA Ops:
  0.6 12.1 %copy-start.2 = (f32[4,128,128]{2,1,0:T(8,128)S(1)}, f32[4,128,128]{2,1,0:T(8,128)}, u32[]{:S(2)}) copy-start(f32[4,128,128]{2,1,0:T(8,128)} %param.6) | copy-start | bytes 786436
  2.0 12.8 %collective-permute-start = (f32[4,128,128]{2,1,0:T(8,128)S(1)}, f32[4,128,128]{2,1,0:T(8,128)S(1)}, u32[]{:S(2)}, u32[]{:S(2)}) collective-permute-start(f32[4,128,128]{2,1,0:T(8,128)S(1)} %get-tuple-element.22), channel_id=1, source_target_pairs={{0,0},{1,1},{2,2},{3,3},{4,32},{5,33},{6,34},{7,35},{8,8},{9,9},{1... | collective-permute-start | bytes 786440 | tf_op jit(solution)/shard_map/ppermute | solution.py:29
  6.5 12.1 %collective-permute-start.1 = (f32[4,128,128]{2,1,0:T(8,128)S(1)}, f32[4,128,128]{2,1,0:T(8,128)S(1)}, u32[]{:S(2)}, u32[]{:S(2)}) collective-permute-start(f32[4,128,128]{2,1,0:T(8,128)S(1)} %get-tuple-element.21), channel_id=1, source_target_pairs={{0,1},{1,2},{2,3},{3,0},{4,33},{5,34},{6,35},{7,32},{8,9},{9,10},{... | collective-permute-start | bytes 786440 | tf_op jit(solution)/shard_map/ppermute | solution.py:29
  8.0 33.7 %copy-start = (bf16[256,128]{1,0:T(8,128)(2,1)S(1)}, bf16[256,128]{1,0:T(8,128)(2,1)}, u32[]{:S(2)}) copy-start(bf16[256,128]{1,0:T(8,128)(2,1)} %constant.69.clone.matrix) | copy-start | bytes 196612
  8.0 11.8 %collective-permute-start.2 = (f32[4,128,128]{2,1,0:T(8,128)S(1)}, f32[4,128,128]{2,1,0:T(8,128)S(1)}, u32[]{:S(2)}, u32[]{:S(2)}) collective-permute-start(f32[4,128,128]{2,1,0:T(8,128)S(1)} %get-tuple-element.23), channel_id=1, source_target_pairs={{0,2},{1,3},{2,0},{3,1},{4,34},{5,35},{6,32},{7,33},{8,10},{9,11},... | collective-permute-start | bytes 786440 | tf_op jit(solution)/shard_map/ppermute | solution.py:29
  12.7 14.2 %collective-permute-start.6 = (f32[4,128,128]{2,1,0:T(8,128)S(1)}, f32[4,128,128]{2,1,0:T(8,128)S(1)}, u32[]{:S(2)}, u32[]{:S(2)}) collective-permute-start(f32[4,128,128]{2,1,0:T(8,128)S(1)} %multiply_add_fusion), channel_id=1, source_target_pairs={{0,0},{1,1},{2,2},{3,3},{4,32},{5,33},{6,34},{7,35},{8,8},{9,9},{1... | collective-permute-start | bytes 786440 | tf_op jit(solution)/shard_map/ppermute | solution.py:29
  14.7 13.9 %collective-permute-start.7 = (f32[4,128,128]{2,1,0:T(8,128)S(1)}, f32[4,128,128]{2,1,0:T(8,128)S(1)}, u32[]{:S(2)}, u32[]{:S(2)}) collective-permute-start(f32[4,128,128]{2,1,0:T(8,128)S(1)} %multiply_add_fusion), channel_id=1, source_target_pairs={{0,1},{1,2},{2,3},{3,0},{4,33},{5,34},{6,35},{7,32},{8,9},{9,10},{... | collective-permute-start | bytes 786440 | tf_op jit(solution)/shard_map/ppermute | solution.py:29
  14.8 12.0 %collective-permute-start.3 = (f32[4,128,128]{2,1,0:T(8,128)S(1)}, f32[4,128,128]{2,1,0:T(8,128)S(1)}, u32[]{:S(2)}, u32[]{:S(2)}) collective-permute-start(f32[4,128,128]{2,1,0:T(8,128)S(1)} %get-tuple-element.20), channel_id=1, source_target_pairs={{0,3},{1,0},{2,1},{3,2},{4,35},{5,32},{6,33},{7,34},{8,11},{9,8},{... | collective-permute-start | bytes 786440 | tf_op jit(solution)/shard_map/ppermute | solution.py:29
  18.6 12.5 %collective-permute-start.8 = (f32[4,128,128]{2,1,0:T(8,128)S(1)}, f32[4,128,128]{2,1,0:T(8,128)S(1)}, u32[]{:S(2)}, u32[]{:S(2)}) collective-permute-start(f32[4,128,128]{2,1,0:T(8,128)S(1)} %multiply_add_fusion), channel_id=1, source_target_pairs={{0,2},{1,3},{2,0},{3,1},{4,34},{5,35},{6,32},{7,33},{8,10},{9,11},... | collective-permute-start | bytes 786440 | tf_op jit(solution)/shard_map/ppermute | solution.py:29
  19.8 12.8 %collective-permute-start.9 = (f32[4,128,128]{2,1,0:T(8,128)S(1)}, f32[4,128,128]{2,1,0:T(8,128)S(1)}, u32[]{:S(2)}, u32[]{:S(2)}) collective-permute-start(f32[4,128,128]{2,1,0:T(8,128)S(1)} %multiply_add_fusion), channel_id=1, source_target_pairs={{0,3},{1,0},{2,1},{3,2},{4,35},{5,32},{6,33},{7,34},{8,11},{9,8},{... | collective-permute-start | bytes 786440 | tf_op jit(solution)/shard_map/ppermute | solution.py:29
  26.8 10.3 %collective-permute-start.4 = (f32[16,128,128]{2,1,0:T(8,128)S(1)}, f32[16,128,128]{2,1,0:T(8,128)S(1)}, u32[]{:S(2)}, u32[]{:S(2)}) collective-permute-start(f32[16,128,128]{2,1,0:T(8,128)S(1)} %constant_dynamic-update-slice_fusion.own), channel_id=1, source_target_pairs={{0,32},{1,33},{2,34},{3,35},{4,36},{5,37},{6,38},{7,39},{8,40},{9,... | collective-permute-start | bytes 3145736 | tf_op jit(solution)/shard_map/ppermute | solution.py:29
  26.9 14.7 %collective-permute-start.5 = (f32[16,128,128]{2,1,0:T(8,128)S(1)}, f32[16,128,128]{2,1,0:T(8,128)}, u32[]{:S(2)}, u32[]{:S(2)}) collective-permute-start(f32[16,128,128]{2,1,0:T(8,128)S(1)} %constant_dynamic-update-slice_fusion.own), channel_id=1, source_target_pairs={{0,56},{1,57},{2,58},{3,59},{4,60},{5,61},{6,62},{7,63},{8,32},{9,... | collective-permute-start | bytes 3145736 | tf_op jit(solution)/shard_map/ppermute | solution.py:29
  32.6 9.0 %collective-permute-start.11 = (f32[16,128,128]{2,1,0:T(8,128)S(1)}, f32[16,128,128]{2,1,0:T(8,128)}, u32[]{:S(2)}, u32[]{:S(2)}) collective-permute-start(f32[16,128,128]{2,1,0:T(8,128)S(1)} %constant_dynamic-update-slice_fusion.4.own_pot), channel_id=1, source_target_pairs={{0,32},{1,33},{2,34},{3,35},{4,36},{5,37},{6,38},{7,39},{8,40},{9,... | collective-permute-start | bytes 3145736 | tf_op jit(solution)/shard_map/ppermute | solution.py:29
  35.7 17.1 %collective-permute-start.10 = (f32[16,128,128]{2,1,0:T(8,128)S(1)}, f32[16,128,128]{2,1,0:T(8,128)}, u32[]{:S(2)}, u32[]{:S(2)}) collective-permute-start(f32[16,128,128]{2,1,0:T(8,128)S(1)} %constant_dynamic-update-slice_fusion.4.own_pot), channel_id=1, source_target_pairs={{0,56},{1,57},{2,58},{3,59},{4,60},{5,61},{6,62},{7,63},{8,32},{9,... | collective-permute-start | bytes 3145736 | tf_op jit(solution)/shard_map/ppermute | solution.py:29
  50.7 35.1 %copy-start.1 = (f32[16,16]{1,0:T(8,128)S(1)}, f32[16,16]{1,0:T(8,128)}, u32[]{:S(2)}) copy-start(f32[16,16]{1,0:T(8,128)} %rotation.3) | copy-start | bytes 3076
  63.9 21.9 %all-to-all-start = ((f32[16,128,128]{2,1,0:T(8,128)}), f32[16,128,128]{2,1,0:T(8,128)S(1)}, u32[]{:S(2)}, u32[]{:S(2)}) async-start(f32[16,128,128]{2,1,0:T(8,128)} %outer.1), calls=%async_computation | async-start | bytes 2097152 | tf_op jit(solution)/shard_map/all_to_all | solution.py:319
  90.0 2.5 %collective-permute-start.16 = (f32[8,256]{1,0:T(8,128)S(1)}, f32[8,256]{1,0:T(8,128)S(1)}, u32[]{:S(2)}, u32[]{:S(2)}) collective-permute-start(f32[8,256]{1,0:T(8,128)S(1)} %gram.1), channel_id=1, source_target_pairs={{0,1},{1,0},{2,3},{3,2},{4,5},{5,4},{6,7},{7,6},{8,9},{9,8},{10,11... | collective-permute-start | bytes 24584 | tf_op jit(solution)/shard_map/ppermute | solution.py:29
  92.5 4.0 %collective-permute-start.17 = (f32[8,256]{1,0:T(8,128)S(1)}, f32[8,256]{1,0:T(8,128)S(1)}, u32[]{:S(2)}, u32[]{:S(2)}) collective-permute-start(f32[8,256]{1,0:T(8,128)S(1)} %add.87), channel_id=1, source_target_pairs={{0,2},{1,3},{2,0},{3,1},{4,6},{5,7},{6,4},{7,5},{8,10},{9,11},{10,... | collective-permute-start | bytes 24584 | tf_op jit(solution)/shard_map/ppermute | solution.py:29
  96.5 10.4 %collective-permute-start.18 = (f32[8,256]{1,0:T(8,128)S(1)}, f32[8,256]{1,0:T(8,128)S(1)}, u32[]{:S(2)}, u32[]{:S(2)}) collective-permute-start(f32[8,256]{1,0:T(8,128)S(1)} %add.88), channel_id=1, source_target_pairs={{0,8},{1,9},{2,10},{3,11},{4,12},{5,13},{6,14},{7,15},{8,0},{9,1},... | collective-permute-start | bytes 24584 | tf_op jit(solution)/shard_map/ppermute | solution.py:29
  97.3 25.6 %collective-permute-start.12 = (f32[4,128,128]{2,1,0:T(8,128)S(1)}, f32[4,128,128]{2,1,0:T(8,128)S(1)}, u32[]{:S(2)}, u32[]{:S(2)}) collective-permute-start(f32[4,128,128]{2,1,0:T(8,128)S(1)} %get-tuple-element.10.o0), channel_id=1, source_target_pairs={{0,0},{1,1},{2,2},{3,3},{4,32},{5,33},{6,34},{7,35},{8,8},{9,9},{1... | collective-permute-start | bytes 786440 | tf_op jit(solution)/shard_map/ppermute | solution.py:29
  104.3 18.7 %collective-permute-start.13 = (f32[4,128,128]{2,1,0:T(8,128)S(1)}, f32[4,128,128]{2,1,0:T(8,128)S(1)}, u32[]{:S(2)}, u32[]{:S(2)}) collective-permute-start(f32[4,128,128]{2,1,0:T(8,128)S(1)} %get-tuple-element.11.o1), channel_id=1, source_target_pairs={{0,32},{1,33},{2,34},{3,35},{4,0},{5,1},{6,2},{7,3},{8,40},{9,41},... | collective-permute-start | bytes 786440 | tf_op jit(solution)/shard_map/ppermute | solution.py:29
  104.4 18.6 %collective-permute-start.14 = (f32[4,128,128]{2,1,0:T(8,128)S(1)}, f32[4,128,128]{2,1,0:T(8,128)S(1)}, u32[]{:S(2)}, u32[]{:S(2)}) collective-permute-start(f32[4,128,128]{2,1,0:T(8,128)S(1)} %get-tuple-element.12.o2), channel_id=1, source_target_pairs={{0,64},{1,65},{2,66},{3,67},{4,96},{5,97},{6,98},{7,99},{8,72},{9,... | collective-permute-start | bytes 786440 | tf_op jit(solution)/shard_map/ppermute | solution.py:29
  106.1 16.9 %collective-permute-start.15 = (f32[4,128,128]{2,1,0:T(8,128)S(1)}, f32[4,128,128]{2,1,0:T(8,128)S(1)}, u32[]{:S(2)}, u32[]{:S(2)}) collective-permute-start(f32[4,128,128]{2,1,0:T(8,128)S(1)} %get-tuple-element.13.o3), channel_id=1, source_target_pairs={{0,96},{1,97},{2,98},{3,99},{4,64},{5,65},{6,66},{7,67},{8,104},{9... | collective-permute-start | bytes 786440 | tf_op jit(solution)/shard_map/ppermute | solution.py:29
  106.9 5.7 %collective-permute-start.19 = (f32[8,256]{1,0:T(8,128)S(1)}, f32[8,256]{1,0:T(8,128)S(1)}, u32[]{:S(2)}, u32[]{:S(2)}) collective-permute-start(f32[8,256]{1,0:T(8,128)S(1)} %add.89), channel_id=1, source_target_pairs={{0,16},{1,17},{2,18},{3,19},{4,20},{5,21},{6,22},{7,23},{8,24},{9,... | collective-permute-start | bytes 24584 | tf_op jit(solution)/shard_map/ppermute | solution.py:29
  112.6 2.9 %collective-permute-start.20 = (f32[8,256]{1,0:T(8,128)S(1)}, f32[8,256]{1,0:T(8,128)S(1)}, u32[]{:S(2)}, u32[]{:S(2)}) collective-permute-start(f32[8,256]{1,0:T(8,128)S(1)} %add.90), channel_id=1, source_target_pairs={{0,32},{1,33},{2,34},{3,35},{4,36},{5,37},{6,38},{7,39},{8,40},{9,... | collective-permute-start | bytes 24584 | tf_op jit(solution)/shard_map/ppermute | solution.py:29
  115.5 2.8 %collective-permute-start.21 = (f32[8,256]{1,0:T(8,128)S(1)}, f32[8,256]{1,0:T(8,128)S(1)}, u32[]{:S(2)}, u32[]{:S(2)}) collective-permute-start(f32[8,256]{1,0:T(8,128)S(1)} %add.91), channel_id=1, source_target_pairs={{0,4},{1,5},{2,6},{3,7},{4,0},{5,1},{6,2},{7,3},{8,12},{9,13},{10,... | collective-permute-start | bytes 24584 | tf_op jit(solution)/shard_map/ppermute | solution.py:29
  118.3 4.0 %collective-permute-start.22 = (f32[8,256]{1,0:T(8,128)S(1)}, f32[8,256]{1,0:T(8,128)S(1)}, u32[]{:S(2)}, u32[]{:S(2)}) collective-permute-start(f32[8,256]{1,0:T(8,128)S(1)} %add.92), channel_id=1, source_target_pairs={{0,64},{1,65},{2,66},{3,67},{4,68},{5,69},{6,70},{7,71},{8,72},{9,... | collective-permute-start | bytes 24584 | tf_op jit(solution)/shard_map/ppermute | solution.py:29

commit v3 on v2

--- a/solution.py
+++ b/solution.py
@@ -37,6 +37,10 @@
     return {**c, "core": 1 - c["core"], "y": c["y"] + (1 if c["core"] == 1 else -1)}
 
 
+def to_outer_natively(c):
+    return {**c, "x_lo": 1 - c["x_lo"], "y": c["y"] + (1 if c["x_lo"] == 1 else -1)}
+
+
 def to_sibling(c):
     return {**c, "core": 1 - c["core"]}
 
@@ -64,12 +68,14 @@
     return jnp.asarray(np.concatenate([m, m], axis=0), jnp.bfloat16)
 
 
-def place_blocks(ref, target, first, z, sems, copies):
+def place_blocks(refs, target, first, z, sems, copies):
+    if not isinstance(refs, (list, tuple)):
+        refs = [refs.at[pl.ds(4 * shift, 4)] for shift in range(4)]
     for shift in range(4):
         where = first + 4 * lax.rem(z + 4 - shift, 4)
         copies.append(
             pltpu.make_async_copy(
-                ref.at[pl.ds(4 * shift, 4)],
+                refs[shift],
                 target.at[pl.ds(where, 4), pl.ds(PAD, N), :],
                 sems.at[len(copies)],
             )
@@ -146,12 +152,12 @@
 
 
 def outer_kernel(
-    place, outer, outer_pot, own_pot, edges, matrix, out, one, two, pot, along, sems
+    place, outer, q0, q1, q2, q3, own_pot, edges, matrix, out, one, two, pot, along, sems
 ):
     core, z = place[0], place[1]
     copies = []
     place_blocks(outer, one, 18 * core, z, sems, copies)
-    place_blocks(outer_pot, pot, 18 * core, z, sems, copies)
+    place_blocks((q0, q1, q2, q3), pot, 18 * core, z, sems, copies)
     place_blocks(own_pot, pot, 16 - 14 * core, z, sems, copies)
     for copy in copies:
         copy.start()
@@ -208,14 +214,14 @@
     )(*args, stencil_matrix())
 
 
-def filtered(place, own, sibling, outer, own_pot, sibling_pot, outer_pot):
+def filtered(place, own, sibling, outer, own_pot, sibling_pot, outer_pots):
     edges = filter_call(
         inner_kernel, "inner", 2 * OWN, [pl.ANY] * 4, (4 * DEGREE, ROWS, N), pltpu.VMEM,
         (place, own, sibling, own_pot, sibling_pot),
     )
     return filter_call(
-        outer_kernel, "outer", 2 * OWN + 2, [pl.ANY] * 3 + [pltpu.VMEM], (OWN, N, N), pl.ANY,
-        (place, outer, outer_pot, own_pot, edges),
+        outer_kernel, "outer", 2 * OWN + 2, [pl.ANY] * 6 + [pltpu.VMEM], (OWN, N, N), pl.ANY,
+        (place, outer, *outer_pots, own_pot, edges),
     )
 
 
@@ -250,48 +256,44 @@
     )(place, rotation, planes)
 
 
-def gram_kernel(place, o0, o1, o2, o3, out, sums):
-    parts = (o0, o1, o2, o3)
-    sums[...] = jnp.zeros_like(sums)
-    for rel in range(4):
-        for j in range(4):
-            row = 16 * (4 * (place[0] ^ rel) + j)
-            for other in range(rel + 1):
-                totals = [jnp.zeros((8, N), jnp.float32) for _ in range(4)]
-                for t in range(N // 8):
-                    a = parts[rel][j, 8 * t : 8 * t + 8, :]
-                    totals = [
-                        s + a * parts[other][k, 8 * t : 8 * t + 8, :]
-                        for k, s in enumerate(totals)
-                    ]
-                for k in range(4):
-                    total = jnp.sum(totals[k], axis=0, keepdims=True)
-                    column = 4 * (place[0] ^ other) + k
-                    sums[pl.ds(row + column, 1), :] = total
-                    if other < rel:
-                        back = 16 * column + 4 * (place[0] ^ rel) + j
-                        sums[pl.ds(back, 1), :] = total
-    out[...] = lax.dot_general(
+def gram_kernel(x, square, out, sums):
+    for i in range(16):
+        for first in range(0, i + 1, 4):
+            others = range(first, min(first + 4, i + 1))
+            totals = [jnp.zeros((8, N), jnp.float32) for _ in others]
+            for t in range(N // 8):
+                a = x[i, 8 * t : 8 * t + 8, :]
+                totals = [
+                    s + a * x[k, 8 * t : 8 * t + 8, :] for s, k in zip(totals, others)
+                ]
+            for k, total in zip(others, totals):
+                total = jnp.sum(total, axis=0, keepdims=True)
+                sums[16 * i + k : 16 * i + k + 1, :] = total
+                if k < i:
+                    sums[16 * k + i : 16 * k + i + 1, :] = total
+    gram = lax.dot_general(
         jnp.ones((8, N), jnp.float32),
         sums[...],
         (((1,), (1,)), ((), ())),
         precision=lax.Precision.HIGHEST,
         preferred_element_type=jnp.float32,
     )
-
-
-def gram_rows(place, parts):
+    out[...] = jnp.dot(
+        gram, square[...], precision=lax.Precision.HIGHEST, preferred_element_type=jnp.float32
+    )
+
+
+def gram_row(planes, square):
     vmem = pl.BlockSpec(memory_space=pltpu.VMEM)
-    smem = pl.BlockSpec(memory_space=pltpu.SMEM)
     return pl.pallas_call(
         gram_kernel,
         out_shape=jax.ShapeDtypeStruct((8, 256), jnp.float32),
-        in_specs=[smem] + [vmem] * 4,
+        in_specs=[vmem] * 2,
         out_specs=vmem,
         scratch_shapes=[pltpu.VMEM((256, N), jnp.float32)],
         compiler_params=pltpu.CompilerParams(vmem_limit_bytes=32 << 20),
         name="gram",
-    )(place, *parts)
+    )(planes, square)
 
 
 def local(orbitals, potential, rotation):
@@ -307,24 +309,35 @@
         for s in range(4)
     ]
     diagonal = FACTOR * potential + DIAG
-    pots = [moved(diagonal, to_orbital(s)) for s in range(4)]
+    beyond = moved(diagonal, to_outer_natively)
     own = jnp.concatenate(orbs, axis=0)
-    own_pot = jnp.concatenate(pots, axis=0)
+    own, diagonal, beyond = lax.optimization_barrier((own, diagonal, beyond))
     outer = moved(own, to_outer)
     sibling = moved(own, to_sibling)
-    outer_pot = moved(own_pot, to_outer)
+    pots, outer_pots = [None] * 4, []
+    for s in (1, 3, 2, 0):
+        sent = diagonal
+        if s == 0:
+            sent, sibling = lax.optimization_barrier((diagonal, sibling))
+        pots[s] = moved(sent, to_orbital(s))
+    for s in range(4):
+        sent, pots[s] = lax.optimization_barrier((beyond, pots[s]))
+        outer_pots.append(moved(sent, to_orbital(s)))
+    pots, outer = lax.optimization_barrier((pots, outer))
+    own_pot = jnp.concatenate(pots, axis=0)
     sibling_pot = moved(own_pot, to_sibling)
-    sibling, outer = lax.optimization_barrier((sibling, outer))
-    mine = filtered(place, own, sibling, outer, own_pot, sibling_pot, outer_pot)
+    mine = filtered(place, own, sibling, outer, own_pot, sibling_pot, outer_pots)
     planes = lax.all_to_all(mine, ("x_hi", "x_lo", "z"), 0, 0, tiled=True)
     base = jnp.stack([2 * x_hi + x_lo]).astype(jnp.int32)
+    square = (rotation[:, None, :, None] * rotation[None, :, None, :]).reshape(256, 256)
+    total = gram_row(planes, square)
     far = rotated_parts(2, base, rotation, planes)
     near = rotated_parts(0, base, rotation, planes)
     home = [None] * 4
     home[2], home[3] = moved(far[0], to_home(1, 0)), moved(far[1], to_home(1, 1))
     home[0], home[1] = moved(near[0], to_home(0, 0)), moved(near[1], to_home(0, 1))
-    total = gram_rows(base, [*near, *far])
-    for axis, bit in (("z", 1), ("z", 2), ("y", 1), ("y", 2), ("core", 1), ("x_lo", 1), ("x_hi", 1)):
+    stages = (("z", 1), ("z", 2), ("y", 1), ("y", 2), ("core", 1), ("x_lo", 1), ("x_hi", 1))
+    for axis, bit in stages:
         total = total + moved(total, lambda c: {**c, axis: c[axis] ^ bit})
     total = total[0].reshape(16, 16) / (N * N * N)
     correlation = lax.dynamic_slice_in_dim(total, 4 * (2 * x_hi + core), 4, 0)

time: 126 us -> 138 us (1.095)
  waiting for transfers between devices: 43.7 us -> 49.9 us
  local copies, waits for them, and re-layouts: 3.2 us -> 6.28 us
  starting transfers between devices: 51.8 us -> 53.8 us
    ppermute x23 -> x27, waiting for transfers between devices: 28.5 us -> 33.9 us  [moved(): return lax.ppermute(array, AXES, pairs)]
    unnamed x13 -> x14, local copies, waits for them, and re-layouts: 1.19 us -> 3.34 us
    ppermute x23 -> x27, starting transfers between devices: 45.1 us -> 45.9 us  [moved(): return lax.ppermute(array, AXES, pairs)]
  transfers between devices with their start and end apart: 24 -> 28, of which waited for: 13 -> 14; matrix products, arithmetic and copies ran while one was open for 1% -> 2% of each run, Pallas kernels for 7% -> 9%
where the time goes in v3:
time: 138 us; the launch traced here: 136 us
  starting transfers between devices  53.8 us (39%)
  waiting for transfers between devices  49.9 us (36%)
  Pallas kernels  24.3 us (18%)
  local copies, waits for them, and re-layouts  6.28 us (5%)
    ppermute x27, starting transfers between devices, moved(): return lax.ppermute(array, AXES, pairs)  45.9 us
    ppermute x27, waiting for transfers between devices, moved(): return lax.ppermute(array, AXES, pairs)  33.9 us
    pallas_call x2, Pallas kernels, filter_call(): pl.pallas_call(kernel, out_shape=jax.ShapeDtypeStruct(shape, jnp.float32)...  19.9 us
    all_to_all x1, waiting for transfers between devices, local(): planes = lax.all_to_all(mine, ('x_hi', 'x_lo', 'z'), 0, 0, tiled=True)  16 us
    all_to_all x1, starting transfers between devices, local(): planes = lax.all_to_all(mine, ('x_hi', 'x_lo', 'z'), 0, 0, tiled=True)  7.83 us
    unnamed x14, local copies, waits for them, and re-layouts  3.34 us
    pallas_call x2, Pallas kernels, rotated_parts(): pl.pallas_call(functools.partial(rotate_kernel, first), out_shape=[jax.Sh...  3.1 us
  transfers between devices with their start and end apart: 28, of which 14 were waited for; matrix products, arithmetic and copies ran while one was open for 2% of the time, Pallas kernels for 9%

profile of v3, /device:TPU:1, one launch (start us, length us, event | category | flops | bytes accessed | tf_op | source)
XLA Modules:
  0.0 135.9 jit_solution(6622333450726307911)
XLA Ops:
  0.7 1.3 dynamic-slice_bitcast_fusion.3
  2.0 4.5 %collective-permute-start = (f32[4,128,128]{2,1,0:T(8,128)S(1)}, f32[4,128,128]{2,1,0:T(8,128)S(1)}, u32[]{:S(2)}, u32[]{:S(2)}) collective-permute-start(f32[4,128,128]{2,1,0:T(8,128)S(1)} %get-tuple-element.52), channel_id=1, source_target_pairs={{0,0},{1,1},{2,2},{3,3},{4,32},{5,33},{6,34},{7,35},{8,8},{9,9},{1... | collective-permute-start | bytes 786440 | tf_op jit(solution)/shard_map/ppermute | solution.py:29
  6.5 1.4 %collective-permute-start.1 = (f32[4,128,128]{2,1,0:T(8,128)S(1)}, f32[4,128,128]{2,1,0:T(8,128)S(1)}, u32[]{:S(2)}, u32[]{:S(2)}) collective-permute-start(f32[4,128,128]{2,1,0:T(8,128)S(1)} %get-tuple-element.53), channel_id=1, source_target_pairs={{0,1},{1,2},{2,3},{3,0},{4,33},{5,34},{6,35},{7,32},{8,9},{9,10},{... | collective-permute-start | bytes 786440 | tf_op jit(solution)/shard_map/ppermute | solution.py:29
  8.0 4.8 %collective-permute-start.2 = (f32[4,128,128]{2,1,0:T(8,128)S(1)}, f32[4,128,128]{2,1,0:T(8,128)S(1)}, u32[]{:S(2)}, u32[]{:S(2)}) collective-permute-start(f32[4,128,128]{2,1,0:T(8,128)S(1)} %get-tuple-element.55), channel_id=1, source_target_pairs={{0,2},{1,3},{2,0},{3,1},{4,34},{5,35},{6,32},{7,33},{8,10},{9,11},... | collective-permute-start | bytes 786440 | tf_op jit(solution)/shard_map/ppermute | solution.py:29
  13.3 3.9 %collective-permute-done.1 = f32[4,128,128]{2,1,0:T(8,128)S(1)} collective-permute-done((f32[4,128,128]{2,1,0:T(8,128)S(1)}, f32[4,128,128]{2,1,0:T(8,128)S(1)}, u32[]{:S(2)}, u32[]{:S(2)}) %collective-permute-start.1) | collective-permute-done | bytes 262176 | tf_op jit(solution)/shard_map/ppermute | solution.py:29
  17.2 4.7 %collective-permute-done.2 = f32[4,128,128]{2,1,0:T(8,128)S(1)} collective-permute-done((f32[4,128,128]{2,1,0:T(8,128)S(1)}, f32[4,128,128]{2,1,0:T(8,128)S(1)}, u32[]{:S(2)}, u32[]{:S(2)}) %collective-permute-start.2) | collective-permute-done | bytes 262176 | tf_op jit(solution)/shard_map/ppermute | solution.py:29
  21.9 1.7 %collective-permute-done.3 = f32[4,128,128]{2,1,0:T(8,128)S(1)} collective-permute-done((f32[4,128,128]{2,1,0:T(8,128)S(1)}, f32[4,128,128]{2,1,0:T(8,128)S(1)}, u32[]{:S(2)}, u32[]{:S(2)}) %collective-permute-start.3) | collective-permute-done | bytes 262176 | tf_op jit(solution)/shard_map/ppermute | solution.py:29
  23.7 1.5 %collective-permute-done.4 = f32[4,128,128]{2,1,0:T(8,128)} collective-permute-done((f32[4,128,128]{2,1,0:T(8,128)S(1)}, f32[4,128,128]{2,1,0:T(8,128)}, u32[]{:S(2)}, u32[]{:S(2)}) %collective-permute-start.4) | collective-permute-done | bytes 262176 | tf_op jit(solution)/shard_map/ppermute | solution.py:29
  25.2 3.3 %collective-permute-start.5 = (f32[16,128,128]{2,1,0:T(8,128)S(1)}, f32[16,128,128]{2,1,0:T(8,128)S(1)}, u32[]{:S(2)}, u32[]{:S(2)}) collective-permute-start(f32[16,128,128]{2,1,0:T(8,128)S(1)} %pad_maximum_fusion.own), channel_id=1, source_target_pairs={{0,32},{1,33},{2,34},{3,35},{4,36},{5,37},{6,38},{7,39},{8,40},{9,... | collective-permute-start | bytes 3145736 | tf_op jit(solution)/shard_map/ppermute | solution.py:29
  28.5 3.6 %collective-permute-start.9 = (f32[4,128,128]{2,1,0:T(8,128)S(1)}, f32[4,128,128]{2,1,0:T(8,128)S(1)}, u32[]{:S(2)}, u32[]{:S(2)}) collective-permute-start(f32[4,128,128]{2,1,0:T(8,128)S(1)} %multiply_add_fusion), channel_id=1, source_target_pairs={{0,3},{1,0},{2,1},{3,2},{4,35},{5,32},{6,33},{7,34},{8,11},{9,8},{... | collective-permute-start | bytes 786440 | tf_op jit(solution)/shard_map/ppermute | solution.py:29
  34.9 3.9 %collective-permute-start.6 = (f32[4,128,128]{2,1,0:T(8,128)S(1)}, f32[4,128,128]{2,1,0:T(8,128)S(1)}, u32[]{:S(2)}, u32[]{:S(2)}) collective-permute-start(f32[4,128,128]{2,1,0:T(8,128)S(1)} %multiply_add_fusion), channel_id=1, source_target_pairs={{0,0},{1,1},{2,2},{3,3},{4,32},{5,33},{6,34},{7,35},{8,8},{9,9},{1... | collective-permute-start | bytes 786440 | tf_op jit(solution)/shard_map/ppermute | solution.py:29
  38.9 1.6 %collective-permute-done.8 = f32[4,128,128]{2,1,0:T(8,128)S(1)} collective-permute-done((f32[4,128,128]{2,1,0:T(8,128)S(1)}, f32[4,128,128]{2,1,0:T(8,128)S(1)}, u32[]{:S(2)}, u32[]{:S(2)}) %collective-permute-start.8) | collective-permute-done | bytes 262176 | tf_op jit(solution)/shard_map/ppermute | solution.py:29
  40.4 3.8 %collective-permute-done.7 = f32[4,128,128]{2,1,0:T(8,128)S(1)} collective-permute-done((f32[4,128,128]{2,1,0:T(8,128)S(1)}, f32[4,128,128]{2,1,0:T(8,128)S(1)}, u32[]{:S(2)}, u32[]{:S(2)}) %collective-permute-start.7) | collective-permute-done | bytes 262176 | tf_op jit(solution)/shard_map/ppermute | solution.py:29
  44.3 4.3 %collective-permute-done.6 = f32[4,128,128]{2,1,0:T(8,128)S(1)} collective-permute-done((f32[4,128,128]{2,1,0:T(8,128)S(1)}, f32[4,128,128]{2,1,0:T(8,128)S(1)}, u32[]{:S(2)}, u32[]{:S(2)}) %collective-permute-start.6) | collective-permute-done | bytes 262176 | tf_op jit(solution)/shard_map/ppermute | solution.py:29
  49.3 1.6 %collective-permute-start.13 = (f32[4,128,128]{2,1,0:T(8,128)}, f32[4,128,128]{2,1,0:T(8,128)}, u32[]{:S(2)}, u32[]{:S(2)}) collective-permute-start(f32[4,128,128]{2,1,0:T(8,128)} %collective-permute-done.4), channel_id=1, source_target_pairs={{0,2},{1,3},{2,0},{3,1},{4,34},{5,35},{6,32},{7,33},{8,10},{9,11},... | collective-permute-start | bytes 786440 | tf_op jit(solution)/shard_map/ppermute | solution.py:29
  51.9 2.9 %collective-permute-start.11 = (f32[4,128,128]{2,1,0:T(8,128)}, f32[4,128,128]{2,1,0:T(8,128)}, u32[]{:S(2)}, u32[]{:S(2)}) collective-permute-start(f32[4,128,128]{2,1,0:T(8,128)} %collective-permute-done.4), channel_id=1, source_target_pairs={{0,0},{1,1},{2,2},{3,3},{4,32},{5,33},{6,34},{7,35},{8,8},{9,9},{1... | collective-permute-start | bytes 786440 | tf_op jit(solution)/shard_map/ppermute | solution.py:29
  56.2 9.1 %inner.1.edges = f32[32,144,128]{2,1,0:T(8,128)S(1)} custom-call(s32[2]{0:T(128)S(1)} %pad_add_fusion.place, f32[16,128,128]{2,1,0:T(8,128)S(1)} %pad_maximum_fusion.own, f32[16,128,128]{2,1,0:T(8,128)S(1)} %copy-done.1, f32[16,128,128]{2,1,0:T(8,128)S(1)} %constant_dynamic-update-slice_fusion.own_pot, f32[16,128,128]{2,1,0:T(8,128)} %collective-permute-done.15.sibling_pot, ...), custom_call_target="tpu_custom_call" | custom-call | flops 1000 | tf_op jit(solution)/shard_map/inner/pallas_call | solution.py:202
  65.3 10.8 %outer.1 = f32[16,128,128]{2,1,0:T(8,128)} custom-call(s32[2]{0:T(128)S(1)} %pad_add_fusion.place, f32[16,128,128]{2,1,0:T(8,128)S(1)} %collective-permute-done.10.outer, f32[4,128,128]{2,1,0:T(8,128)} %collective-permute-done.11.q0, f32[4,128,128]{2,1,0:T(8,128)} %collective-permute-done.12.q1, f32[4,128,128]{2,1,0:T(8,128)} %collective-permute-done.13.q2, ...), custom_call_target="tpu_custom_call" | custom-call | flops 1000 | tf_op jit(solution)/shard_map/outer/pallas_call | solution.py:202
  76.1 7.8 %all-to-all-start = ((f32[16,128,128]{2,1,0:T(8,128)}), f32[16,128,128]{2,1,0:T(8,128)S(1)}, u32[]{:S(2)}, u32[]{:S(2)}) async-start(f32[16,128,128]{2,1,0:T(8,128)} %outer.1), calls=%async_computation | async-start | bytes 2097152 | tf_op jit(solution)/shard_map/all_to_all | solution.py:330
  85.1 16.0 %all-to-all-done.x = f32[16,128,128]{2,1,0:T(8,128)S(1)} async-done(((f32[16,128,128]{2,1,0:T(8,128)}), f32[16,128,128]{2,1,0:T(8,128)S(1)}, u32[]{:S(2)}, u32[]{:S(2)}) %all-to-all-start) | async-done | bytes 1048608 | tf_op jit(solution)/shard_map/all_to_all | solution.py:330
  102.8 2.2 %collective-permute-done.20 = f32[8,256]{1,0:T(8,128)S(1)} collective-permute-done((f32[8,256]{1,0:T(8,128)S(1)}, f32[8,256]{1,0:T(8,128)S(1)}, u32[]{:S(2)}, u32[]{:S(2)}) %collective-permute-start.20) | collective-permute-done | bytes 8224 | tf_op jit(solution)/shard_map/ppermute | solution.py:29
  105.5 3.5 %collective-permute-done.21 = f32[8,256]{1,0:T(8,128)S(1)} collective-permute-done((f32[8,256]{1,0:T(8,128)S(1)}, f32[8,256]{1,0:T(8,128)S(1)}, u32[]{:S(2)}, u32[]{:S(2)}) %collective-permute-start.21) | collective-permute-done | bytes 8224 | tf_op jit(solution)/shard_map/ppermute | solution.py:29
  109.1 1.5 %rotate.2 = (f32[4,128,128]{2,1,0:T(8,128)S(1)}, f32[4,128,128]{2,1,0:T(8,128)S(1)}) custom-call(s32[1]{0:T(128)} %bitcast.place, f32[16,16]{1,0:T(8,128)S(1)} %copy-done.3, f32[16,128,128]{2,1,0:T(8,128)S(1)} %all-to-all-done.x), custom_call_target="tpu_custom_call" | custom-call | tf_op jit(solution)/shard_map/rotate/pallas_call | solution.py:249
  110.6 5.2 %collective-permute-start.16 = (f32[4,128,128]{2,1,0:T(8,128)S(1)}, f32[4,128,128]{2,1,0:T(8,128)S(1)}, u32[]{:S(2)}, u32[]{:S(2)}) collective-permute-start(f32[4,128,128]{2,1,0:T(8,128)S(1)} %get-tuple-element.42), channel_id=1, source_target_pairs={{0,0},{1,1},{2,2},{3,3},{4,32},{5,33},{6,34},{7,35},{8,8},{9,9},{1... | collective-permute-start | bytes 786440 | tf_op jit(solution)/shard_map/ppermute | solution.py:29
  115.9 1.6 %rotate.3 = (f32[4,128,128]{2,1,0:T(8,128)S(1)}, f32[4,128,128]{2,1,0:T(8,128)S(1)}) custom-call(s32[1]{0:T(128)} %bitcast.place, f32[16,16]{1,0:T(8,128)S(1)} %copy-done.3, f32[16,128,128]{2,1,0:T(8,128)S(1)} %all-to-all-done.x), custom_call_target="tpu_custom_call" | custom-call | tf_op jit(solution)/shard_map/rotate/pallas_call | solution.py:249
  117.5 1.6 %collective-permute-start.18 = (f32[4,128,128]{2,1,0:T(8,128)S(1)}, f32[4,128,128]{2,1,0:T(8,128)S(1)}, u32[]{:S(2)}, u32[]{:S(2)}) collective-permute-start(f32[4,128,128]{2,1,0:T(8,128)S(1)} %get-tuple-element.44), channel_id=1, source_target_pairs={{0,64},{1,65},{2,66},{3,67},{4,96},{5,97},{6,98},{7,99},{8,72},{9,... | collective-permute-start | bytes 786440 | tf_op jit(solution)/shard_map/ppermute | solution.py:29
  120.1 2.5 %collective-permute-start.23 = (f32[8,256]{1,0:T(8,128)S(1)}, f32[8,256]{1,0:T(8,128)S(1)}, u32[]{:S(2)}, u32[]{:S(2)}) collective-permute-start(f32[8,256]{1,0:T(8,128)S(1)} %add.89), channel_id=1, source_target_pairs={{0,16},{1,17},{2,18},{3,19},{4,20},{5,21},{6,22},{7,23},{8,24},{9,... | collective-permute-start | bytes 24584 | tf_op jit(solution)/shard_map/ppermute | solution.py:29
  122.5 1.8 %collective-permute-done.23 = f32[8,256]{1,0:T(8,128)S(1)} collective-permute-done((f32[8,256]{1,0:T(8,128)S(1)}, f32[8,256]{1,0:T(8,128)S(1)}, u32[]{:S(2)}, u32[]{:S(2)}) %collective-permute-start.23) | collective-permute-done | bytes 8224 | tf_op jit(solution)/shard_map/ppermute | solution.py:29
  124.4 1.9 %collective-permute-start.24 = (f32[8,256]{1,0:T(8,128)S(1)}, f32[8,256]{1,0:T(8,128)S(1)}, u32[]{:S(2)}, u32[]{:S(2)}) collective-permute-start(f32[8,256]{1,0:T(8,128)S(1)} %add.90), channel_id=1, source_target_pairs={{0,32},{1,33},{2,34},{3,35},{4,36},{5,37},{6,38},{7,39},{8,40},{9,... | collective-permute-start | bytes 24584 | tf_op jit(solution)/shard_map/ppermute | solution.py:29
  127.3 2.6 %collective-permute-done.25 = f32[8,256]{1,0:T(8,128)S(1)} collective-permute-done((f32[8,256]{1,0:T(8,128)S(1)}, f32[8,256]{1,0:T(8,128)S(1)}, u32[]{:S(2)}, u32[]{:S(2)}) %collective-permute-start.25) | collective-permute-done | bytes 8224 | tf_op jit(solution)/shard_map/ppermute | solution.py:29
  129.9 2.6 %collective-permute-start.26 = (f32[8,256]{1,0:T(8,128)S(1)}, f32[8,256]{1,0:T(8,128)S(1)}, u32[]{:S(2)}, u32[]{:S(2)}) collective-permute-start(f32[8,256]{1,0:T(8,128)S(1)} %add.92), channel_id=1, source_target_pairs={{0,64},{1,65},{2,66},{3,67},{4,68},{5,69},{6,70},{7,71},{8,72},{9,... | collective-permute-start | bytes 24584 | tf_op jit(solution)/shard_map/ppermute | solution.py:29
  132.5 1.4 %collective-permute-done.26 = f32[8,256]{1,0:T(8,128)S(1)} collective-permute-done((f32[8,256]{1,0:T(8,128)S(1)}, f32[8,256]{1,0:T(8,128)S(1)}, u32[]{:S(2)}, u32[]{:S(2)}) %collective-permute-start.26) | collective-permute-done | bytes 8224 | tf_op jit(solution)/shard_map/ppermute | solution.py:29
  (61 shorter events, 14.0 us)
Async XLA Ops:
  0.6 12.6 %copy-start.4 = (f32[4,128,128]{2,1,0:T(8,128)S(1)}, f32[4,128,128]{2,1,0:T(8,128)}, u32[]{:S(2)}) copy-start(f32[4,128,128]{2,1,0:T(8,128)} %param.6) | copy-start | bytes 786436
  2.0 11.3 %collective-permute-start = (f32[4,128,128]{2,1,0:T(8,128)S(1)}, f32[4,128,128]{2,1,0:T(8,128)S(1)}, u32[]{:S(2)}, u32[]{:S(2)}) collective-permute-start(f32[4,128,128]{2,1,0:T(8,128)S(1)} %get-tuple-element.52), channel_id=1, source_target_pairs={{0,0},{1,1},{2,2},{3,3},{4,32},{5,33},{6,34},{7,35},{8,8},{9,9},{1... | collective-permute-start | bytes 786440 | tf_op jit(solution)/shard_map/ppermute | solution.py:29
  6.5 10.7 %collective-permute-start.1 = (f32[4,128,128]{2,1,0:T(8,128)S(1)}, f32[4,128,128]{2,1,0:T(8,128)S(1)}, u32[]{:S(2)}, u32[]{:S(2)}) collective-permute-start(f32[4,128,128]{2,1,0:T(8,128)S(1)} %get-tuple-element.53), channel_id=1, source_target_pairs={{0,1},{1,2},{2,3},{3,0},{4,33},{5,34},{6,35},{7,32},{8,9},{9,10},{... | collective-permute-start | bytes 786440 | tf_op jit(solution)/shard_map/ppermute | solution.py:29
  8.0 13.9 %collective-permute-start.2 = (f32[4,128,128]{2,1,0:T(8,128)S(1)}, f32[4,128,128]{2,1,0:T(8,128)S(1)}, u32[]{:S(2)}, u32[]{:S(2)}) collective-permute-start(f32[4,128,128]{2,1,0:T(8,128)S(1)} %get-tuple-element.55), channel_id=1, source_target_pairs={{0,2},{1,3},{2,0},{3,1},{4,34},{5,35},{6,32},{7,33},{8,10},{9,11},... | collective-permute-start | bytes 786440 | tf_op jit(solution)/shard_map/ppermute | solution.py:29
  12.7 10.9 %collective-permute-start.3 = (f32[4,128,128]{2,1,0:T(8,128)S(1)}, f32[4,128,128]{2,1,0:T(8,128)S(1)}, u32[]{:S(2)}, u32[]{:S(2)}) collective-permute-start(f32[4,128,128]{2,1,0:T(8,128)S(1)} %get-tuple-element.54), channel_id=1, source_target_pairs={{0,3},{1,0},{2,1},{3,2},{4,35},{5,32},{6,33},{7,34},{8,11},{9,8},{... | collective-permute-start | bytes 786440 | tf_op jit(solution)/shard_map/ppermute | solution.py:29
  13.2 41.7 %copy-start.2 = (bf16[256,128]{1,0:T(8,128)(2,1)S(1)}, bf16[256,128]{1,0:T(8,128)(2,1)}, u32[]{:S(2)}) copy-start(bf16[256,128]{1,0:T(8,128)(2,1)} %constant.69.clone.matrix) | copy-start | bytes 196612
  13.2 11.9 %collective-permute-start.4 = (f32[4,128,128]{2,1,0:T(8,128)S(1)}, f32[4,128,128]{2,1,0:T(8,128)}, u32[]{:S(2)}, u32[]{:S(2)}) collective-permute-start(f32[4,128,128]{2,1,0:T(8,128)S(1)} %multiply_add_fusion), channel_id=1, source_target_pairs={{0,28},{1,29},{2,30},{3,31},{4,8},{5,9},{6,10},{7,11},{8,4},{9,5},... | collective-permute-start | bytes 786440 | tf_op jit(solution)/shard_map/ppermute | solution.py:29
  25.2 8.8 %collective-permute-start.5 = (f32[16,128,128]{2,1,0:T(8,128)S(1)}, f32[16,128,128]{2,1,0:T(8,128)S(1)}, u32[]{:S(2)}, u32[]{:S(2)}) collective-permute-start(f32[16,128,128]{2,1,0:T(8,128)S(1)} %pad_maximum_fusion.own), channel_id=1, source_target_pairs={{0,32},{1,33},{2,34},{3,35},{4,36},{5,37},{6,38},{7,39},{8,40},{9,... | collective-permute-start | bytes 3145736 | tf_op jit(solution)/shard_map/ppermute | solution.py:29
  28.5 20.1 %collective-permute-start.10 = (f32[16,128,128]{2,1,0:T(8,128)S(1)}, f32[16,128,128]{2,1,0:T(8,128)S(1)}, u32[]{:S(2)}, u32[]{:S(2)}) collective-permute-start(f32[16,128,128]{2,1,0:T(8,128)S(1)} %pad_maximum_fusion.own), channel_id=1, source_target_pairs={{0,56},{1,57},{2,58},{3,59},{4,60},{5,61},{6,62},{7,63},{8,32},{9,... | collective-permute-start | bytes 3145736 | tf_op jit(solution)/shard_map/ppermute | solution.py:29
  28.5 10.4 %collective-permute-start.9 = (f32[4,128,128]{2,1,0:T(8,128)S(1)}, f32[4,128,128]{2,1,0:T(8,128)S(1)}, u32[]{:S(2)}, u32[]{:S(2)}) collective-permute-start(f32[4,128,128]{2,1,0:T(8,128)S(1)} %multiply_add_fusion), channel_id=1, source_target_pairs={{0,3},{1,0},{2,1},{3,2},{4,35},{5,32},{6,33},{7,34},{8,11},{9,8},{... | collective-permute-start | bytes 786440 | tf_op jit(solution)/shard_map/ppermute | solution.py:29
  32.0 8.4 %collective-permute-start.8 = (f32[4,128,128]{2,1,0:T(8,128)S(1)}, f32[4,128,128]{2,1,0:T(8,128)S(1)}, u32[]{:S(2)}, u32[]{:S(2)}) collective-permute-start(f32[4,128,128]{2,1,0:T(8,128)S(1)} %multiply_add_fusion), channel_id=1, source_target_pairs={{0,2},{1,3},{2,0},{3,1},{4,34},{5,35},{6,32},{7,33},{8,10},{9,11},... | collective-permute-start | bytes 786440 | tf_op jit(solution)/shard_map/ppermute | solution.py:29
  32.9 11.4 %collective-permute-start.7 = (f32[4,128,128]{2,1,0:T(8,128)S(1)}, f32[4,128,128]{2,1,0:T(8,128)S(1)}, u32[]{:S(2)}, u32[]{:S(2)}) collective-permute-start(f32[4,128,128]{2,1,0:T(8,128)S(1)} %multiply_add_fusion), channel_id=1, source_target_pairs={{0,1},{1,2},{2,3},{3,0},{4,33},{5,34},{6,35},{7,32},{8,9},{9,10},{... | collective-permute-start | bytes 786440 | tf_op jit(solution)/shard_map/ppermute | solution.py:29
  34.9 13.6 %collective-permute-start.6 = (f32[4,128,128]{2,1,0:T(8,128)S(1)}, f32[4,128,128]{2,1,0:T(8,128)S(1)}, u32[]{:S(2)}, u32[]{:S(2)}) collective-permute-start(f32[4,128,128]{2,1,0:T(8,128)S(1)} %multiply_add_fusion), channel_id=1, source_target_pairs={{0,0},{1,1},{2,2},{3,3},{4,32},{5,33},{6,34},{7,35},{8,8},{9,9},{1... | collective-permute-start | bytes 786440 | tf_op jit(solution)/shard_map/ppermute | solution.py:29
  48.6 6.3 %collective-permute-start.15 = (f32[16,128,128]{2,1,0:T(8,128)S(1)}, f32[16,128,128]{2,1,0:T(8,128)}, u32[]{:S(2)}, u32[]{:S(2)}) collective-permute-start(f32[16,128,128]{2,1,0:T(8,128)S(1)} %constant_dynamic-update-slice_fusion.own_pot), channel_id=1, source_target_pairs={{0,32},{1,33},{2,34},{3,35},{4,36},{5,37},{6,38},{7,39},{8,40},{9,... | collective-permute-start | bytes 3145736 | tf_op jit(solution)/shard_map/ppermute | solution.py:29
  49.3 16.0 %collective-permute-start.14 = (f32[4,128,128]{2,1,0:T(8,128)}, f32[4,128,128]{2,1,0:T(8,128)S(1)}, u32[]{:S(2)}, u32[]{:S(2)}) collective-permute-start(f32[4,128,128]{2,1,0:T(8,128)} %collective-permute-done.4), channel_id=1, source_target_pairs={{0,3},{1,0},{2,1},{3,2},{4,35},{5,32},{6,33},{7,34},{8,11},{9,8},{... | collective-permute-start | bytes 786440 | tf_op jit(solution)/shard_map/ppermute | solution.py:29
  49.3 16.0 %collective-permute-start.13 = (f32[4,128,128]{2,1,0:T(8,128)}, f32[4,128,128]{2,1,0:T(8,128)}, u32[]{:S(2)}, u32[]{:S(2)}) collective-permute-start(f32[4,128,128]{2,1,0:T(8,128)} %collective-permute-done.4), channel_id=1, source_target_pairs={{0,2},{1,3},{2,0},{3,1},{4,34},{5,35},{6,32},{7,33},{8,10},{9,11},... | collective-permute-start | bytes 786440 | tf_op jit(solution)/shard_map/ppermute | solution.py:29
  50.9 14.4 %collective-permute-start.12 = (f32[4,128,128]{2,1,0:T(8,128)}, f32[4,128,128]{2,1,0:T(8,128)}, u32[]{:S(2)}, u32[]{:S(2)}) collective-permute-start(f32[4,128,128]{2,1,0:T(8,128)} %collective-permute-done.4), channel_id=1, source_target_pairs={{0,1},{1,2},{2,3},{3,0},{4,33},{5,34},{6,35},{7,32},{8,9},{9,10},{... | collective-permute-start | bytes 786440 | tf_op jit(solution)/shard_map/ppermute | solution.py:29
  51.9 13.4 %collective-permute-start.11 = (f32[4,128,128]{2,1,0:T(8,128)}, f32[4,128,128]{2,1,0:T(8,128)}, u32[]{:S(2)}, u32[]{:S(2)}) collective-permute-start(f32[4,128,128]{2,1,0:T(8,128)} %collective-permute-done.4), channel_id=1, source_target_pairs={{0,0},{1,1},{2,2},{3,3},{4,32},{5,33},{6,34},{7,35},{8,8},{9,9},{1... | collective-permute-start | bytes 786440 | tf_op jit(solution)/shard_map/ppermute | solution.py:29
  54.9 1.2 copy-start.1
  76.1 7.9 %copy-start.3 = (f32[16,16]{1,0:T(8,128)S(1)}, f32[16,16]{1,0:T(8,128)}, u32[]{:S(2)}) copy-start(f32[16,16]{1,0:T(8,128)} %rotation.3) | copy-start | bytes 3076
  76.1 25.0 %all-to-all-start = ((f32[16,128,128]{2,1,0:T(8,128)}), f32[16,128,128]{2,1,0:T(8,128)S(1)}, u32[]{:S(2)}, u32[]{:S(2)}) async-start(f32[16,128,128]{2,1,0:T(8,128)} %outer.1), calls=%async_computation | async-start | bytes 2097152 | tf_op jit(solution)/shard_map/all_to_all | solution.py:330
  102.5 2.5 %collective-permute-start.20 = (f32[8,256]{1,0:T(8,128)S(1)}, f32[8,256]{1,0:T(8,128)S(1)}, u32[]{:S(2)}, u32[]{:S(2)}) collective-permute-start(f32[8,256]{1,0:T(8,128)S(1)} %gram.1), channel_id=1, source_target_pairs={{0,1},{1,0},{2,3},{3,2},{4,5},{5,4},{6,7},{7,6},{8,9},{9,8},{10,11... | collective-permute-start | bytes 24584 | tf_op jit(solution)/shard_map/ppermute | solution.py:29
  105.0 4.0 %collective-permute-start.21 = (f32[8,256]{1,0:T(8,128)S(1)}, f32[8,256]{1,0:T(8,128)S(1)}, u32[]{:S(2)}, u32[]{:S(2)}) collective-permute-start(f32[8,256]{1,0:T(8,128)S(1)} %add.87), channel_id=1, source_target_pairs={{0,2},{1,3},{2,0},{3,1},{4,6},{5,7},{6,4},{7,5},{8,10},{9,11},{10,... | collective-permute-start | bytes 24584 | tf_op jit(solution)/shard_map/ppermute | solution.py:29
  109.0 11.1 %collective-permute-start.22 = (f32[8,256]{1,0:T(8,128)S(1)}, f32[8,256]{1,0:T(8,128)S(1)}, u32[]{:S(2)}, u32[]{:S(2)}) collective-permute-start(f32[8,256]{1,0:T(8,128)S(1)} %add.88), channel_id=1, source_target_pairs={{0,8},{1,9},{2,10},{3,11},{4,12},{5,13},{6,14},{7,15},{8,0},{9,1},... | collective-permute-start | bytes 24584 | tf_op jit(solution)/shard_map/ppermute | solution.py:29
  110.6 24.0 %collective-permute-start.16 = (f32[4,128,128]{2,1,0:T(8,128)S(1)}, f32[4,128,128]{2,1,0:T(8,128)S(1)}, u32[]{:S(2)}, u32[]{:S(2)}) collective-permute-start(f32[4,128,128]{2,1,0:T(8,128)S(1)} %get-tuple-element.42), channel_id=1, source_target_pairs={{0,0},{1,1},{2,2},{3,3},{4,32},{5,33},{6,34},{7,35},{8,8},{9,9},{1... | collective-permute-start | bytes 786440 | tf_op jit(solution)/shard_map/ppermute | solution.py:29
  115.8 18.8 %collective-permute-start.17 = (f32[4,128,128]{2,1,0:T(8,128)S(1)}, f32[4,128,128]{2,1,0:T(8,128)S(1)}, u32[]{:S(2)}, u32[]{:S(2)}) collective-permute-start(f32[4,128,128]{2,1,0:T(8,128)S(1)} %get-tuple-element.43), channel_id=1, source_target_pairs={{0,32},{1,33},{2,34},{3,35},{4,0},{5,1},{6,2},{7,3},{8,40},{9,41},... | collective-permute-start | bytes 786440 | tf_op jit(solution)/shard_map/ppermute | solution.py:29
  117.5 17.1 %collective-permute-start.18 = (f32[4,128,128]{2,1,0:T(8,128)S(1)}, f32[4,128,128]{2,1,0:T(8,128)S(1)}, u32[]{:S(2)}, u32[]{:S(2)}) collective-permute-start(f32[4,128,128]{2,1,0:T(8,128)S(1)} %get-tuple-element.44), channel_id=1, source_target_pairs={{0,64},{1,65},{2,66},{3,67},{4,96},{5,97},{6,98},{7,99},{8,72},{9,... | collective-permute-start | bytes 786440 | tf_op jit(solution)/shard_map/ppermute | solution.py:29
  119.1 15.5 %collective-permute-start.19 = (f32[4,128,128]{2,1,0:T(8,128)S(1)}, f32[4,128,128]{2,1,0:T(8,128)S(1)}, u32[]{:S(2)}, u32[]{:S(2)}) collective-permute-start(f32[4,128,128]{2,1,0:T(8,128)S(1)} %get-tuple-element.45), channel_id=1, source_target_pairs={{0,96},{1,97},{2,98},{3,99},{4,64},{5,65},{6,66},{7,67},{8,104},{9... | collective-permute-start | bytes 786440 | tf_op jit(solution)/shard_map/ppermute | solution.py:29
  120.1 4.3 %collective-permute-start.23 = (f32[8,256]{1,0:T(8,128)S(1)}, f32[8,256]{1,0:T(8,128)S(1)}, u32[]{:S(2)}, u32[]{:S(2)}) collective-permute-start(f32[8,256]{1,0:T(8,128)S(1)} %add.89), channel_id=1, source_target_pairs={{0,16},{1,17},{2,18},{3,19},{4,20},{5,21},{6,22},{7,23},{8,24},{9,... | collective-permute-start | bytes 24584 | tf_op jit(solution)/shard_map/ppermute | solution.py:29
  124.4 2.7 %collective-permute-start.24 = (f32[8,256]{1,0:T(8,128)S(1)}, f32[8,256]{1,0:T(8,128)S(1)}, u32[]{:S(2)}, u32[]{:S(2)}) collective-permute-start(f32[8,256]{1,0:T(8,128)S(1)} %add.90), channel_id=1, source_target_pairs={{0,32},{1,33},{2,34},{3,35},{4,36},{5,37},{6,38},{7,39},{8,40},{9,... | collective-permute-start | bytes 24584 | tf_op jit(solution)/shard_map/ppermute | solution.py:29
  127.1 2.8 %collective-permute-start.25 = (f32[8,256]{1,0:T(8,128)S(1)}, f32[8,256]{1,0:T(8,128)S(1)}, u32[]{:S(2)}, u32[]{:S(2)}) collective-permute-start(f32[8,256]{1,0:T(8,128)S(1)} %add.91), channel_id=1, source_target_pairs={{0,4},{1,5},{2,6},{3,7},{4,0},{5,1},{6,2},{7,3},{8,12},{9,13},{10,... | collective-permute-start | bytes 24584 | tf_op jit(solution)/shard_map/ppermute | solution.py:29
  129.9 4.0 %collective-permute-start.26 = (f32[8,256]{1,0:T(8,128)S(1)}, f32[8,256]{1,0:T(8,128)S(1)}, u32[]{:S(2)}, u32[]{:S(2)}) collective-permute-start(f32[8,256]{1,0:T(8,128)S(1)} %add.92), channel_id=1, source_target_pairs={{0,64},{1,65},{2,66},{3,67},{4,68},{5,69},{6,70},{7,71},{8,72},{9,... | collective-permute-start | bytes 24584 | tf_op jit(solution)/shard_map/ppermute | solution.py:29
  (1 other events, 1.0 us)

commit v4 on v3

--- a/solution.py
+++ b/solution.py
@@ -37,8 +37,8 @@
     return {**c, "core": 1 - c["core"], "y": c["y"] + (1 if c["core"] == 1 else -1)}
 
 
-def to_outer_natively(c):
-    return {**c, "x_lo": 1 - c["x_lo"], "y": c["y"] + (1 if c["x_lo"] == 1 else -1)}
+def pot_to_orbital(shift):
+    return lambda c: {**to_orbital(shift)(c), "x_hi": c["x_hi"] ^ c["core"] ^ c["x_lo"]}
 
 
 def to_sibling(c):
@@ -68,14 +68,12 @@
     return jnp.asarray(np.concatenate([m, m], axis=0), jnp.bfloat16)
 
 
-def place_blocks(refs, target, first, z, sems, copies):
-    if not isinstance(refs, (list, tuple)):
-        refs = [refs.at[pl.ds(4 * shift, 4)] for shift in range(4)]
+def place_blocks(ref, target, first, z, sems, copies):
     for shift in range(4):
         where = first + 4 * lax.rem(z + 4 - shift, 4)
         copies.append(
             pltpu.make_async_copy(
-                refs[shift],
+                ref.at[pl.ds(4 * shift, 4)],
                 target.at[pl.ds(where, 4), pl.ds(PAD, N), :],
                 sems.at[len(copies)],
             )
@@ -152,12 +150,12 @@
 
 
 def outer_kernel(
-    place, outer, q0, q1, q2, q3, own_pot, edges, matrix, out, one, two, pot, along, sems
+    place, outer, outer_pot, own_pot, edges, matrix, out, one, two, pot, along, sems
 ):
     core, z = place[0], place[1]
     copies = []
     place_blocks(outer, one, 18 * core, z, sems, copies)
-    place_blocks((q0, q1, q2, q3), pot, 18 * core, z, sems, copies)
+    place_blocks(outer_pot, pot, 18 * core, z, sems, copies)
     place_blocks(own_pot, pot, 16 - 14 * core, z, sems, copies)
     for copy in copies:
         copy.start()
@@ -214,14 +212,14 @@
     )(*args, stencil_matrix())
 
 
-def filtered(place, own, sibling, outer, own_pot, sibling_pot, outer_pots):
+def filtered(place, own, sibling, outer, own_pot, sibling_pot, outer_pot):
     edges = filter_call(
         inner_kernel, "inner", 2 * OWN, [pl.ANY] * 4, (4 * DEGREE, ROWS, N), pltpu.VMEM,
         (place, own, sibling, own_pot, sibling_pot),
     )
     return filter_call(
-        outer_kernel, "outer", 2 * OWN + 2, [pl.ANY] * 6 + [pltpu.VMEM], (OWN, N, N), pl.ANY,
-        (place, outer, *outer_pots, own_pot, edges),
+        outer_kernel, "outer", 2 * OWN + 2, [pl.ANY] * 3 + [pltpu.VMEM], (OWN, N, N), pl.ANY,
+        (place, outer, outer_pot, own_pot, edges),
     )
 
 
@@ -272,7 +270,7 @@
                 if k < i:
                     sums[16 * k + i : 16 * k + i + 1, :] = total
     gram = lax.dot_general(
-        jnp.ones((8, N), jnp.float32),
+        jnp.ones((16, N), jnp.float32),
         sums[...],
         (((1,), (1,)), ((), ())),
         precision=lax.Precision.HIGHEST,
@@ -287,7 +285,7 @@
     vmem = pl.BlockSpec(memory_space=pltpu.VMEM)
     return pl.pallas_call(
         gram_kernel,
-        out_shape=jax.ShapeDtypeStruct((8, 256), jnp.float32),
+        out_shape=jax.ShapeDtypeStruct((16, 256), jnp.float32),
         in_specs=[vmem] * 2,
         out_specs=vmem,
         scratch_shapes=[pltpu.VMEM((256, N), jnp.float32)],
@@ -309,37 +307,35 @@
         for s in range(4)
     ]
     diagonal = FACTOR * potential + DIAG
-    beyond = moved(diagonal, to_outer_natively)
     own = jnp.concatenate(orbs, axis=0)
-    own, diagonal, beyond = lax.optimization_barrier((own, diagonal, beyond))
+    own, diagonal = lax.optimization_barrier((own, diagonal))
     outer = moved(own, to_outer)
     sibling = moved(own, to_sibling)
-    pots, outer_pots = [None] * 4, []
+    pots = [None] * 4
     for s in (1, 3, 2, 0):
         sent = diagonal
         if s == 0:
             sent, sibling = lax.optimization_barrier((diagonal, sibling))
-        pots[s] = moved(sent, to_orbital(s))
-    for s in range(4):
-        sent, pots[s] = lax.optimization_barrier((beyond, pots[s]))
-        outer_pots.append(moved(sent, to_orbital(s)))
+        pots[s] = moved(sent, pot_to_orbital(s))
     pots, outer = lax.optimization_barrier((pots, outer))
     own_pot = jnp.concatenate(pots, axis=0)
+    outer_pot = moved(own_pot, to_outer)
     sibling_pot = moved(own_pot, to_sibling)
-    mine = filtered(place, own, sibling, outer, own_pot, sibling_pot, outer_pots)
+    mine = filtered(place, own, sibling, outer, own_pot, sibling_pot, outer_pot)
     planes = lax.all_to_all(mine, ("x_hi", "x_lo", "z"), 0, 0, tiled=True)
     base = jnp.stack([2 * x_hi + x_lo]).astype(jnp.int32)
     square = (rotation[:, None, :, None] * rotation[None, :, None, :]).reshape(256, 256)
-    total = gram_row(planes, square)
+    rows = lax.all_to_all(gram_row(planes, square), ("y", "z"), 0, 0, tiled=True)
     far = rotated_parts(2, base, rotation, planes)
     near = rotated_parts(0, base, rotation, planes)
     home = [None] * 4
     home[2], home[3] = moved(far[0], to_home(1, 0)), moved(far[1], to_home(1, 1))
     home[0], home[1] = moved(near[0], to_home(0, 0)), moved(near[1], to_home(0, 1))
-    stages = (("z", 1), ("z", 2), ("y", 1), ("y", 2), ("core", 1), ("x_lo", 1), ("x_hi", 1))
-    for axis, bit in stages:
-        total = total + moved(total, lambda c: {**c, axis: c[axis] ^ bit})
-    total = total[0].reshape(16, 16) / (N * N * N)
+    total = jnp.sum(rows, axis=0, keepdims=True)
+    total, home[0] = lax.optimization_barrier((total, home[0]))
+    for axis in ("core", "x_lo", "x_hi"):
+        total = total + moved(total, lambda c: {**c, axis: 1 - c[axis]})
+    total = total.reshape(16, 16) / (N * N * N)
     correlation = lax.dynamic_slice_in_dim(total, 4 * (2 * x_hi + core), 4, 0)
     band = 2 * x_hi + core
     pieces = []

time: 138 us -> 128 us (0.928)
  starting transfers between devices: 53.8 us -> 46.5 us
  waiting for transfers between devices: 49.9 us -> 44.2 us
  local copies, waits for them, and re-layouts: 6.28 us -> 8.42 us
    ppermute x27 -> x19, waiting for transfers between devices: 33.9 us -> 22.6 us  [moved(): return lax.ppermute(array, AXES, pairs)]
    ppermute x27 -> x19, starting transfers between devices: 45.9 us -> 36.7 us  [moved(): return lax.ppermute(array, AXES, pairs)]
    all_to_all x0 -> x1, waiting for transfers between devices: none -> 6.44 us  [local(): lax.all_to_all(gram_row(planes, square), ('y', 'z'), 0, 0, tiled=True)]
    all_to_all x0 -> x1, starting transfers between devices: none -> 4.91 us  [local(): lax.all_to_all(gram_row(planes, square), ('y', 'z'), 0, 0, tiled=True)]
    all_to_all x1, starting transfers between devices: 7.83 us -> 4.93 us  [local(): planes = lax.all_to_all(mine, ('x_hi', 'x_lo', 'z'), 0, 0, tiled=True)]
    mul x1, local copies, waits for them, and re-layouts: 0.94 us -> 2.44 us  [local(): rotation[:, None, :, None] * rotation[None, :, None, :]]
  transfers between devices with their start and end apart: 28 -> 21, of which waited for: 14 -> 13; matrix products, arithmetic and copies ran while one was open for 2% -> 5% of each run, Pallas kernels for 9% -> 9%
where the time goes in v4:
time: 128 us; the launch traced here: 126 us
  starting transfers between devices  46.5 us (36%)
  waiting for transfers between devices  44.2 us (35%)
  Pallas kernels  24.4 us (19%)
  local copies, waits for them, and re-layouts  8.42 us (7%)
  other arithmetic  2.01 us (2%)
    ppermute x19, starting transfers between devices, moved(): return lax.ppermute(array, AXES, pairs)  36.7 us
    ppermute x19, waiting for transfers between devices, moved(): return lax.ppermute(array, AXES, pairs)  22.6 us
    pallas_call x2, Pallas kernels, filter_call(): pl.pallas_call(kernel, out_shape=jax.ShapeDtypeStruct(shape, jnp.float32)...  19.9 us
    all_to_all x1, waiting for transfers between devices, local(): planes = lax.all_to_all(mine, ('x_hi', 'x_lo', 'z'), 0, 0, tiled=True)  15.2 us
    all_to_all x1, waiting for transfers between devices, local(): lax.all_to_all(gram_row(planes, square), ('y', 'z'), 0, 0, tiled=True)  6.44 us
    all_to_all x1, starting transfers between devices, local(): planes = lax.all_to_all(mine, ('x_hi', 'x_lo', 'z'), 0, 0, tiled=True)  4.93 us
    all_to_all x1, starting transfers between devices, local(): lax.all_to_all(gram_row(planes, square), ('y', 'z'), 0, 0, tiled=True)  4.91 us
    unnamed x14, local copies, waits for them, and re-layouts  3.34 us
  transfers between devices with their start and end apart: 21, of which 13 were waited for; matrix products, arithmetic and copies ran while one was open for 5% of the time, Pallas kernels for 9%

profile of v4, /device:TPU:1, one launch (start us, length us, event | category | flops | bytes accessed | tf_op | source)
XLA Modules:
  0.0 126.5 jit_solution(10827100210044748177)
XLA Ops:
  0.7 1.3 %dynamic-slice_bitcast_fusion.3 = (f32[4,128,128]{2,1,0:T(8,128)S(1)}, f32[4,128,128]{2,1,0:T(8,128)S(1)}, f32[4,128,128]{2,1,0:T(8,128)S(1)}, f32[4,128,128]{2,1,0:T(8,128)S(1)}) fusion(f32[4,4,128,128]{3,2,1,0:T(8,128)} %param.5, s32[]{:T(128)S(6)} %select_n.112, s32[]{:T(128)S(6)} %select_n.114, s32[]{:T(128)S(6)} %select_n.118, s32[]{:T(128)S(6)} %select_n.116), kind=kLoop, calls=%fused_computation.11 | loop fusion | bytes 2097168 | tf_op jit(solution)/shard_map/jit(dynamic_index_in_dim)/squeeze | solution.py:305
  2.0 4.5 %collective-permute-start = (f32[4,128,128]{2,1,0:T(8,128)S(1)}, f32[4,128,128]{2,1,0:T(8,128)S(1)}, u32[]{:S(2)}, u32[]{:S(2)}) collective-permute-start(f32[4,128,128]{2,1,0:T(8,128)S(1)} %get-tuple-element.40), channel_id=1, source_target_pairs={{0,0},{1,1},{2,2},{3,3},{4,32},{5,33},{6,34},{7,35},{8,8},{9,9},{1... | collective-permute-start | bytes 786440 | tf_op jit(solution)/shard_map/ppermute | solution.py:29
  6.5 1.4 %collective-permute-start.1 = (f32[4,128,128]{2,1,0:T(8,128)S(1)}, f32[4,128,128]{2,1,0:T(8,128)S(1)}, u32[]{:S(2)}, u32[]{:S(2)}) collective-permute-start(f32[4,128,128]{2,1,0:T(8,128)S(1)} %get-tuple-element.41), channel_id=1, source_target_pairs={{0,1},{1,2},{2,3},{3,0},{4,33},{5,34},{6,35},{7,32},{8,9},{9,10},{... | collective-permute-start | bytes 786440 | tf_op jit(solution)/shard_map/ppermute | solution.py:29
  8.0 4.8 %collective-permute-start.2 = (f32[4,128,128]{2,1,0:T(8,128)S(1)}, f32[4,128,128]{2,1,0:T(8,128)S(1)}, u32[]{:S(2)}, u32[]{:S(2)}) collective-permute-start(f32[4,128,128]{2,1,0:T(8,128)S(1)} %get-tuple-element.43), channel_id=1, source_target_pairs={{0,2},{1,3},{2,0},{3,1},{4,34},{5,35},{6,32},{7,33},{8,10},{9,11},... | collective-permute-start | bytes 786440 | tf_op jit(solution)/shard_map/ppermute | solution.py:29
  13.2 3.9 %collective-permute-done.1 = f32[4,128,128]{2,1,0:T(8,128)S(1)} collective-permute-done((f32[4,128,128]{2,1,0:T(8,128)S(1)}, f32[4,128,128]{2,1,0:T(8,128)S(1)}, u32[]{:S(2)}, u32[]{:S(2)}) %collective-permute-start.1) | collective-permute-done | bytes 262176 | tf_op jit(solution)/shard_map/ppermute | solution.py:29
  17.2 2.5 %collective-permute-done.2 = f32[4,128,128]{2,1,0:T(8,128)S(1)} collective-permute-done((f32[4,128,128]{2,1,0:T(8,128)S(1)}, f32[4,128,128]{2,1,0:T(8,128)S(1)}, u32[]{:S(2)}, u32[]{:S(2)}) %collective-permute-start.2) | collective-permute-done | bytes 262176 | tf_op jit(solution)/shard_map/ppermute | solution.py:29
  19.7 1.4 %collective-permute-done.3 = f32[4,128,128]{2,1,0:T(8,128)S(1)} collective-permute-done((f32[4,128,128]{2,1,0:T(8,128)S(1)}, f32[4,128,128]{2,1,0:T(8,128)S(1)}, u32[]{:S(2)}, u32[]{:S(2)}) %collective-permute-start.3) | collective-permute-done | bytes 262176 | tf_op jit(solution)/shard_map/ppermute | solution.py:29
  21.2 1.6 %collective-permute-start.4 = (f32[16,128,128]{2,1,0:T(8,128)S(1)}, f32[16,128,128]{2,1,0:T(8,128)S(1)}, u32[]{:S(2)}, u32[]{:S(2)}) collective-permute-start(f32[16,128,128]{2,1,0:T(8,128)S(1)} %pad_maximum_fusion.own), channel_id=1, source_target_pairs={{0,32},{1,33},{2,34},{3,35},{4,36},{5,37},{6,38},{7,39},{8,40},{9,... | collective-permute-start | bytes 3145736 | tf_op jit(solution)/shard_map/ppermute | solution.py:29
  22.7 1.3 %collective-permute-start.9 = (f32[16,128,128]{2,1,0:T(8,128)S(1)}, f32[16,128,128]{2,1,0:T(8,128)S(1)}, u32[]{:S(2)}, u32[]{:S(2)}) collective-permute-start(f32[16,128,128]{2,1,0:T(8,128)S(1)} %pad_maximum_fusion.own), channel_id=1, source_target_pairs={{0,56},{1,57},{2,58},{3,59},{4,60},{5,61},{6,62},{7,63},{8,32},{9,... | collective-permute-start | bytes 3145736 | tf_op jit(solution)/shard_map/ppermute | solution.py:29
  24.0 5.1 %collective-permute-start.6 = (f32[4,128,128]{2,1,0:T(8,128)S(1)}, f32[4,128,128]{2,1,0:T(8,128)S(1)}, u32[]{:S(2)}, u32[]{:S(2)}) collective-permute-start(f32[4,128,128]{2,1,0:T(8,128)S(1)} %multiply_add_fusion), channel_id=1, source_target_pairs={{0,1},{1,2},{2,3},{3,0},{4,97},{5,98},{6,99},{7,96},{8,9},{9,10},{... | collective-permute-start | bytes 786440 | tf_op jit(solution)/shard_map/ppermute | solution.py:29
  29.7 4.5 %collective-permute-start.8 = (f32[4,128,128]{2,1,0:T(8,128)S(1)}, f32[4,128,128]{2,1,0:T(8,128)S(1)}, u32[]{:S(2)}, u32[]{:S(2)}) collective-permute-start(f32[4,128,128]{2,1,0:T(8,128)S(1)} %multiply_add_fusion), channel_id=1, source_target_pairs={{0,3},{1,0},{2,1},{3,2},{4,99},{5,96},{6,97},{7,98},{8,11},{9,8},{... | collective-permute-start | bytes 786440 | tf_op jit(solution)/shard_map/ppermute | solution.py:29
  35.1 1.9 %collective-permute-start.5 = (f32[4,128,128]{2,1,0:T(8,128)S(1)}, f32[4,128,128]{2,1,0:T(8,128)S(1)}, u32[]{:S(2)}, u32[]{:S(2)}) collective-permute-start(f32[4,128,128]{2,1,0:T(8,128)S(1)} %multiply_add_fusion), channel_id=1, source_target_pairs={{0,0},{1,1},{2,2},{3,3},{4,96},{5,97},{6,98},{7,99},{8,8},{9,9},{1... | collective-permute-start | bytes 786440 | tf_op jit(solution)/shard_map/ppermute | solution.py:29
  37.0 1.5 %collective-permute-done.7 = f32[4,128,128]{2,1,0:T(8,128)S(1)} collective-permute-done((f32[4,128,128]{2,1,0:T(8,128)S(1)}, f32[4,128,128]{2,1,0:T(8,128)S(1)}, u32[]{:S(2)}, u32[]{:S(2)}) %collective-permute-start.7) | collective-permute-done | bytes 262176 | tf_op jit(solution)/shard_map/ppermute | solution.py:29
  39.3 4.7 %collective-permute-done.5 = f32[4,128,128]{2,1,0:T(8,128)S(1)} collective-permute-done((f32[4,128,128]{2,1,0:T(8,128)S(1)}, f32[4,128,128]{2,1,0:T(8,128)S(1)}, u32[]{:S(2)}, u32[]{:S(2)}) %collective-permute-start.5) | collective-permute-done | bytes 262176 | tf_op jit(solution)/shard_map/ppermute | solution.py:29
  44.4 2.6 %collective-permute-done.11.sibling_pot = f32[16,128,128]{2,1,0:T(8,128)} collective-permute-done((f32[16,128,128]{2,1,0:T(8,128)S(1)}, f32[16,128,128]{2,1,0:T(8,128)}, u32[]{:S(2)}, u32[]{:S(2)}) %collective-permute-start.11) | collective-permute-done | bytes 1048608 | tf_op jit(solution)/shard_map/ppermute | solution.py:29
  48.2 9.1 %inner.1.edges = f32[32,144,128]{2,1,0:T(8,128)S(1)} custom-call(s32[2]{0:T(128)S(1)} %pad_add_fusion.place, f32[16,128,128]{2,1,0:T(8,128)S(1)} %pad_maximum_fusion.own, f32[16,128,128]{2,1,0:T(8,128)S(1)} %copy-done.1, f32[16,128,128]{2,1,0:T(8,128)S(1)} %constant_dynamic-update-slice_fusion.own_pot, f32[16,128,128]{2,1,0:T(8,128)} %collective-permute-done.11.sibling_pot, ...), custom_call_target="tpu_custom_call" | custom-call | flops 1000 | tf_op jit(solution)/shard_map/inner/pallas_call | solution.py:200
  57.3 1.6 %collective-permute-done.10.outer_pot = f32[16,128,128]{2,1,0:T(8,128)} collective-permute-done((f32[16,128,128]{2,1,0:T(8,128)S(1)}, f32[16,128,128]{2,1,0:T(8,128)}, u32[]{:S(2)}, u32[]{:S(2)}) %collective-permute-start.10) | collective-permute-done | bytes 1048608 | tf_op jit(solution)/shard_map/ppermute | solution.py:29
  58.9 10.8 %outer.1 = f32[16,128,128]{2,1,0:T(8,128)} custom-call(s32[2]{0:T(128)S(1)} %pad_add_fusion.place, f32[16,128,128]{2,1,0:T(8,128)S(1)} %collective-permute-done.9.outer, f32[16,128,128]{2,1,0:T(8,128)} %collective-permute-done.10.outer_pot, f32[16,128,128]{2,1,0:T(8,128)S(1)} %constant_dynamic-update-slice_fusion.own_pot, f32[32,144,128]{2,1,0:T(8,128)S(1)} %inner.1.edges, ...), custom_call_target="tpu_custom_call" | custom-call | flops 1000 | tf_op jit(solution)/shard_map/outer/pallas_call | solution.py:200
  69.8 4.9 %all-to-all-start = ((f32[16,128,128]{2,1,0:T(8,128)}), f32[16,128,128]{2,1,0:T(8,128)S(1)}, u32[]{:S(2)}, u32[]{:S(2)}) async-start(f32[16,128,128]{2,1,0:T(8,128)} %outer.1), calls=%async_computation | async-start | bytes 2097152 | tf_op jit(solution)/shard_map/all_to_all | solution.py:325
  74.7 15.2 %all-to-all-done.x = f32[16,128,128]{2,1,0:T(8,128)S(1)} async-done(((f32[16,128,128]{2,1,0:T(8,128)}), f32[16,128,128]{2,1,0:T(8,128)S(1)}, u32[]{:S(2)}, u32[]{:S(2)}) %all-to-all-start) | async-done | bytes 1048608 | tf_op jit(solution)/shard_map/all_to_all | solution.py:325
  89.9 1.5 %rotate.2 = (f32[4,128,128]{2,1,0:T(8,128)S(1)}, f32[4,128,128]{2,1,0:T(8,128)S(1)}) custom-call(s32[1]{0:T(128)} %bitcast.8.place, f32[16,16]{1,0:T(8,128)S(1)} %copy-done.3, f32[16,128,128]{2,1,0:T(8,128)S(1)} %all-to-all-done.x), custom_call_target="tpu_custom_call" | custom-call | tf_op jit(solution)/shard_map/rotate/pallas_call | solution.py:247
  91.5 4.4 %collective-permute-start.12 = (f32[4,128,128]{2,1,0:T(8,128)S(1)}, f32[4,128,128]{2,1,0:T(8,128)S(1)}, u32[]{:S(2)}, u32[]{:S(2)}) collective-permute-start(f32[4,128,128]{2,1,0:T(8,128)S(1)} %get-tuple-element.26), channel_id=1, source_target_pairs={{0,0},{1,1},{2,2},{3,3},{4,32},{5,33},{6,34},{7,35},{8,8},{9,9},{1... | collective-permute-start | bytes 786440 | tf_op jit(solution)/shard_map/ppermute | solution.py:29
  96.0 1.6 %rotate.3 = (f32[4,128,128]{2,1,0:T(8,128)S(1)}, f32[4,128,128]{2,1,0:T(8,128)S(1)}) custom-call(s32[1]{0:T(128)} %bitcast.8.place, f32[16,16]{1,0:T(8,128)S(1)} %copy-done.3, f32[16,128,128]{2,1,0:T(8,128)S(1)} %all-to-all-done.x), custom_call_target="tpu_custom_call" | custom-call | tf_op jit(solution)/shard_map/rotate/pallas_call | solution.py:247
  97.5 1.3 %collective-permute-start.14 = (f32[4,128,128]{2,1,0:T(8,128)S(1)}, f32[4,128,128]{2,1,0:T(8,128)S(1)}, u32[]{:S(2)}, u32[]{:S(2)}) collective-permute-start(f32[4,128,128]{2,1,0:T(8,128)S(1)} %get-tuple-element.29), channel_id=1, source_target_pairs={{0,64},{1,65},{2,66},{3,67},{4,96},{5,97},{6,98},{7,99},{8,72},{9,... | collective-permute-start | bytes 786440 | tf_op jit(solution)/shard_map/ppermute | solution.py:29
  98.8 1.3 collective-permute-start.15
  100.1 1.5 %broadcast_multiply_fusion = f32[16,16,16,16]{3,2,1,0:T(8,128)} fusion(f32[16,16]{1,0:T(8,128)S(1)} %copy-done.3), kind=kLoop, calls=%fused_computation.2 | loop fusion | flops 65536 | bytes 263168 | tf_op jit(solution)/shard_map/mul | solution.py:327
  101.6 2.4 %mul.37.square = f32[256,256]{1,0:T(8,128)S(1)} reshape(f32[16,16,16,16]{3,2,1,0:T(8,128)} %broadcast_multiply_fusion) | data formatting | bytes 524288 | tf_op jit(solution)/shard_map/mul | solution.py:327
  104.1 1.3 %gram.1 = f32[16,256]{1,0:T(8,128)S(1)} custom-call(f32[16,128,128]{2,1,0:T(8,128)S(1)} %all-to-all-done.x, f32[256,256]{1,0:T(8,128)S(1)} %mul.37.square), custom_call_target="tpu_custom_call" | custom-call | tf_op jit(solution)/shard_map/gram/pallas_call | solution.py:286
  106.0 4.9 %all-to-all-start.1 = ((f32[16,1,256]{2,1,0:T(1,128)}), f32[16,1,256]{2,1,0:T(1,128)S(1)}, u32[]{:S(2)}, u32[]{:S(2)}) async-start(f32[16,1,256]{2,1,0:T(1,128)} %copy.8), calls=%async_computation.1 | async-start | bytes 32768 | tf_op jit(solution)/shard_map/all_to_all | solution.py:328
  111.0 6.4 %all-to-all-done.1 = f32[16,1,256]{2,1,0:T(1,128)S(1)} async-done(((f32[16,1,256]{2,1,0:T(1,128)}), f32[16,1,256]{2,1,0:T(1,128)S(1)}, u32[]{:S(2)}, u32[]{:S(2)}) %all-to-all-start.1) | async-done | bytes 16416 | tf_op jit(solution)/shard_map/all_to_all | solution.py:328
  120.0 1.9 %collective-permute-done.17 = f32[1,256]{1,0:T(1,128)S(1)} collective-permute-done((f32[1,256]{1,0:T(1,128)S(1)}, f32[1,256]{1,0:T(1,128)S(1)}, u32[]{:S(2)}, u32[]{:S(2)}) %collective-permute-start.17) | collective-permute-done | bytes 1056 | tf_op jit(solution)/shard_map/ppermute | solution.py:29
  121.9 1.9 %collective-permute-start.18 = (f32[1,256]{1,0:T(1,128)S(1)}, f32[1,256]{1,0:T(1,128)S(1)}, u32[]{:S(2)}, u32[]{:S(2)}) collective-permute-start(f32[1,256]{1,0:T(1,128)S(1)} %add.76), channel_id=1, source_target_pairs={{0,64},{1,65},{2,66},{3,67},{4,68},{5,69},{6,70},{7,71},{8,72},{9,... | collective-permute-start | bytes 3080 | tf_op jit(solution)/shard_map/ppermute | solution.py:29
  (45 shorter events, 10.4 us)
Async XLA Ops:
  0.6 12.6 %copy-start.4 = (f32[4,128,128]{2,1,0:T(8,128)S(1)}, f32[4,128,128]{2,1,0:T(8,128)}, u32[]{:S(2)}) copy-start(f32[4,128,128]{2,1,0:T(8,128)} %param.6) | copy-start | bytes 786436
  2.0 11.2 %collective-permute-start = (f32[4,128,128]{2,1,0:T(8,128)S(1)}, f32[4,128,128]{2,1,0:T(8,128)S(1)}, u32[]{:S(2)}, u32[]{:S(2)}) collective-permute-start(f32[4,128,128]{2,1,0:T(8,128)S(1)} %get-tuple-element.40), channel_id=1, source_target_pairs={{0,0},{1,1},{2,2},{3,3},{4,32},{5,33},{6,34},{7,35},{8,8},{9,9},{1... | collective-permute-start | bytes 786440 | tf_op jit(solution)/shard_map/ppermute | solution.py:29
  6.5 10.6 %collective-permute-start.1 = (f32[4,128,128]{2,1,0:T(8,128)S(1)}, f32[4,128,128]{2,1,0:T(8,128)S(1)}, u32[]{:S(2)}, u32[]{:S(2)}) collective-permute-start(f32[4,128,128]{2,1,0:T(8,128)S(1)} %get-tuple-element.41), channel_id=1, source_target_pairs={{0,1},{1,2},{2,3},{3,0},{4,33},{5,34},{6,35},{7,32},{8,9},{9,10},{... | collective-permute-start | bytes 786440 | tf_op jit(solution)/shard_map/ppermute | solution.py:29
  8.0 11.7 %collective-permute-start.2 = (f32[4,128,128]{2,1,0:T(8,128)S(1)}, f32[4,128,128]{2,1,0:T(8,128)S(1)}, u32[]{:S(2)}, u32[]{:S(2)}) collective-permute-start(f32[4,128,128]{2,1,0:T(8,128)S(1)} %get-tuple-element.43), channel_id=1, source_target_pairs={{0,2},{1,3},{2,0},{3,1},{4,34},{5,35},{6,32},{7,33},{8,10},{9,11},... | collective-permute-start | bytes 786440 | tf_op jit(solution)/shard_map/ppermute | solution.py:29
  12.7 8.4 %collective-permute-start.3 = (f32[4,128,128]{2,1,0:T(8,128)S(1)}, f32[4,128,128]{2,1,0:T(8,128)S(1)}, u32[]{:S(2)}, u32[]{:S(2)}) collective-permute-start(f32[4,128,128]{2,1,0:T(8,128)S(1)} %get-tuple-element.42), channel_id=1, source_target_pairs={{0,3},{1,0},{2,1},{3,2},{4,35},{5,32},{6,33},{7,34},{8,11},{9,8},{... | collective-permute-start | bytes 786440 | tf_op jit(solution)/shard_map/ppermute | solution.py:29
  13.2 33.7 %copy-start.2 = (bf16[256,128]{1,0:T(8,128)(2,1)S(1)}, bf16[256,128]{1,0:T(8,128)(2,1)}, u32[]{:S(2)}) copy-start(bf16[256,128]{1,0:T(8,128)(2,1)} %constant.71.clone.matrix) | copy-start | bytes 196612
  21.2 13.0 %collective-permute-start.4 = (f32[16,128,128]{2,1,0:T(8,128)S(1)}, f32[16,128,128]{2,1,0:T(8,128)S(1)}, u32[]{:S(2)}, u32[]{:S(2)}) collective-permute-start(f32[16,128,128]{2,1,0:T(8,128)S(1)} %pad_maximum_fusion.own), channel_id=1, source_target_pairs={{0,32},{1,33},{2,34},{3,35},{4,36},{5,37},{6,38},{7,39},{8,40},{9,... | collective-permute-start | bytes 3145736 | tf_op jit(solution)/shard_map/ppermute | solution.py:29
  22.7 16.5 %collective-permute-start.9 = (f32[16,128,128]{2,1,0:T(8,128)S(1)}, f32[16,128,128]{2,1,0:T(8,128)S(1)}, u32[]{:S(2)}, u32[]{:S(2)}) collective-permute-start(f32[16,128,128]{2,1,0:T(8,128)S(1)} %pad_maximum_fusion.own), channel_id=1, source_target_pairs={{0,56},{1,57},{2,58},{3,59},{4,60},{5,61},{6,62},{7,63},{8,32},{9,... | collective-permute-start | bytes 3145736 | tf_op jit(solution)/shard_map/ppermute | solution.py:29
  24.0 13.0 %collective-permute-start.6 = (f32[4,128,128]{2,1,0:T(8,128)S(1)}, f32[4,128,128]{2,1,0:T(8,128)S(1)}, u32[]{:S(2)}, u32[]{:S(2)}) collective-permute-start(f32[4,128,128]{2,1,0:T(8,128)S(1)} %multiply_add_fusion), channel_id=1, source_target_pairs={{0,1},{1,2},{2,3},{3,0},{4,97},{5,98},{6,99},{7,96},{8,9},{9,10},{... | collective-permute-start | bytes 786440 | tf_op jit(solution)/shard_map/ppermute | solution.py:29
  29.1 9.5 %collective-permute-start.7 = (f32[4,128,128]{2,1,0:T(8,128)S(1)}, f32[4,128,128]{2,1,0:T(8,128)S(1)}, u32[]{:S(2)}, u32[]{:S(2)}) collective-permute-start(f32[4,128,128]{2,1,0:T(8,128)S(1)} %multiply_add_fusion), channel_id=1, source_target_pairs={{0,2},{1,3},{2,0},{3,1},{4,98},{5,99},{6,96},{7,97},{8,10},{9,11},... | collective-permute-start | bytes 786440 | tf_op jit(solution)/shard_map/ppermute | solution.py:29
  29.7 9.6 %collective-permute-start.8 = (f32[4,128,128]{2,1,0:T(8,128)S(1)}, f32[4,128,128]{2,1,0:T(8,128)S(1)}, u32[]{:S(2)}, u32[]{:S(2)}) collective-permute-start(f32[4,128,128]{2,1,0:T(8,128)S(1)} %multiply_add_fusion), channel_id=1, source_target_pairs={{0,3},{1,0},{2,1},{3,2},{4,99},{5,96},{6,97},{7,98},{8,11},{9,8},{... | collective-permute-start | bytes 786440 | tf_op jit(solution)/shard_map/ppermute | solution.py:29
  34.1 1.0 copy-start
  35.1 8.9 %collective-permute-start.5 = (f32[4,128,128]{2,1,0:T(8,128)S(1)}, f32[4,128,128]{2,1,0:T(8,128)S(1)}, u32[]{:S(2)}, u32[]{:S(2)}) collective-permute-start(f32[4,128,128]{2,1,0:T(8,128)S(1)} %multiply_add_fusion), channel_id=1, source_target_pairs={{0,0},{1,1},{2,2},{3,3},{4,96},{5,97},{6,98},{7,99},{8,8},{9,9},{1... | collective-permute-start | bytes 786440 | tf_op jit(solution)/shard_map/ppermute | solution.py:29
  44.1 2.9 %collective-permute-start.11 = (f32[16,128,128]{2,1,0:T(8,128)S(1)}, f32[16,128,128]{2,1,0:T(8,128)}, u32[]{:S(2)}, u32[]{:S(2)}) collective-permute-start(f32[16,128,128]{2,1,0:T(8,128)S(1)} %constant_dynamic-update-slice_fusion.own_pot), channel_id=1, source_target_pairs={{0,32},{1,33},{2,34},{3,35},{4,36},{5,37},{6,38},{7,39},{8,40},{9,... | collective-permute-start | bytes 3145736 | tf_op jit(solution)/shard_map/ppermute | solution.py:29
  44.2 14.7 %collective-permute-start.10 = (f32[16,128,128]{2,1,0:T(8,128)S(1)}, f32[16,128,128]{2,1,0:T(8,128)}, u32[]{:S(2)}, u32[]{:S(2)}) collective-permute-start(f32[16,128,128]{2,1,0:T(8,128)S(1)} %constant_dynamic-update-slice_fusion.own_pot), channel_id=1, source_target_pairs={{0,56},{1,57},{2,58},{3,59},{4,60},{5,61},{6,62},{7,63},{8,32},{9,... | collective-permute-start | bytes 3145736 | tf_op jit(solution)/shard_map/ppermute | solution.py:29
  47.0 1.2 copy-start.1
  69.7 20.2 %copy-start.3 = (f32[16,16]{1,0:T(8,128)S(1)}, f32[16,16]{1,0:T(8,128)}, u32[]{:S(2)}) copy-start(f32[16,16]{1,0:T(8,128)} %rotation.3) | copy-start | bytes 3076
  69.8 20.2 %all-to-all-start = ((f32[16,128,128]{2,1,0:T(8,128)}), f32[16,128,128]{2,1,0:T(8,128)S(1)}, u32[]{:S(2)}, u32[]{:S(2)}) async-start(f32[16,128,128]{2,1,0:T(8,128)} %outer.1), calls=%async_computation | async-start | bytes 2097152 | tf_op jit(solution)/shard_map/all_to_all | solution.py:325
  91.5 25.9 %collective-permute-start.12 = (f32[4,128,128]{2,1,0:T(8,128)S(1)}, f32[4,128,128]{2,1,0:T(8,128)S(1)}, u32[]{:S(2)}, u32[]{:S(2)}) collective-permute-start(f32[4,128,128]{2,1,0:T(8,128)S(1)} %get-tuple-element.26), channel_id=1, source_target_pairs={{0,0},{1,1},{2,2},{3,3},{4,32},{5,33},{6,34},{7,35},{8,8},{9,9},{1... | collective-permute-start | bytes 786440 | tf_op jit(solution)/shard_map/ppermute | solution.py:29
  95.9 24.0 %collective-permute-start.13 = (f32[4,128,128]{2,1,0:T(8,128)S(1)}, f32[4,128,128]{2,1,0:T(8,128)S(1)}, u32[]{:S(2)}, u32[]{:S(2)}) collective-permute-start(f32[4,128,128]{2,1,0:T(8,128)S(1)} %get-tuple-element.28), channel_id=1, source_target_pairs={{0,32},{1,33},{2,34},{3,35},{4,0},{5,1},{6,2},{7,3},{8,40},{9,41},... | collective-permute-start | bytes 786440 | tf_op jit(solution)/shard_map/ppermute | solution.py:29
  97.5 22.3 %collective-permute-start.14 = (f32[4,128,128]{2,1,0:T(8,128)S(1)}, f32[4,128,128]{2,1,0:T(8,128)S(1)}, u32[]{:S(2)}, u32[]{:S(2)}) collective-permute-start(f32[4,128,128]{2,1,0:T(8,128)S(1)} %get-tuple-element.29), channel_id=1, source_target_pairs={{0,64},{1,65},{2,66},{3,67},{4,96},{5,97},{6,98},{7,99},{8,72},{9,... | collective-permute-start | bytes 786440 | tf_op jit(solution)/shard_map/ppermute | solution.py:29
  98.8 21.0 %collective-permute-start.15 = (f32[4,128,128]{2,1,0:T(8,128)S(1)}, f32[4,128,128]{2,1,0:T(8,128)S(1)}, u32[]{:S(2)}, u32[]{:S(2)}) collective-permute-start(f32[4,128,128]{2,1,0:T(8,128)S(1)} %get-tuple-element.30), channel_id=1, source_target_pairs={{0,96},{1,97},{2,98},{3,99},{4,64},{5,65},{6,66},{7,67},{8,104},{9... | collective-permute-start | bytes 786440 | tf_op jit(solution)/shard_map/ppermute | solution.py:29
  106.0 11.4 %all-to-all-start.1 = ((f32[16,1,256]{2,1,0:T(1,128)}), f32[16,1,256]{2,1,0:T(1,128)S(1)}, u32[]{:S(2)}, u32[]{:S(2)}) async-start(f32[16,1,256]{2,1,0:T(1,128)} %copy.8), calls=%async_computation.1 | async-start | bytes 32768 | tf_op jit(solution)/shard_map/all_to_all | solution.py:328
  117.4 2.0 %collective-permute-start.16 = (f32[1,256]{1,0:T(1,128)S(1)}, f32[1,256]{1,0:T(1,128)S(1)}, u32[]{:S(2)}, u32[]{:S(2)}) collective-permute-start(f32[1,256]{1,0:T(1,128)S(1)} %bitcast.24), channel_id=1, source_target_pairs={{0,32},{1,33},{2,34},{3,35},{4,36},{5,37},{6,38},{7,39},{8,40},{9,... | collective-permute-start | bytes 3080 | tf_op jit(solution)/shard_map/ppermute | solution.py:29
  119.5 2.4 %collective-permute-start.17 = (f32[1,256]{1,0:T(1,128)S(1)}, f32[1,256]{1,0:T(1,128)S(1)}, u32[]{:S(2)}, u32[]{:S(2)}) collective-permute-start(f32[1,256]{1,0:T(1,128)S(1)} %add.75), channel_id=1, source_target_pairs={{0,4},{1,5},{2,6},{3,7},{4,0},{5,1},{6,2},{7,3},{8,12},{9,13},{10,... | collective-permute-start | bytes 3080 | tf_op jit(solution)/shard_map/ppermute | solution.py:29
  121.9 3.9 %collective-permute-start.18 = (f32[1,256]{1,0:T(1,128)S(1)}, f32[1,256]{1,0:T(1,128)S(1)}, u32[]{:S(2)}, u32[]{:S(2)}) collective-permute-start(f32[1,256]{1,0:T(1,128)S(1)} %add.76), channel_id=1, source_target_pairs={{0,64},{1,65},{2,66},{3,67},{4,68},{5,69},{6,70},{7,71},{8,72},{9,... | collective-permute-start | bytes 3080 | tf_op jit(solution)/shard_map/ppermute | solution.py:29

commit v5 on v2

--- a/solution.py
+++ b/solution.py
@@ -37,6 +37,10 @@
     return {**c, "core": 1 - c["core"], "y": c["y"] + (1 if c["core"] == 1 else -1)}
 
 
+def pot_to_orbital(shift):
+    return lambda c: {**to_orbital(shift)(c), "x_hi": c["x_hi"] ^ c["core"] ^ c["x_lo"]}
+
+
 def to_sibling(c):
     return {**c, "core": 1 - c["core"]}
 
@@ -81,7 +85,7 @@
     ref[p, N + PAD : ROWS, :] = ref[p, PAD : 2 * PAD, :]
 
 
-def four_planes(src, dst, pot, along, matrix, p, first_step):
+def products(src, along, matrix, p):
     for k in range(4):
         v = src[p + k, PAD : PAD + N, :]
         high = v.astype(jnp.bfloat16)
@@ -91,6 +95,9 @@
             matrix[...],
             preferred_element_type=jnp.float32,
         )
+
+
+def four_planes(src, dst, pot, along, p, first_step):
     for t in range(N // 8):
         r = PAD + 8 * t
         column = [src[p + k - 2, r : r + 8, :] for k in range(8)]
@@ -112,8 +119,17 @@
                 dst[p + k, 0:PAD, :] = res
 
 
+def advance(src, dst, pot, along, matrix, first, count, first_step):
+    products(src, along[0], matrix, first)
+    for group in range(count // 4):
+        p = first + 4 * group
+        if 4 * group + 4 < count:
+            products(src, along[(group + 1) % 2], matrix, p + 4)
+        four_planes(src, dst, pot, along[group % 2], p, first_step)
+
+
 def inner_kernel(
-    place, own, sibling, own_pot, sibling_pot, matrix, edges, one, two, pot, along, sems
+    place, own, sibling, own_pot, sibling_pot, matrix, edges, one, two, pot, even, odd, sems
 ):
     core, z = place[0], place[1]
     copies = []
@@ -133,10 +149,9 @@
     for step in range(DEGREE):
         src, dst = (one, two) if step % 2 == 1 else (two, one)
         if step > 0:
-
-            @pl.loop(0, (2 * OWN - 4 * step) // 4)
-            def _(group):
-                four_planes(src, dst, pot, along, matrix, 2 * step + 4 * group, step == 1)
+            advance(
+                src, dst, pot, (even, odd), matrix, 2 * step, 2 * OWN - 4 * step, step == 1
+            )
 
         base = 2 * step + core * (28 - 4 * step)
 
@@ -146,7 +161,7 @@
 
 
 def outer_kernel(
-    place, outer, outer_pot, own_pot, edges, matrix, out, one, two, pot, along, sems
+    place, outer, outer_pot, own_pot, edges, matrix, out, one, two, pot, even, odd, sems
 ):
     core, z = place[0], place[1]
     copies = []
@@ -172,10 +187,7 @@
             src[base + k] = edges[4 * before + k]
 
         first = 2 * step + core * (18 - 4 * step)
-
-        @pl.loop(0, OWN // 4)
-        def _(group):
-            four_planes(src, dst, pot, along, matrix, first + 4 * group, step == 1)
+        advance(src, dst, pot, (even, odd), matrix, first, OWN, step == 1)
 
     last = one if DEGREE % 2 == 0 else two
     copies = []
@@ -201,7 +213,8 @@
         + [pl.BlockSpec(memory_space=pltpu.VMEM)],
         out_specs=pl.BlockSpec(memory_space=place_out),
         scratch_shapes=[pltpu.VMEM((planes, ROWS, N), jnp.float32)] * 3
-        + [pltpu.VMEM((4, N, N), jnp.float32), pltpu.SemaphoreType.DMA((16,))],
+        + [pltpu.VMEM((4, N, N), jnp.float32)] * 2
+        + [pltpu.SemaphoreType.DMA((16,))],
         compiler_params=pltpu.CompilerParams(vmem_limit_bytes=40 << 20),
         cost_estimate=pl.CostEstimate(flops=1000, bytes_accessed=0, transcendentals=0),
         name=name,
@@ -272,7 +285,7 @@
                         back = 16 * column + 4 * (place[0] ^ rel) + j
                         sums[pl.ds(back, 1), :] = total
     out[...] = lax.dot_general(
-        jnp.ones((8, N), jnp.float32),
+        jnp.ones((16, N), jnp.float32),
         sums[...],
         (((1,), (1,)), ((), ())),
         precision=lax.Precision.HIGHEST,
@@ -285,7 +298,7 @@
     smem = pl.BlockSpec(memory_space=pltpu.SMEM)
     return pl.pallas_call(
         gram_kernel,
-        out_shape=jax.ShapeDtypeStruct((8, 256), jnp.float32),
+        out_shape=jax.ShapeDtypeStruct((16, 256), jnp.float32),
         in_specs=[smem] + [vmem] * 4,
         out_specs=vmem,
         scratch_shapes=[pltpu.VMEM((256, N), jnp.float32)],
@@ -307,7 +320,7 @@
         for s in range(4)
     ]
     diagonal = FACTOR * potential + DIAG
-    pots = [moved(diagonal, to_orbital(s)) for s in range(4)]
+    pots = [moved(diagonal, pot_to_orbital(s)) for s in range(4)]
     own = jnp.concatenate(orbs, axis=0)
     own_pot = jnp.concatenate(pots, axis=0)
     outer = moved(own, to_outer)
@@ -319,14 +332,17 @@
     planes = lax.all_to_all(mine, ("x_hi", "x_lo", "z"), 0, 0, tiled=True)
     base = jnp.stack([2 * x_hi + x_lo]).astype(jnp.int32)
     far = rotated_parts(2, base, rotation, planes)
+    far, planes = lax.optimization_barrier((far, planes))
     near = rotated_parts(0, base, rotation, planes)
     home = [None] * 4
     home[2], home[3] = moved(far[0], to_home(1, 0)), moved(far[1], to_home(1, 1))
     home[0], home[1] = moved(near[0], to_home(0, 0)), moved(near[1], to_home(0, 1))
-    total = gram_rows(base, [*near, *far])
-    for axis, bit in (("z", 1), ("z", 2), ("y", 1), ("y", 2), ("core", 1), ("x_lo", 1), ("x_hi", 1)):
-        total = total + moved(total, lambda c: {**c, axis: c[axis] ^ bit})
-    total = total[0].reshape(16, 16) / (N * N * N)
+    rows = lax.all_to_all(gram_rows(base, [*near, *far]), ("y", "z"), 0, 0, tiled=True)
+    total = jnp.sum(rows, axis=0, keepdims=True)
+    total, home[0] = lax.optimization_barrier((total, home[0]))
+    for axis in ("core", "x_lo", "x_hi"):
+        total = total + moved(total, lambda c: {**c, axis: 1 - c[axis]})
+    total = total.reshape(16, 16) / (N * N * N)
     correlation = lax.dynamic_slice_in_dim(total, 4 * (2 * x_hi + core), 4, 0)
     band = 2 * x_hi + core
     pieces = []

time: 126 us -> 123 us (0.976)
  waiting for transfers between devices: 43.7 us -> 38.7 us
  starting transfers between devices: 51.8 us -> 56.2 us
  Pallas kernels: 24.2 us -> 21.6 us
    ppermute x23 -> x19, waiting for transfers between devices: 28.5 us -> 17.1 us  [moved(): return lax.ppermute(array, AXES, pairs)]
    all_to_all x0 -> x1, starting transfers between devices: none -> 8.26 us  [local(): lax.all_to_all(gram_rows(base, [*near, *far]), ('y', 'z'), 0, 0, tiled=True)]
    ppermute x23 -> x19, starting transfers between devices: 45.1 us -> 37.9 us  [moved(): return lax.ppermute(array, AXES, pairs)]
    all_to_all x0 -> x1, waiting for transfers between devices: none -> 6.44 us  [local(): lax.all_to_all(gram_rows(base, [*near, *far]), ('y', 'z'), 0, 0, tiled=True)]
    all_to_all x1, starting transfers between devices: 6.71 us -> 10 us  [local(): planes = lax.all_to_all(mine, ('x_hi', 'x_lo', 'z'), 0, 0, tiled=True)]
    pallas_call x2, Pallas kernels: 20.2 us -> 17.6 us  [filter_call(): pl.pallas_call(kernel, out_shape=jax.ShapeDtypeStruct(shape, jnp.float32)...]
  transfers between devices with their start and end apart: 24 -> 21, of which waited for: 13 -> 11; matrix products, arithmetic and copies ran while one was open for 1% -> 2% of each run, Pallas kernels for 7% -> 7%
where the time goes in v5:
time: 123 us; the launch traced here: 122 us
  starting transfers between devices  56.2 us (46%)
  waiting for transfers between devices  38.7 us (31%)
  Pallas kernels  21.6 us (18%)
  local copies, waits for them, and re-layouts  3.85 us (3%)
    ppermute x19, starting transfers between devices, moved(): return lax.ppermute(array, AXES, pairs)  37.9 us
    pallas_call x2, Pallas kernels, filter_call(): pl.pallas_call(kernel, out_shape=jax.ShapeDtypeStruct(shape, jnp.float32)...  17.6 us
    ppermute x19, waiting for transfers between devices, moved(): return lax.ppermute(array, AXES, pairs)  17.1 us
    all_to_all x1, waiting for transfers between devices, local(): planes = lax.all_to_all(mine, ('x_hi', 'x_lo', 'z'), 0, 0, tiled=True)  15.2 us
    all_to_all x1, starting transfers between devices, local(): planes = lax.all_to_all(mine, ('x_hi', 'x_lo', 'z'), 0, 0, tiled=True)  10 us
    all_to_all x1, starting transfers between devices, local(): lax.all_to_all(gram_rows(base, [*near, *far]), ('y', 'z'), 0, 0, tiled=True)  8.26 us
    all_to_all x1, waiting for transfers between devices, local(): lax.all_to_all(gram_rows(base, [*near, *far]), ('y', 'z'), 0, 0, tiled=True)  6.44 us
    pallas_call x2, Pallas kernels, rotated_parts(): pl.pallas_call(functools.partial(rotate_kernel, first), out_shape=[jax.Sh...  3.1 us
  transfers between devices with their start and end apart: 21, of which 11 were waited for; matrix products, arithmetic and copies ran while one was open for 2% of the time, Pallas kernels for 7%

profile of v5, /device:TPU:1, one launch (start us, length us, event | category | flops | bytes accessed | tf_op | source)
XLA Modules:
  0.0 121.7 jit_solution(494368380535267810)
XLA Ops:
  0.7 1.3 %dynamic-slice_bitcast_fusion = (f32[4,128,128]{2,1,0:T(8,128)S(1)}, f32[4,128,128]{2,1,0:T(8,128)S(1)}, f32[4,128,128]{2,1,0:T(8,128)S(1)}, f32[4,128,128]{2,1,0:T(8,128)S(1)}) fusion(f32[4,4,128,128]{3,2,1,0:T(8,128)} %param.5, s32[]{:T(128)S(6)} %select_n.118, s32[]{:T(128)S(6)} %select_n.114, s32[]{:T(128)S(6)} %select_n.112, s32[]{:T(128)S(6)} %select_n.116), kind=kLoop, calls=%fused_computation.6 | loop fusion | bytes 2097168 | tf_op jit(solution)/shard_map/jit(dynamic_index_in_dim)/squeeze | solution.py:318
  2.0 4.5 %collective-permute-start = (f32[4,128,128]{2,1,0:T(8,128)S(1)}, f32[4,128,128]{2,1,0:T(8,128)S(1)}, u32[]{:S(2)}, u32[]{:S(2)}) collective-permute-start(f32[4,128,128]{2,1,0:T(8,128)S(1)} %get-tuple-element.34), channel_id=1, source_target_pairs={{0,0},{1,1},{2,2},{3,3},{4,32},{5,33},{6,34},{7,35},{8,8},{9,9},{1... | collective-permute-start | bytes 786440 | tf_op jit(solution)/shard_map/ppermute | solution.py:29
  6.5 1.4 %collective-permute-start.1 = (f32[4,128,128]{2,1,0:T(8,128)S(1)}, f32[4,128,128]{2,1,0:T(8,128)S(1)}, u32[]{:S(2)}, u32[]{:S(2)}) collective-permute-start(f32[4,128,128]{2,1,0:T(8,128)S(1)} %get-tuple-element.33), channel_id=1, source_target_pairs={{0,1},{1,2},{2,3},{3,0},{4,33},{5,34},{6,35},{7,32},{8,9},{9,10},{... | collective-permute-start | bytes 786440 | tf_op jit(solution)/shard_map/ppermute | solution.py:29
  8.0 4.8 %collective-permute-start.2 = (f32[4,128,128]{2,1,0:T(8,128)S(1)}, f32[4,128,128]{2,1,0:T(8,128)S(1)}, u32[]{:S(2)}, u32[]{:S(2)}) collective-permute-start(f32[4,128,128]{2,1,0:T(8,128)S(1)} %get-tuple-element.35), channel_id=1, source_target_pairs={{0,2},{1,3},{2,0},{3,1},{4,34},{5,35},{6,32},{7,33},{8,10},{9,11},... | collective-permute-start | bytes 786440 | tf_op jit(solution)/shard_map/ppermute | solution.py:29
  12.7 3.4 %collective-permute-start.6 = (f32[4,128,128]{2,1,0:T(8,128)S(1)}, f32[4,128,128]{2,1,0:T(8,128)S(1)}, u32[]{:S(2)}, u32[]{:S(2)}) collective-permute-start(f32[4,128,128]{2,1,0:T(8,128)S(1)} %multiply_add_fusion), channel_id=1, source_target_pairs={{0,0},{1,1},{2,2},{3,3},{4,96},{5,97},{6,98},{7,99},{8,8},{9,9},{1... | collective-permute-start | bytes 786440 | tf_op jit(solution)/shard_map/ppermute | solution.py:29
  16.3 3.0 %collective-permute-start.3 = (f32[4,128,128]{2,1,0:T(8,128)S(1)}, f32[4,128,128]{2,1,0:T(8,128)S(1)}, u32[]{:S(2)}, u32[]{:S(2)}) collective-permute-start(f32[4,128,128]{2,1,0:T(8,128)S(1)} %get-tuple-element.32), channel_id=1, source_target_pairs={{0,3},{1,0},{2,1},{3,2},{4,35},{5,32},{6,33},{7,34},{8,11},{9,8},{... | collective-permute-start | bytes 786440 | tf_op jit(solution)/shard_map/ppermute | solution.py:29
  19.3 1.4 %collective-permute-start.8 = (f32[4,128,128]{2,1,0:T(8,128)S(1)}, f32[4,128,128]{2,1,0:T(8,128)S(1)}, u32[]{:S(2)}, u32[]{:S(2)}) collective-permute-start(f32[4,128,128]{2,1,0:T(8,128)S(1)} %multiply_add_fusion), channel_id=1, source_target_pairs={{0,2},{1,3},{2,0},{3,1},{4,98},{5,99},{6,96},{7,97},{8,10},{9,11},... | collective-permute-start | bytes 786440 | tf_op jit(solution)/shard_map/ppermute | solution.py:29
  20.7 2.7 %collective-permute-start.9 = (f32[4,128,128]{2,1,0:T(8,128)S(1)}, f32[4,128,128]{2,1,0:T(8,128)S(1)}, u32[]{:S(2)}, u32[]{:S(2)}) collective-permute-start(f32[4,128,128]{2,1,0:T(8,128)S(1)} %multiply_add_fusion), channel_id=1, source_target_pairs={{0,3},{1,0},{2,1},{3,2},{4,99},{5,96},{6,97},{7,98},{8,11},{9,8},{... | collective-permute-start | bytes 786440 | tf_op jit(solution)/shard_map/ppermute | solution.py:29
  23.6 1.7 %collective-permute-start.5 = (f32[16,128,128]{2,1,0:T(8,128)S(1)}, f32[16,128,128]{2,1,0:T(8,128)}, u32[]{:S(2)}, u32[]{:S(2)}) collective-permute-start(f32[16,128,128]{2,1,0:T(8,128)S(1)} %constant_dynamic-update-slice_fusion.own), channel_id=1, source_target_pairs={{0,56},{1,57},{2,58},{3,59},{4,60},{5,61},{6,62},{7,63},{8,32},{9,... | collective-permute-start | bytes 3145736 | tf_op jit(solution)/shard_map/ppermute | solution.py:29
  25.5 3.5 %collective-permute-done.8 = f32[4,128,128]{2,1,0:T(8,128)S(1)} collective-permute-done((f32[4,128,128]{2,1,0:T(8,128)S(1)}, f32[4,128,128]{2,1,0:T(8,128)S(1)}, u32[]{:S(2)}, u32[]{:S(2)}) %collective-permute-start.8) | collective-permute-done | bytes 262176 | tf_op jit(solution)/shard_map/ppermute | solution.py:29
  29.0 3.7 %collective-permute-done.9 = f32[4,128,128]{2,1,0:T(8,128)S(1)} collective-permute-done((f32[4,128,128]{2,1,0:T(8,128)S(1)}, f32[4,128,128]{2,1,0:T(8,128)S(1)}, u32[]{:S(2)}, u32[]{:S(2)}) %collective-permute-start.9) | collective-permute-done | bytes 262176 | tf_op jit(solution)/shard_map/ppermute | solution.py:29
  32.7 3.7 %collective-permute-start.11 = (f32[16,128,128]{2,1,0:T(8,128)S(1)}, f32[16,128,128]{2,1,0:T(8,128)}, u32[]{:S(2)}, u32[]{:S(2)}) collective-permute-start(f32[16,128,128]{2,1,0:T(8,128)S(1)} %constant_dynamic-update-slice_fusion.4.own_pot), channel_id=1, source_target_pairs={{0,32},{1,33},{2,34},{3,35},{4,36},{5,37},{6,38},{7,39},{8,40},{9,... | collective-permute-start | bytes 3145736 | tf_op jit(solution)/shard_map/ppermute | solution.py:29
  36.4 1.3 %collective-permute-start.10 = (f32[16,128,128]{2,1,0:T(8,128)S(1)}, f32[16,128,128]{2,1,0:T(8,128)}, u32[]{:S(2)}, u32[]{:S(2)}) collective-permute-start(f32[16,128,128]{2,1,0:T(8,128)S(1)} %constant_dynamic-update-slice_fusion.4.own_pot), channel_id=1, source_target_pairs={{0,56},{1,57},{2,58},{3,59},{4,60},{5,61},{6,62},{7,63},{8,32},{9,... | collective-permute-start | bytes 3145736 | tf_op jit(solution)/shard_map/ppermute | solution.py:29
  38.8 7.9 %inner.1.edges = f32[32,144,128]{2,1,0:T(8,128)S(1)} custom-call(s32[2]{0:T(128)S(1)} %pad_add_fusion.place, f32[16,128,128]{2,1,0:T(8,128)S(1)} %constant_dynamic-update-slice_fusion.own, f32[16,128,128]{2,1,0:T(8,128)S(1)} %collective-permute-done.4.sibling, f32[16,128,128]{2,1,0:T(8,128)S(1)} %constant_dynamic-update-slice_fusion.4.own_pot, ...), custom_call_target="tpu_custom_call" | custom-call | flops 1000 | tf_op jit(solution)/shard_map/inner/pallas_call | solution.py:208
  46.8 4.3 %collective-permute-done.10.outer_pot = f32[16,128,128]{2,1,0:T(8,128)} collective-permute-done((f32[16,128,128]{2,1,0:T(8,128)S(1)}, f32[16,128,128]{2,1,0:T(8,128)}, u32[]{:S(2)}, u32[]{:S(2)}) %collective-permute-start.10) | collective-permute-done | bytes 1048608 | tf_op jit(solution)/shard_map/ppermute | solution.py:29
  51.1 9.6 %outer.1 = f32[16,128,128]{2,1,0:T(8,128)} custom-call(s32[2]{0:T(128)S(1)} %pad_add_fusion.place, f32[16,128,128]{2,1,0:T(8,128)} %collective-permute-done.5.outer, f32[16,128,128]{2,1,0:T(8,128)} %collective-permute-done.10.outer_pot, f32[16,128,128]{2,1,0:T(8,128)S(1)} %constant_dynamic-update-slice_fusion.4.own_pot, f32[32,144,128]{2,1,0:T(8,128)S(1)} %inner.1.edges, ...), custom_call_target="tpu_custom_call" | custom-call | flops 1000 | tf_op jit(solution)/shard_map/outer/pallas_call | solution.py:208
  60.7 10.0 %all-to-all-start = ((f32[16,128,128]{2,1,0:T(8,128)}), f32[16,128,128]{2,1,0:T(8,128)S(1)}, u32[]{:S(2)}, u32[]{:S(2)}) async-start(f32[16,128,128]{2,1,0:T(8,128)} %outer.1), calls=%async_computation | async-start | bytes 2097152 | tf_op jit(solution)/shard_map/all_to_all | solution.py:332
  70.7 15.2 %all-to-all-done.x = f32[16,128,128]{2,1,0:T(8,128)S(1)} async-done(((f32[16,128,128]{2,1,0:T(8,128)}), f32[16,128,128]{2,1,0:T(8,128)S(1)}, u32[]{:S(2)}, u32[]{:S(2)}) %all-to-all-start) | async-done | bytes 1048608 | tf_op jit(solution)/shard_map/all_to_all | solution.py:332
  85.9 1.5 %rotate.2 = (f32[4,128,128]{2,1,0:T(8,128)S(1)}, f32[4,128,128]{2,1,0:T(8,128)S(1)}) custom-call(s32[1]{0:T(128)} %bitcast.place, f32[16,16]{1,0:T(8,128)S(1)} %copy-done.1, f32[16,128,128]{2,1,0:T(8,128)S(1)} %all-to-all-done.x), custom_call_target="tpu_custom_call" | custom-call | tf_op jit(solution)/shard_map/rotate/pallas_call | solution.py:256
  87.5 1.6 %rotate.3 = (f32[4,128,128]{2,1,0:T(8,128)S(1)}, f32[4,128,128]{2,1,0:T(8,128)S(1)}) custom-call(s32[1]{0:T(128)} %bitcast.place, f32[16,16]{1,0:T(8,128)S(1)} %copy-done.1, f32[16,128,128]{2,1,0:T(8,128)S(1)} %all-to-all-done.x), custom_call_target="tpu_custom_call" | custom-call | tf_op jit(solution)/shard_map/rotate/pallas_call | solution.py:256
  89.1 4.5 %collective-permute-start.12 = (f32[4,128,128]{2,1,0:T(8,128)S(1)}, f32[4,128,128]{2,1,0:T(8,128)S(1)}, u32[]{:S(2)}, u32[]{:S(2)}) collective-permute-start(f32[4,128,128]{2,1,0:T(8,128)S(1)} %get-tuple-element.18.o0), channel_id=1, source_target_pairs={{0,0},{1,1},{2,2},{3,3},{4,32},{5,33},{6,34},{7,35},{8,8},{9,9},{1... | collective-permute-start | bytes 786440 | tf_op jit(solution)/shard_map/ppermute | solution.py:29
  93.7 1.2 collective-permute-start.14
  94.9 1.3 %collective-permute-start.15 = (f32[4,128,128]{2,1,0:T(8,128)S(1)}, f32[4,128,128]{2,1,0:T(8,128)S(1)}, u32[]{:S(2)}, u32[]{:S(2)}) collective-permute-start(f32[4,128,128]{2,1,0:T(8,128)S(1)} %get-tuple-element.21.o3), channel_id=1, source_target_pairs={{0,96},{1,97},{2,98},{3,99},{4,64},{5,65},{6,66},{7,67},{8,104},{9... | collective-permute-start | bytes 786440 | tf_op jit(solution)/shard_map/ppermute | solution.py:29
  96.2 1.0 gram.1
  97.8 8.3 %all-to-all-start.1 = ((f32[16,1,256]{2,1,0:T(1,128)}), f32[16,1,256]{2,1,0:T(1,128)S(1)}, u32[]{:S(2)}, u32[]{:S(2)}) async-start(f32[16,1,256]{2,1,0:T(1,128)} %copy.8), calls=%async_computation.1 | async-start | bytes 32768 | tf_op jit(solution)/shard_map/all_to_all | solution.py:340
  106.1 6.4 %all-to-all-done.1 = f32[16,1,256]{2,1,0:T(1,128)S(1)} async-done(((f32[16,1,256]{2,1,0:T(1,128)}), f32[16,1,256]{2,1,0:T(1,128)S(1)}, u32[]{:S(2)}, u32[]{:S(2)}) %all-to-all-start.1) | async-done | bytes 16416 | tf_op jit(solution)/shard_map/all_to_all | solution.py:340
  112.6 1.3 %collective-permute-start.16 = (f32[1,256]{1,0:T(1,128)S(1)}, f32[1,256]{1,0:T(1,128)S(1)}, u32[]{:S(2)}, u32[]{:S(2)}) collective-permute-start(f32[1,256]{1,0:T(1,128)S(1)} %bitcast.22), channel_id=1, source_target_pairs={{0,32},{1,33},{2,34},{3,35},{4,36},{5,37},{6,38},{7,39},{8,40},{9,... | collective-permute-start | bytes 3080 | tf_op jit(solution)/shard_map/ppermute | solution.py:29
  113.8 0.8 collective-permute-done.16
  114.8 2.2 %collective-permute-done.17 = f32[1,256]{1,0:T(1,128)S(1)} collective-permute-done((f32[1,256]{1,0:T(1,128)S(1)}, f32[1,256]{1,0:T(1,128)S(1)}, u32[]{:S(2)}, u32[]{:S(2)}) %collective-permute-start.17) | collective-permute-done | bytes 1056 | tf_op jit(solution)/shard_map/ppermute | solution.py:29
  117.1 1.5 %collective-permute-start.18 = (f32[1,256]{1,0:T(1,128)S(1)}, f32[1,256]{1,0:T(1,128)S(1)}, u32[]{:S(2)}, u32[]{:S(2)}) collective-permute-start(f32[1,256]{1,0:T(1,128)S(1)} %add.76), channel_id=1, source_target_pairs={{0,64},{1,65},{2,66},{3,67},{4,68},{5,69},{6,70},{7,71},{8,72},{9,... | collective-permute-start | bytes 3080 | tf_op jit(solution)/shard_map/ppermute | solution.py:29
  118.7 1.1 copy.9
  119.8 1.3 %collective-permute-done.18 = f32[1,256]{1,0:T(1,128)S(1)} collective-permute-done((f32[1,256]{1,0:T(1,128)S(1)}, f32[1,256]{1,0:T(1,128)S(1)}, u32[]{:S(2)}, u32[]{:S(2)}) %collective-permute-start.18) | collective-permute-done | bytes 1056 | tf_op jit(solution)/shard_map/ppermute | solution.py:29
  (42 shorter events, 3.4 us)
Async XLA Ops:
  0.6 12.1 %copy-start.2 = (f32[4,128,128]{2,1,0:T(8,128)S(1)}, f32[4,128,128]{2,1,0:T(8,128)}, u32[]{:S(2)}) copy-start(f32[4,128,128]{2,1,0:T(8,128)} %param.6) | copy-start | bytes 786436
  2.0 14.3 %collective-permute-start = (f32[4,128,128]{2,1,0:T(8,128)S(1)}, f32[4,128,128]{2,1,0:T(8,128)S(1)}, u32[]{:S(2)}, u32[]{:S(2)}) collective-permute-start(f32[4,128,128]{2,1,0:T(8,128)S(1)} %get-tuple-element.34), channel_id=1, source_target_pairs={{0,0},{1,1},{2,2},{3,3},{4,32},{5,33},{6,34},{7,35},{8,8},{9,9},{1... | collective-permute-start | bytes 786440 | tf_op jit(solution)/shard_map/ppermute | solution.py:29
  6.5 12.8 %collective-permute-start.1 = (f32[4,128,128]{2,1,0:T(8,128)S(1)}, f32[4,128,128]{2,1,0:T(8,128)S(1)}, u32[]{:S(2)}, u32[]{:S(2)}) collective-permute-start(f32[4,128,128]{2,1,0:T(8,128)S(1)} %get-tuple-element.33), channel_id=1, source_target_pairs={{0,1},{1,2},{2,3},{3,0},{4,33},{5,34},{6,35},{7,32},{8,9},{9,10},{... | collective-permute-start | bytes 786440 | tf_op jit(solution)/shard_map/ppermute | solution.py:29
  8.0 30.9 %copy-start = (bf16[256,128]{1,0:T(8,128)(2,1)S(1)}, bf16[256,128]{1,0:T(8,128)(2,1)}, u32[]{:S(2)}) copy-start(bf16[256,128]{1,0:T(8,128)(2,1)} %constant.71.clone.matrix) | copy-start | bytes 196612
  8.0 12.8 %collective-permute-start.2 = (f32[4,128,128]{2,1,0:T(8,128)S(1)}, f32[4,128,128]{2,1,0:T(8,128)S(1)}, u32[]{:S(2)}, u32[]{:S(2)}) collective-permute-start(f32[4,128,128]{2,1,0:T(8,128)S(1)} %get-tuple-element.35), channel_id=1, source_target_pairs={{0,2},{1,3},{2,0},{3,1},{4,34},{5,35},{6,32},{7,33},{8,10},{9,11},... | collective-permute-start | bytes 786440 | tf_op jit(solution)/shard_map/ppermute | solution.py:29
  12.7 10.8 %collective-permute-start.6 = (f32[4,128,128]{2,1,0:T(8,128)S(1)}, f32[4,128,128]{2,1,0:T(8,128)S(1)}, u32[]{:S(2)}, u32[]{:S(2)}) collective-permute-start(f32[4,128,128]{2,1,0:T(8,128)S(1)} %multiply_add_fusion), channel_id=1, source_target_pairs={{0,0},{1,1},{2,2},{3,3},{4,96},{5,97},{6,98},{7,99},{8,8},{9,9},{1... | collective-permute-start | bytes 786440 | tf_op jit(solution)/shard_map/ppermute | solution.py:29
  16.2 9.2 %collective-permute-start.7 = (f32[4,128,128]{2,1,0:T(8,128)S(1)}, f32[4,128,128]{2,1,0:T(8,128)S(1)}, u32[]{:S(2)}, u32[]{:S(2)}) collective-permute-start(f32[4,128,128]{2,1,0:T(8,128)S(1)} %multiply_add_fusion), channel_id=1, source_target_pairs={{0,1},{1,2},{2,3},{3,0},{4,97},{5,98},{6,99},{7,96},{8,9},{9,10},{... | collective-permute-start | bytes 786440 | tf_op jit(solution)/shard_map/ppermute | solution.py:29
  16.3 7.1 %collective-permute-start.3 = (f32[4,128,128]{2,1,0:T(8,128)S(1)}, f32[4,128,128]{2,1,0:T(8,128)S(1)}, u32[]{:S(2)}, u32[]{:S(2)}) collective-permute-start(f32[4,128,128]{2,1,0:T(8,128)S(1)} %get-tuple-element.32), channel_id=1, source_target_pairs={{0,3},{1,0},{2,1},{3,2},{4,35},{5,32},{6,33},{7,34},{8,11},{9,8},{... | collective-permute-start | bytes 786440 | tf_op jit(solution)/shard_map/ppermute | solution.py:29
  19.3 9.7 %collective-permute-start.8 = (f32[4,128,128]{2,1,0:T(8,128)S(1)}, f32[4,128,128]{2,1,0:T(8,128)S(1)}, u32[]{:S(2)}, u32[]{:S(2)}) collective-permute-start(f32[4,128,128]{2,1,0:T(8,128)S(1)} %multiply_add_fusion), channel_id=1, source_target_pairs={{0,2},{1,3},{2,0},{3,1},{4,98},{5,99},{6,96},{7,97},{8,10},{9,11},... | collective-permute-start | bytes 786440 | tf_op jit(solution)/shard_map/ppermute | solution.py:29
  20.7 12.0 %collective-permute-start.9 = (f32[4,128,128]{2,1,0:T(8,128)S(1)}, f32[4,128,128]{2,1,0:T(8,128)S(1)}, u32[]{:S(2)}, u32[]{:S(2)}) collective-permute-start(f32[4,128,128]{2,1,0:T(8,128)S(1)} %multiply_add_fusion), channel_id=1, source_target_pairs={{0,3},{1,0},{2,1},{3,2},{4,99},{5,96},{6,97},{7,98},{8,11},{9,8},{... | collective-permute-start | bytes 786440 | tf_op jit(solution)/shard_map/ppermute | solution.py:29
  23.5 14.3 %collective-permute-start.4 = (f32[16,128,128]{2,1,0:T(8,128)S(1)}, f32[16,128,128]{2,1,0:T(8,128)S(1)}, u32[]{:S(2)}, u32[]{:S(2)}) collective-permute-start(f32[16,128,128]{2,1,0:T(8,128)S(1)} %constant_dynamic-update-slice_fusion.own), channel_id=1, source_target_pairs={{0,32},{1,33},{2,34},{3,35},{4,36},{5,37},{6,38},{7,39},{8,40},{9,... | collective-permute-start | bytes 3145736 | tf_op jit(solution)/shard_map/ppermute | solution.py:29
  23.6 14.7 %collective-permute-start.5 = (f32[16,128,128]{2,1,0:T(8,128)S(1)}, f32[16,128,128]{2,1,0:T(8,128)}, u32[]{:S(2)}, u32[]{:S(2)}) collective-permute-start(f32[16,128,128]{2,1,0:T(8,128)S(1)} %constant_dynamic-update-slice_fusion.own), channel_id=1, source_target_pairs={{0,56},{1,57},{2,58},{3,59},{4,60},{5,61},{6,62},{7,63},{8,32},{9,... | collective-permute-start | bytes 3145736 | tf_op jit(solution)/shard_map/ppermute | solution.py:29
  32.7 6.1 %collective-permute-start.11 = (f32[16,128,128]{2,1,0:T(8,128)S(1)}, f32[16,128,128]{2,1,0:T(8,128)}, u32[]{:S(2)}, u32[]{:S(2)}) collective-permute-start(f32[16,128,128]{2,1,0:T(8,128)S(1)} %constant_dynamic-update-slice_fusion.4.own_pot), channel_id=1, source_target_pairs={{0,32},{1,33},{2,34},{3,35},{4,36},{5,37},{6,38},{7,39},{8,40},{9,... | collective-permute-start | bytes 3145736 | tf_op jit(solution)/shard_map/ppermute | solution.py:29
  36.4 14.6 %collective-permute-start.10 = (f32[16,128,128]{2,1,0:T(8,128)S(1)}, f32[16,128,128]{2,1,0:T(8,128)}, u32[]{:S(2)}, u32[]{:S(2)}) collective-permute-start(f32[16,128,128]{2,1,0:T(8,128)S(1)} %constant_dynamic-update-slice_fusion.4.own_pot), channel_id=1, source_target_pairs={{0,56},{1,57},{2,58},{3,59},{4,60},{5,61},{6,62},{7,63},{8,32},{9,... | collective-permute-start | bytes 3145736 | tf_op jit(solution)/shard_map/ppermute | solution.py:29
  46.8 39.2 %copy-start.1 = (f32[16,16]{1,0:T(8,128)S(1)}, f32[16,16]{1,0:T(8,128)}, u32[]{:S(2)}) copy-start(f32[16,16]{1,0:T(8,128)} %rotation.3) | copy-start | bytes 3076
  60.7 25.3 %all-to-all-start = ((f32[16,128,128]{2,1,0:T(8,128)}), f32[16,128,128]{2,1,0:T(8,128)S(1)}, u32[]{:S(2)}, u32[]{:S(2)}) async-start(f32[16,128,128]{2,1,0:T(8,128)} %outer.1), calls=%async_computation | async-start | bytes 2097152 | tf_op jit(solution)/shard_map/all_to_all | solution.py:332
  89.1 23.5 %collective-permute-start.12 = (f32[4,128,128]{2,1,0:T(8,128)S(1)}, f32[4,128,128]{2,1,0:T(8,128)S(1)}, u32[]{:S(2)}, u32[]{:S(2)}) collective-permute-start(f32[4,128,128]{2,1,0:T(8,128)S(1)} %get-tuple-element.18.o0), channel_id=1, source_target_pairs={{0,0},{1,1},{2,2},{3,3},{4,32},{5,33},{6,34},{7,35},{8,8},{9,9},{1... | collective-permute-start | bytes 786440 | tf_op jit(solution)/shard_map/ppermute | solution.py:29
  93.6 21.1 %collective-permute-start.13 = (f32[4,128,128]{2,1,0:T(8,128)S(1)}, f32[4,128,128]{2,1,0:T(8,128)S(1)}, u32[]{:S(2)}, u32[]{:S(2)}) collective-permute-start(f32[4,128,128]{2,1,0:T(8,128)S(1)} %get-tuple-element.19.o1), channel_id=1, source_target_pairs={{0,32},{1,33},{2,34},{3,35},{4,0},{5,1},{6,2},{7,3},{8,40},{9,41},... | collective-permute-start | bytes 786440 | tf_op jit(solution)/shard_map/ppermute | solution.py:29
  93.7 21.0 %collective-permute-start.14 = (f32[4,128,128]{2,1,0:T(8,128)S(1)}, f32[4,128,128]{2,1,0:T(8,128)S(1)}, u32[]{:S(2)}, u32[]{:S(2)}) collective-permute-start(f32[4,128,128]{2,1,0:T(8,128)S(1)} %get-tuple-element.20.o2), channel_id=1, source_target_pairs={{0,64},{1,65},{2,66},{3,67},{4,96},{5,97},{6,98},{7,99},{8,72},{9,... | collective-permute-start | bytes 786440 | tf_op jit(solution)/shard_map/ppermute | solution.py:29
  94.9 19.8 %collective-permute-start.15 = (f32[4,128,128]{2,1,0:T(8,128)S(1)}, f32[4,128,128]{2,1,0:T(8,128)S(1)}, u32[]{:S(2)}, u32[]{:S(2)}) collective-permute-start(f32[4,128,128]{2,1,0:T(8,128)S(1)} %get-tuple-element.21.o3), channel_id=1, source_target_pairs={{0,96},{1,97},{2,98},{3,99},{4,64},{5,65},{6,66},{7,67},{8,104},{9... | collective-permute-start | bytes 786440 | tf_op jit(solution)/shard_map/ppermute | solution.py:29
  97.8 14.7 %all-to-all-start.1 = ((f32[16,1,256]{2,1,0:T(1,128)}), f32[16,1,256]{2,1,0:T(1,128)S(1)}, u32[]{:S(2)}, u32[]{:S(2)}) async-start(f32[16,1,256]{2,1,0:T(1,128)} %copy.8), calls=%async_computation.1 | async-start | bytes 32768 | tf_op jit(solution)/shard_map/all_to_all | solution.py:340
  112.6 2.1 %collective-permute-start.16 = (f32[1,256]{1,0:T(1,128)S(1)}, f32[1,256]{1,0:T(1,128)S(1)}, u32[]{:S(2)}, u32[]{:S(2)}) collective-permute-start(f32[1,256]{1,0:T(1,128)S(1)} %bitcast.22), channel_id=1, source_target_pairs={{0,32},{1,33},{2,34},{3,35},{4,36},{5,37},{6,38},{7,39},{8,40},{9,... | collective-permute-start | bytes 3080 | tf_op jit(solution)/shard_map/ppermute | solution.py:29
  114.7 2.4 %collective-permute-start.17 = (f32[1,256]{1,0:T(1,128)S(1)}, f32[1,256]{1,0:T(1,128)S(1)}, u32[]{:S(2)}, u32[]{:S(2)}) collective-permute-start(f32[1,256]{1,0:T(1,128)S(1)} %add.75), channel_id=1, source_target_pairs={{0,4},{1,5},{2,6},{3,7},{4,0},{5,1},{6,2},{7,3},{8,12},{9,13},{10,... | collective-permute-start | bytes 3080 | tf_op jit(solution)/shard_map/ppermute | solution.py:29
  117.1 3.9 %collective-permute-start.18 = (f32[1,256]{1,0:T(1,128)S(1)}, f32[1,256]{1,0:T(1,128)S(1)}, u32[]{:S(2)}, u32[]{:S(2)}) collective-permute-start(f32[1,256]{1,0:T(1,128)S(1)} %add.76), channel_id=1, source_target_pairs={{0,64},{1,65},{2,66},{3,67},{4,68},{5,69},{6,70},{7,71},{8,72},{9,... | collective-permute-start | bytes 3080 | tf_op jit(solution)/shard_map/ppermute | solution.py:29

commit v6 on v5

--- a/solution.py
+++ b/solution.py
@@ -1,5 +1,3 @@
-import functools
-
 import jax
 import jax.numpy as jnp
 import numpy as np
@@ -215,7 +213,7 @@
         scratch_shapes=[pltpu.VMEM((planes, ROWS, N), jnp.float32)] * 3
         + [pltpu.VMEM((4, N, N), jnp.float32)] * 2
         + [pltpu.SemaphoreType.DMA((16,))],
-        compiler_params=pltpu.CompilerParams(vmem_limit_bytes=40 << 20),
+        compiler_params=pltpu.CompilerParams(vmem_limit_bytes=20 << 20),
         cost_estimate=pl.CostEstimate(flops=1000, bytes_accessed=0, transcendentals=0),
         name=name,
     )(*args, stencil_matrix())
@@ -232,17 +230,15 @@
     )
 
 
-def rotate_kernel(first, place, rotation, x, *outs):
+def rotate_kernel(place, rotation, x, *outs):
     for n, out in enumerate(outs):
-        b = place[0] ^ (first + n)
+        b = place[0] ^ n
 
         @pl.loop(0, 4)
         def _(j, out=out, b=b):
             coeffs = [rotation[i, 4 * b + j] for i in range(16)]
-
-            @pl.loop(0, 2)
-            def _(half):
-                rows = [pl.ds(pl.multiple_of(64 * half + 8 * u, 8), 8) for u in range(8)]
+            for first in range(0, N, 64):
+                rows = [slice(first + 8 * u, first + 8 * u + 8) for u in range(8)]
                 totals = [coeffs[0] * x[0, r, :] for r in rows]
                 for i in range(1, 16):
                     totals = [a + coeffs[i] * x[i, r, :] for a, r in zip(totals, rows)]
@@ -250,15 +246,15 @@
                     out[j, r, :] = a
 
 
-def rotated_parts(first, place, rotation, planes):
+def rotated_parts(place, rotation, planes):
     vmem = pl.BlockSpec(memory_space=pltpu.VMEM)
     smem = pl.BlockSpec(memory_space=pltpu.SMEM)
     return pl.pallas_call(
-        functools.partial(rotate_kernel, first),
-        out_shape=[jax.ShapeDtypeStruct((4, N, N), jnp.float32)] * 2,
+        rotate_kernel,
+        out_shape=[jax.ShapeDtypeStruct((4, N, N), jnp.float32)] * 4,
         in_specs=[smem, smem, vmem],
-        out_specs=[vmem] * 2,
-        compiler_params=pltpu.CompilerParams(vmem_limit_bytes=32 << 20),
+        out_specs=[vmem] * 4,
+        compiler_params=pltpu.CompilerParams(vmem_limit_bytes=16 << 20),
         name="rotate",
     )(place, rotation, planes)
 
@@ -285,7 +281,7 @@
                         back = 16 * column + 4 * (place[0] ^ rel) + j
                         sums[pl.ds(back, 1), :] = total
     out[...] = lax.dot_general(
-        jnp.ones((16, N), jnp.float32),
+        jnp.ones((N, N), jnp.float32),
         sums[...],
         (((1,), (1,)), ((), ())),
         precision=lax.Precision.HIGHEST,
@@ -298,11 +294,11 @@
     smem = pl.BlockSpec(memory_space=pltpu.SMEM)
     return pl.pallas_call(
         gram_kernel,
-        out_shape=jax.ShapeDtypeStruct((16, 256), jnp.float32),
+        out_shape=jax.ShapeDtypeStruct((N, 256), jnp.float32),
         in_specs=[smem] + [vmem] * 4,
         out_specs=vmem,
         scratch_shapes=[pltpu.VMEM((256, N), jnp.float32)],
-        compiler_params=pltpu.CompilerParams(vmem_limit_bytes=32 << 20),
+        compiler_params=pltpu.CompilerParams(vmem_limit_bytes=16 << 20),
         name="gram",
     )(place, *parts)
 
@@ -331,17 +327,11 @@
     mine = filtered(place, own, sibling, outer, own_pot, sibling_pot, outer_pot)
     planes = lax.all_to_all(mine, ("x_hi", "x_lo", "z"), 0, 0, tiled=True)
     base = jnp.stack([2 * x_hi + x_lo]).astype(jnp.int32)
-    far = rotated_parts(2, base, rotation, planes)
-    far, planes = lax.optimization_barrier((far, planes))
-    near = rotated_parts(0, base, rotation, planes)
-    home = [None] * 4
-    home[2], home[3] = moved(far[0], to_home(1, 0)), moved(far[1], to_home(1, 1))
-    home[0], home[1] = moved(near[0], to_home(0, 0)), moved(near[1], to_home(0, 1))
-    rows = lax.all_to_all(gram_rows(base, [*near, *far]), ("y", "z"), 0, 0, tiled=True)
-    total = jnp.sum(rows, axis=0, keepdims=True)
-    total, home[0] = lax.optimization_barrier((total, home[0]))
-    for axis in ("core", "x_lo", "x_hi"):
-        total = total + moved(total, lambda c: {**c, axis: 1 - c[axis]})
+    parts = rotated_parts(base, rotation, planes)
+    home = [moved(parts[2 * a + e], to_home(a, e)) for a in range(2) for e in range(2)]
+    parts, home[0] = lax.optimization_barrier((parts, home[0]))
+    rows = lax.all_to_all(gram_rows(base, parts), AXES, 0, 0, tiled=True)
+    total = jnp.sum(rows, axis=0)
     total = total.reshape(16, 16) / (N * N * N)
     correlation = lax.dynamic_slice_in_dim(total, 4 * (2 * x_hi + core), 4, 0)
     band = 2 * x_hi + core

time: 123 us -> 120 us (0.976); the launches traced: 122 us -> 120 us
  starting transfers between devices: 56.2 us -> 54.5 us
    ppermute x19 -> x16, starting transfers between devices: 37.9 us -> 35.1 us  [moved(): return lax.ppermute(array, AXES, pairs)]
    all_to_all x1, waiting for transfers between devices: 6.44 us -> 8.63 us  [local(): rows = lax.all_to_all(gram_rows(base, parts), AXES, 0, 0, tiled=True)]
    ppermute x19 -> x16, waiting for transfers between devices: 17.1 us -> 15.6 us  [moved(): return lax.ppermute(array, AXES, pairs)]
    pallas_call x3 -> x2, Pallas kernels: 4.07 us -> 3.03 us  [the longest x1 1.97 us: rotated_parts(): pl.pallas_call(rotate_kernel, out_shape=[jax.ShapeDtypeStruct((4, N, N),...]
  transfers between devices with their start and end apart: 21 -> 18, of which waited for: 11 -> 9; matrix products, arithmetic and copies ran while one was open for 2% -> 2% of each run, Pallas kernels for 7% -> 7%
where the time goes in v6:
time: 120 us
  starting transfers between devices  54.5 us (45%)
  waiting for transfers between devices  39.4 us (33%)
  Pallas kernels  20.6 us (17%)
  local copies, waits for them, and re-layouts  3.98 us (3%)
    ppermute x16, starting transfers between devices, moved(): return lax.ppermute(array, AXES, pairs)  35.1 us
    pallas_call x2, Pallas kernels, filter_call(): pl.pallas_call(kernel, out_shape=jax.ShapeDtypeStruct(shape, jnp.float32)...  17.6 us
    ppermute x16, waiting for transfers between devices, moved(): return lax.ppermute(array, AXES, pairs)  15.6 us
    all_to_all x1, waiting for transfers between devices, local(): planes = lax.all_to_all(mine, ('x_hi', 'x_lo', 'z'), 0, 0, tiled=True)  15.2 us
    all_to_all x1, starting transfers between devices, local(): planes = lax.all_to_all(mine, ('x_hi', 'x_lo', 'z'), 0, 0, tiled=True)  10 us
    all_to_all x1, starting transfers between devices, local(): rows = lax.all_to_all(gram_rows(base, parts), AXES, 0, 0, tiled=True)  9.36 us
    all_to_all x1, waiting for transfers between devices, local(): rows = lax.all_to_all(gram_rows(base, parts), AXES, 0, 0, tiled=True)  8.63 us
  transfers between devices with their start and end apart: 18, of which 9 were waited for; matrix products, arithmetic and copies ran while one was open for 2% of the time, Pallas kernels for 7%

profile of v6, /device:TPU:1, one launch (start us, length us, event | category | flops | bytes accessed | tf_op | source)
XLA Modules:
  0.0 120.0 jit_solution(10555196537594245148)
XLA Ops:
  0.7 1.3 %dynamic-slice_bitcast_fusion = (f32[4,128,128]{2,1,0:T(8,128)S(1)}, f32[4,128,128]{2,1,0:T(8,128)S(1)}, f32[4,128,128]{2,1,0:T(8,128)S(1)}, f32[4,128,128]{2,1,0:T(8,128)S(1)}) fusion(f32[4,4,128,128]{3,2,1,0:T(8,128)} %param.5, s32[]{:T(128)S(6)} %select_n.118, s32[]{:T(128)S(6)} %select_n.114, s32[]{:T(128)S(6)} %select_n.112, s32[]{:T(128)S(6)} %select_n.116), kind=kLoop, calls=%fused_computation.6 | loop fusion | bytes 2097168 | tf_op jit(solution)/shard_map/jit(dynamic_index_in_dim)/squeeze | solution.py:314
  2.0 4.5 %collective-permute-start = (f32[4,128,128]{2,1,0:T(8,128)S(1)}, f32[4,128,128]{2,1,0:T(8,128)S(1)}, u32[]{:S(2)}, u32[]{:S(2)}) collective-permute-start(f32[4,128,128]{2,1,0:T(8,128)S(1)} %get-tuple-element.34), channel_id=1, source_target_pairs={{0,0},{1,1},{2,2},{3,3},{4,32},{5,33},{6,34},{7,35},{8,8},{9,9},{1... | collective-permute-start | bytes 786440 | tf_op jit(solution)/shard_map/ppermute | solution.py:27
  6.5 1.4 %collective-permute-start.1 = (f32[4,128,128]{2,1,0:T(8,128)S(1)}, f32[4,128,128]{2,1,0:T(8,128)S(1)}, u32[]{:S(2)}, u32[]{:S(2)}) collective-permute-start(f32[4,128,128]{2,1,0:T(8,128)S(1)} %get-tuple-element.33), channel_id=1, source_target_pairs={{0,1},{1,2},{2,3},{3,0},{4,33},{5,34},{6,35},{7,32},{8,9},{9,10},{... | collective-permute-start | bytes 786440 | tf_op jit(solution)/shard_map/ppermute | solution.py:27
  8.0 4.8 %collective-permute-start.2 = (f32[4,128,128]{2,1,0:T(8,128)S(1)}, f32[4,128,128]{2,1,0:T(8,128)S(1)}, u32[]{:S(2)}, u32[]{:S(2)}) collective-permute-start(f32[4,128,128]{2,1,0:T(8,128)S(1)} %get-tuple-element.35), channel_id=1, source_target_pairs={{0,2},{1,3},{2,0},{3,1},{4,34},{5,35},{6,32},{7,33},{8,10},{9,11},... | collective-permute-start | bytes 786440 | tf_op jit(solution)/shard_map/ppermute | solution.py:27
  12.7 3.4 %collective-permute-start.6 = (f32[4,128,128]{2,1,0:T(8,128)S(1)}, f32[4,128,128]{2,1,0:T(8,128)S(1)}, u32[]{:S(2)}, u32[]{:S(2)}) collective-permute-start(f32[4,128,128]{2,1,0:T(8,128)S(1)} %multiply_add_fusion), channel_id=1, source_target_pairs={{0,0},{1,1},{2,2},{3,3},{4,96},{5,97},{6,98},{7,99},{8,8},{9,9},{1... | collective-permute-start | bytes 786440 | tf_op jit(solution)/shard_map/ppermute | solution.py:27
  16.3 3.0 %collective-permute-start.3 = (f32[4,128,128]{2,1,0:T(8,128)S(1)}, f32[4,128,128]{2,1,0:T(8,128)S(1)}, u32[]{:S(2)}, u32[]{:S(2)}) collective-permute-start(f32[4,128,128]{2,1,0:T(8,128)S(1)} %get-tuple-element.32), channel_id=1, source_target_pairs={{0,3},{1,0},{2,1},{3,2},{4,35},{5,32},{6,33},{7,34},{8,11},{9,8},{... | collective-permute-start | bytes 786440 | tf_op jit(solution)/shard_map/ppermute | solution.py:27
  19.3 1.4 %collective-permute-start.8 = (f32[4,128,128]{2,1,0:T(8,128)S(1)}, f32[4,128,128]{2,1,0:T(8,128)S(1)}, u32[]{:S(2)}, u32[]{:S(2)}) collective-permute-start(f32[4,128,128]{2,1,0:T(8,128)S(1)} %multiply_add_fusion), channel_id=1, source_target_pairs={{0,2},{1,3},{2,0},{3,1},{4,98},{5,99},{6,96},{7,97},{8,10},{9,11},... | collective-permute-start | bytes 786440 | tf_op jit(solution)/shard_map/ppermute | solution.py:27
  20.7 2.7 %collective-permute-start.9 = (f32[4,128,128]{2,1,0:T(8,128)S(1)}, f32[4,128,128]{2,1,0:T(8,128)S(1)}, u32[]{:S(2)}, u32[]{:S(2)}) collective-permute-start(f32[4,128,128]{2,1,0:T(8,128)S(1)} %multiply_add_fusion), channel_id=1, source_target_pairs={{0,3},{1,0},{2,1},{3,2},{4,99},{5,96},{6,97},{7,98},{8,11},{9,8},{... | collective-permute-start | bytes 786440 | tf_op jit(solution)/shard_map/ppermute | solution.py:27
  23.6 1.7 %collective-permute-start.5 = (f32[16,128,128]{2,1,0:T(8,128)S(1)}, f32[16,128,128]{2,1,0:T(8,128)}, u32[]{:S(2)}, u32[]{:S(2)}) collective-permute-start(f32[16,128,128]{2,1,0:T(8,128)S(1)} %constant_dynamic-update-slice_fusion.own), channel_id=1, source_target_pairs={{0,56},{1,57},{2,58},{3,59},{4,60},{5,61},{6,62},{7,63},{8,32},{9,... | collective-permute-start | bytes 3145736 | tf_op jit(solution)/shard_map/ppermute | solution.py:27
  25.3 0.2 collective-permute-done.7
  25.5 3.5 %collective-permute-done.8 = f32[4,128,128]{2,1,0:T(8,128)S(1)} collective-permute-done((f32[4,128,128]{2,1,0:T(8,128)S(1)}, f32[4,128,128]{2,1,0:T(8,128)S(1)}, u32[]{:S(2)}, u32[]{:S(2)}) %collective-permute-start.8) | collective-permute-done | bytes 262176 | tf_op jit(solution)/shard_map/ppermute | solution.py:27
  29.0 3.7 %collective-permute-done.9 = f32[4,128,128]{2,1,0:T(8,128)S(1)} collective-permute-done((f32[4,128,128]{2,1,0:T(8,128)S(1)}, f32[4,128,128]{2,1,0:T(8,128)S(1)}, u32[]{:S(2)}, u32[]{:S(2)}) %collective-permute-start.9) | collective-permute-done | bytes 262176 | tf_op jit(solution)/shard_map/ppermute | solution.py:27
  32.7 3.7 %collective-permute-start.11 = (f32[16,128,128]{2,1,0:T(8,128)S(1)}, f32[16,128,128]{2,1,0:T(8,128)}, u32[]{:S(2)}, u32[]{:S(2)}) collective-permute-start(f32[16,128,128]{2,1,0:T(8,128)S(1)} %constant_dynamic-update-slice_fusion.4.own_pot), channel_id=1, source_target_pairs={{0,32},{1,33},{2,34},{3,35},{4,36},{5,37},{6,38},{7,39},{8,40},{9,... | collective-permute-start | bytes 3145736 | tf_op jit(solution)/shard_map/ppermute | solution.py:27
  36.4 1.3 %collective-permute-start.10 = (f32[16,128,128]{2,1,0:T(8,128)S(1)}, f32[16,128,128]{2,1,0:T(8,128)}, u32[]{:S(2)}, u32[]{:S(2)}) collective-permute-start(f32[16,128,128]{2,1,0:T(8,128)S(1)} %constant_dynamic-update-slice_fusion.4.own_pot), channel_id=1, source_target_pairs={{0,56},{1,57},{2,58},{3,59},{4,60},{5,61},{6,62},{7,63},{8,32},{9,... | collective-permute-start | bytes 3145736 | tf_op jit(solution)/shard_map/ppermute | solution.py:27
  37.8 0.5 collective-permute-done.5.outer
  38.3 0.6 collective-permute-done.11.sibling_pot
  38.8 7.9 %inner.1.edges = f32[32,144,128]{2,1,0:T(8,128)S(1)} custom-call(s32[2]{0:T(128)S(1)} %pad_add_fusion.place, f32[16,128,128]{2,1,0:T(8,128)S(1)} %constant_dynamic-update-slice_fusion.own, f32[16,128,128]{2,1,0:T(8,128)S(1)} %collective-permute-done.4.sibling, f32[16,128,128]{2,1,0:T(8,128)S(1)} %constant_dynamic-update-slice_fusion.4.own_pot, ...), custom_call_target="tpu_custom_call" | custom-call | flops 1000 | tf_op jit(solution)/shard_map/inner/pallas_call | solution.py:206
  46.8 4.3 %collective-permute-done.10.outer_pot = f32[16,128,128]{2,1,0:T(8,128)} collective-permute-done((f32[16,128,128]{2,1,0:T(8,128)S(1)}, f32[16,128,128]{2,1,0:T(8,128)}, u32[]{:S(2)}, u32[]{:S(2)}) %collective-permute-start.10) | collective-permute-done | bytes 1048608 | tf_op jit(solution)/shard_map/ppermute | solution.py:27
  51.1 9.6 %outer.1 = f32[16,128,128]{2,1,0:T(8,128)} custom-call(s32[2]{0:T(128)S(1)} %pad_add_fusion.place, f32[16,128,128]{2,1,0:T(8,128)} %collective-permute-done.5.outer, f32[16,128,128]{2,1,0:T(8,128)} %collective-permute-done.10.outer_pot, f32[16,128,128]{2,1,0:T(8,128)S(1)} %constant_dynamic-update-slice_fusion.4.own_pot, f32[32,144,128]{2,1,0:T(8,128)S(1)} %inner.1.edges, ...), custom_call_target="tpu_custom_call" | custom-call | flops 1000 | tf_op jit(solution)/shard_map/outer/pallas_call | solution.py:206
  60.7 10.0 %all-to-all-start = ((f32[16,128,128]{2,1,0:T(8,128)}), f32[16,128,128]{2,1,0:T(8,128)S(1)}, u32[]{:S(2)}, u32[]{:S(2)}) async-start(f32[16,128,128]{2,1,0:T(8,128)} %outer.1), calls=%async_computation | async-start | bytes 2097152 | tf_op jit(solution)/shard_map/all_to_all | solution.py:328
  70.7 15.2 %all-to-all-done.x = f32[16,128,128]{2,1,0:T(8,128)S(1)} async-done(((f32[16,128,128]{2,1,0:T(8,128)}), f32[16,128,128]{2,1,0:T(8,128)S(1)}, u32[]{:S(2)}, u32[]{:S(2)}) %all-to-all-start) | async-done | bytes 1048608 | tf_op jit(solution)/shard_map/all_to_all | solution.py:328
  85.9 2.0 %rotate.1 = (f32[4,128,128]{2,1,0:T(8,128)S(1)}, f32[4,128,128]{2,1,0:T(8,128)S(1)}, f32[4,128,128]{2,1,0:T(8,128)S(1)}, f32[4,128,128]{2,1,0:T(8,128)S(1)}) custom-call(s32[1]{0:T(128)} %bitcast.place, f32[16,16]{1,0:T(8,128)S(1)} %copy-done.1, f32[16,128,128]{2,1,0:T(8,128)S(1)} %all-to-all-done.x), custom_call_target="tpu_custom_call" | custom-call | tf_op jit(solution)/shard_map/rotate/pallas_call | solution.py:252
  87.9 4.5 %collective-permute-start.12 = (f32[4,128,128]{2,1,0:T(8,128)S(1)}, f32[4,128,128]{2,1,0:T(8,128)S(1)}, u32[]{:S(2)}, u32[]{:S(2)}) collective-permute-start(f32[4,128,128]{2,1,0:T(8,128)S(1)} %get-tuple-element.20.o0), channel_id=1, source_target_pairs={{0,0},{1,1},{2,2},{3,3},{4,32},{5,33},{6,34},{7,35},{8,8},{9,9},{1... | collective-permute-start | bytes 786440 | tf_op jit(solution)/shard_map/ppermute | solution.py:27
  92.6 1.2 collective-permute-start.14
  93.7 1.3 %collective-permute-start.15 = (f32[4,128,128]{2,1,0:T(8,128)S(1)}, f32[4,128,128]{2,1,0:T(8,128)S(1)}, u32[]{:S(2)}, u32[]{:S(2)}) collective-permute-start(f32[4,128,128]{2,1,0:T(8,128)S(1)} %get-tuple-element.23.o3), channel_id=1, source_target_pairs={{0,96},{1,97},{2,98},{3,99},{4,64},{5,65},{6,66},{7,67},{8,104},{9... | collective-permute-start | bytes 786440 | tf_op jit(solution)/shard_map/ppermute | solution.py:27
  95.1 2.9 %collective-permute-done.12 = f32[4,128,128]{2,1,0:T(8,128)S(1)} collective-permute-done((f32[4,128,128]{2,1,0:T(8,128)S(1)}, f32[4,128,128]{2,1,0:T(8,128)S(1)}, u32[]{:S(2)}, u32[]{:S(2)}) %collective-permute-start.12) | collective-permute-done | bytes 262176 | tf_op jit(solution)/shard_map/ppermute | solution.py:27
  97.9 1.1 gram.1
  99.0 0.8 copy.8
  99.8 9.4 %all-to-all-start.1 = ((f32[128,1,256]{2,1,0:T(1,128)}), f32[128,1,256]{2,1,0:T(1,128)S(1)}, u32[]{:S(2)}, u32[]{:S(2)}) async-start(f32[128,1,256]{2,1,0:T(1,128)} %copy.8), calls=%async_computation.1 | async-start | bytes 262144 | tf_op jit(solution)/shard_map/all_to_all | solution.py:333
  109.4 1.1 copy.9
  110.5 8.6 %all-to-all-done.1 = f32[128,1,256]{2,1,0:T(1,128)S(1)} async-done(((f32[128,1,256]{2,1,0:T(1,128)}), f32[128,1,256]{2,1,0:T(1,128)S(1)}, u32[]{:S(2)}, u32[]{:S(2)}) %all-to-all-start.1) | async-done | bytes 131104 | tf_op jit(solution)/shard_map/all_to_all | solution.py:333
  119.4 0.6 constant_dynamic-slice_fusion
  (33 shorter events, 1.0 us)
Async XLA Ops:
  0.6 12.1 %copy-start.2 = (f32[4,128,128]{2,1,0:T(8,128)S(1)}, f32[4,128,128]{2,1,0:T(8,128)}, u32[]{:S(2)}) copy-start(f32[4,128,128]{2,1,0:T(8,128)} %param.6) | copy-start | bytes 786436
  2.0 14.3 %collective-permute-start = (f32[4,128,128]{2,1,0:T(8,128)S(1)}, f32[4,128,128]{2,1,0:T(8,128)S(1)}, u32[]{:S(2)}, u32[]{:S(2)}) collective-permute-start(f32[4,128,128]{2,1,0:T(8,128)S(1)} %get-tuple-element.34), channel_id=1, source_target_pairs={{0,0},{1,1},{2,2},{3,3},{4,32},{5,33},{6,34},{7,35},{8,8},{9,9},{1... | collective-permute-start | bytes 786440 | tf_op jit(solution)/shard_map/ppermute | solution.py:27
  6.5 12.8 %collective-permute-start.1 = (f32[4,128,128]{2,1,0:T(8,128)S(1)}, f32[4,128,128]{2,1,0:T(8,128)S(1)}, u32[]{:S(2)}, u32[]{:S(2)}) collective-permute-start(f32[4,128,128]{2,1,0:T(8,128)S(1)} %get-tuple-element.33), channel_id=1, source_target_pairs={{0,1},{1,2},{2,3},{3,0},{4,33},{5,34},{6,35},{7,32},{8,9},{9,10},{... | collective-permute-start | bytes 786440 | tf_op jit(solution)/shard_map/ppermute | solution.py:27
  8.0 30.9 %copy-start = (bf16[256,128]{1,0:T(8,128)(2,1)S(1)}, bf16[256,128]{1,0:T(8,128)(2,1)}, u32[]{:S(2)}) copy-start(bf16[256,128]{1,0:T(8,128)(2,1)} %constant.71.clone.matrix) | copy-start | bytes 196612
  8.0 12.8 %collective-permute-start.2 = (f32[4,128,128]{2,1,0:T(8,128)S(1)}, f32[4,128,128]{2,1,0:T(8,128)S(1)}, u32[]{:S(2)}, u32[]{:S(2)}) collective-permute-start(f32[4,128,128]{2,1,0:T(8,128)S(1)} %get-tuple-element.35), channel_id=1, source_target_pairs={{0,2},{1,3},{2,0},{3,1},{4,34},{5,35},{6,32},{7,33},{8,10},{9,11},... | collective-permute-start | bytes 786440 | tf_op jit(solution)/shard_map/ppermute | solution.py:27
  12.7 10.8 %collective-permute-start.6 = (f32[4,128,128]{2,1,0:T(8,128)S(1)}, f32[4,128,128]{2,1,0:T(8,128)S(1)}, u32[]{:S(2)}, u32[]{:S(2)}) collective-permute-start(f32[4,128,128]{2,1,0:T(8,128)S(1)} %multiply_add_fusion), channel_id=1, source_target_pairs={{0,0},{1,1},{2,2},{3,3},{4,96},{5,97},{6,98},{7,99},{8,8},{9,9},{1... | collective-permute-start | bytes 786440 | tf_op jit(solution)/shard_map/ppermute | solution.py:27
  16.2 9.2 %collective-permute-start.7 = (f32[4,128,128]{2,1,0:T(8,128)S(1)}, f32[4,128,128]{2,1,0:T(8,128)S(1)}, u32[]{:S(2)}, u32[]{:S(2)}) collective-permute-start(f32[4,128,128]{2,1,0:T(8,128)S(1)} %multiply_add_fusion), channel_id=1, source_target_pairs={{0,1},{1,2},{2,3},{3,0},{4,97},{5,98},{6,99},{7,96},{8,9},{9,10},{... | collective-permute-start | bytes 786440 | tf_op jit(solution)/shard_map/ppermute | solution.py:27
  16.3 7.1 %collective-permute-start.3 = (f32[4,128,128]{2,1,0:T(8,128)S(1)}, f32[4,128,128]{2,1,0:T(8,128)S(1)}, u32[]{:S(2)}, u32[]{:S(2)}) collective-permute-start(f32[4,128,128]{2,1,0:T(8,128)S(1)} %get-tuple-element.32), channel_id=1, source_target_pairs={{0,3},{1,0},{2,1},{3,2},{4,35},{5,32},{6,33},{7,34},{8,11},{9,8},{... | collective-permute-start | bytes 786440 | tf_op jit(solution)/shard_map/ppermute | solution.py:27
  19.3 9.7 %collective-permute-start.8 = (f32[4,128,128]{2,1,0:T(8,128)S(1)}, f32[4,128,128]{2,1,0:T(8,128)S(1)}, u32[]{:S(2)}, u32[]{:S(2)}) collective-permute-start(f32[4,128,128]{2,1,0:T(8,128)S(1)} %multiply_add_fusion), channel_id=1, source_target_pairs={{0,2},{1,3},{2,0},{3,1},{4,98},{5,99},{6,96},{7,97},{8,10},{9,11},... | collective-permute-start | bytes 786440 | tf_op jit(solution)/shard_map/ppermute | solution.py:27
  20.7 12.0 %collective-permute-start.9 = (f32[4,128,128]{2,1,0:T(8,128)S(1)}, f32[4,128,128]{2,1,0:T(8,128)S(1)}, u32[]{:S(2)}, u32[]{:S(2)}) collective-permute-start(f32[4,128,128]{2,1,0:T(8,128)S(1)} %multiply_add_fusion), channel_id=1, source_target_pairs={{0,3},{1,0},{2,1},{3,2},{4,99},{5,96},{6,97},{7,98},{8,11},{9,8},{... | collective-permute-start | bytes 786440 | tf_op jit(solution)/shard_map/ppermute | solution.py:27
  23.5 14.3 %collective-permute-start.4 = (f32[16,128,128]{2,1,0:T(8,128)S(1)}, f32[16,128,128]{2,1,0:T(8,128)S(1)}, u32[]{:S(2)}, u32[]{:S(2)}) collective-permute-start(f32[16,128,128]{2,1,0:T(8,128)S(1)} %constant_dynamic-update-slice_fusion.own), channel_id=1, source_target_pairs={{0,32},{1,33},{2,34},{3,35},{4,36},{5,37},{6,38},{7,39},{8,40},{9,... | collective-permute-start | bytes 3145736 | tf_op jit(solution)/shard_map/ppermute | solution.py:27
  23.6 14.7 %collective-permute-start.5 = (f32[16,128,128]{2,1,0:T(8,128)S(1)}, f32[16,128,128]{2,1,0:T(8,128)}, u32[]{:S(2)}, u32[]{:S(2)}) collective-permute-start(f32[16,128,128]{2,1,0:T(8,128)S(1)} %constant_dynamic-update-slice_fusion.own), channel_id=1, source_target_pairs={{0,56},{1,57},{2,58},{3,59},{4,60},{5,61},{6,62},{7,63},{8,32},{9,... | collective-permute-start | bytes 3145736 | tf_op jit(solution)/shard_map/ppermute | solution.py:27
  32.7 6.1 %collective-permute-start.11 = (f32[16,128,128]{2,1,0:T(8,128)S(1)}, f32[16,128,128]{2,1,0:T(8,128)}, u32[]{:S(2)}, u32[]{:S(2)}) collective-permute-start(f32[16,128,128]{2,1,0:T(8,128)S(1)} %constant_dynamic-update-slice_fusion.4.own_pot), channel_id=1, source_target_pairs={{0,32},{1,33},{2,34},{3,35},{4,36},{5,37},{6,38},{7,39},{8,40},{9,... | collective-permute-start | bytes 3145736 | tf_op jit(solution)/shard_map/ppermute | solution.py:27
  36.4 14.6 %collective-permute-start.10 = (f32[16,128,128]{2,1,0:T(8,128)S(1)}, f32[16,128,128]{2,1,0:T(8,128)}, u32[]{:S(2)}, u32[]{:S(2)}) collective-permute-start(f32[16,128,128]{2,1,0:T(8,128)S(1)} %constant_dynamic-update-slice_fusion.4.own_pot), channel_id=1, source_target_pairs={{0,56},{1,57},{2,58},{3,59},{4,60},{5,61},{6,62},{7,63},{8,32},{9,... | collective-permute-start | bytes 3145736 | tf_op jit(solution)/shard_map/ppermute | solution.py:27
  46.8 39.2 %copy-start.1 = (f32[16,16]{1,0:T(8,128)S(1)}, f32[16,16]{1,0:T(8,128)}, u32[]{:S(2)}) copy-start(f32[16,16]{1,0:T(8,128)} %rotation.1) | copy-start | bytes 3076
  60.7 25.3 %all-to-all-start = ((f32[16,128,128]{2,1,0:T(8,128)}), f32[16,128,128]{2,1,0:T(8,128)S(1)}, u32[]{:S(2)}, u32[]{:S(2)}) async-start(f32[16,128,128]{2,1,0:T(8,128)} %outer.1), calls=%async_computation | async-start | bytes 2097152 | tf_op jit(solution)/shard_map/all_to_all | solution.py:328
  87.9 10.0 %collective-permute-start.12 = (f32[4,128,128]{2,1,0:T(8,128)S(1)}, f32[4,128,128]{2,1,0:T(8,128)S(1)}, u32[]{:S(2)}, u32[]{:S(2)}) collective-permute-start(f32[4,128,128]{2,1,0:T(8,128)S(1)} %get-tuple-element.20.o0), channel_id=1, source_target_pairs={{0,0},{1,1},{2,2},{3,3},{4,32},{5,33},{6,34},{7,35},{8,8},{9,9},{1... | collective-permute-start | bytes 786440 | tf_op jit(solution)/shard_map/ppermute | solution.py:27
  92.5 16.7 %collective-permute-start.13 = (f32[4,128,128]{2,1,0:T(8,128)S(1)}, f32[4,128,128]{2,1,0:T(8,128)S(1)}, u32[]{:S(2)}, u32[]{:S(2)}) collective-permute-start(f32[4,128,128]{2,1,0:T(8,128)S(1)} %get-tuple-element.21.o1), channel_id=1, source_target_pairs={{0,32},{1,33},{2,34},{3,35},{4,0},{5,1},{6,2},{7,3},{8,40},{9,41},... | collective-permute-start | bytes 786440 | tf_op jit(solution)/shard_map/ppermute | solution.py:27
  92.6 16.6 %collective-permute-start.14 = (f32[4,128,128]{2,1,0:T(8,128)S(1)}, f32[4,128,128]{2,1,0:T(8,128)S(1)}, u32[]{:S(2)}, u32[]{:S(2)}) collective-permute-start(f32[4,128,128]{2,1,0:T(8,128)S(1)} %get-tuple-element.22.o2), channel_id=1, source_target_pairs={{0,64},{1,65},{2,66},{3,67},{4,96},{5,97},{6,98},{7,99},{8,72},{9,... | collective-permute-start | bytes 786440 | tf_op jit(solution)/shard_map/ppermute | solution.py:27
  93.7 15.4 %collective-permute-start.15 = (f32[4,128,128]{2,1,0:T(8,128)S(1)}, f32[4,128,128]{2,1,0:T(8,128)S(1)}, u32[]{:S(2)}, u32[]{:S(2)}) collective-permute-start(f32[4,128,128]{2,1,0:T(8,128)S(1)} %get-tuple-element.23.o3), channel_id=1, source_target_pairs={{0,96},{1,97},{2,98},{3,99},{4,64},{5,65},{6,66},{7,67},{8,104},{9... | collective-permute-start | bytes 786440 | tf_op jit(solution)/shard_map/ppermute | solution.py:27
  99.8 19.4 %all-to-all-start.1 = ((f32[128,1,256]{2,1,0:T(1,128)}), f32[128,1,256]{2,1,0:T(1,128)S(1)}, u32[]{:S(2)}, u32[]{:S(2)}) async-start(f32[128,1,256]{2,1,0:T(1,128)} %copy.8), calls=%async_computation.1 | async-start | bytes 262144 | tf_op jit(solution)/shard_map/all_to_all | solution.py:333

commit v7 on v6

--- a/solution.py
+++ b/solution.py
@@ -95,7 +95,7 @@
         )
 
 
-def four_planes(src, dst, pot, along, p, first_step):
+def four_planes(src, dst, pot, along, p, first_step, out=None, places=None):
     for t in range(N // 8):
         r = PAD + 8 * t
         column = [src[p + k - 2, r : r + 8, :] for k in range(8)]
@@ -110,6 +110,9 @@
                 res = 0.5 * res
             else:
                 res = res - dst[p + k, r : r + 8, :]
+            if out is not None:
+                out[places[k], 8 * t : 8 * t + 8, :] = res
+                continue
             dst[p + k, r : r + 8, :] = res
             if t == 0:
                 dst[p + k, N + PAD : ROWS, :] = res
@@ -117,13 +120,14 @@
                 dst[p + k, 0:PAD, :] = res
 
 
-def advance(src, dst, pot, along, matrix, first, count, first_step):
+def advance(src, dst, pot, along, matrix, first, count, first_step, out=None):
     products(src, along[0], matrix, first)
     for group in range(count // 4):
         p = first + 4 * group
         if 4 * group + 4 < count:
             products(src, along[(group + 1) % 2], matrix, p + 4)
-        four_planes(src, dst, pot, along[group % 2], p, first_step)
+        places = [4 * k + group for k in range(4)]
+        four_planes(src, dst, pot, along[group % 2], p, first_step, out, places)
 
 
 def inner_kernel(
@@ -185,21 +189,10 @@
             src[base + k] = edges[4 * before + k]
 
         first = 2 * step + core * (18 - 4 * step)
-        advance(src, dst, pot, (even, odd), matrix, first, OWN, step == 1)
-
-    last = one if DEGREE % 2 == 0 else two
-    copies = []
-    for n in range(OWN):
-        q = 4 * (n % 4) + n // 4
-        copies.append(
-            pltpu.make_async_copy(
-                last.at[16 - 14 * core + q, pl.ds(PAD, N), :], out.at[n], sems.at[n]
-            )
+        advance(
+            src, dst, pot, (even, odd), matrix, first, OWN, step == 1,
+            out if step == DEGREE else None,
         )
-    for copy in copies:
-        copy.start()
-    for copy in copies:
-        copy.wait()
 
 
 def filter_call(kernel, name, planes, places, shape, place_out, args):
@@ -225,7 +218,7 @@
         (place, own, sibling, own_pot, sibling_pot),
     )
     return filter_call(
-        outer_kernel, "outer", 2 * OWN + 2, [pl.ANY] * 3 + [pltpu.VMEM], (OWN, N, N), pl.ANY,
+        outer_kernel, "outer", 2 * OWN + 2, [pl.ANY] * 3 + [pltpu.VMEM], (OWN, N, N), pltpu.VMEM,
         (place, outer, outer_pot, own_pot, edges),
     )
 
@@ -280,7 +273,7 @@
                     if other < rel:
                         back = 16 * column + 4 * (place[0] ^ rel) + j
                         sums[pl.ds(back, 1), :] = total
-    out[...] = lax.dot_general(
+    out[:, 0, :] = lax.dot_general(
         jnp.ones((N, N), jnp.float32),
         sums[...],
         (((1,), (1,)), ((), ())),
@@ -294,7 +287,7 @@
     smem = pl.BlockSpec(memory_space=pltpu.SMEM)
     return pl.pallas_call(
         gram_kernel,
-        out_shape=jax.ShapeDtypeStruct((N, 256), jnp.float32),
+        out_shape=jax.ShapeDtypeStruct((N, 1, 256), jnp.float32),
         in_specs=[smem] + [vmem] * 4,
         out_specs=vmem,
         scratch_shapes=[pltpu.VMEM((256, N), jnp.float32)],
@@ -309,18 +302,18 @@
     x_lo = lax.axis_index("x_lo")
     z = lax.axis_index("z")
     place = jnp.stack([core, z]).astype(jnp.int32)
-    orbs = [
-        moved(
-            lax.dynamic_index_in_dim(orbitals, (z + s) % 4, 0, keepdims=False), to_orbital(s)
-        )
-        for s in range(4)
+    blocks = [
+        lax.dynamic_index_in_dim(orbitals, (z + s) % 4, 0, keepdims=False) for s in range(4)
     ]
     diagonal = FACTOR * potential + DIAG
+    blocks[2], diagonal = lax.optimization_barrier((blocks[2], diagonal))
+    orbs = [moved(block, to_orbital(s)) for s, block in enumerate(blocks)]
     pots = [moved(diagonal, pot_to_orbital(s)) for s in range(4)]
     own = jnp.concatenate(orbs, axis=0)
     own_pot = jnp.concatenate(pots, axis=0)
     outer = moved(own, to_outer)
-    sibling = moved(own, to_sibling)
+    late, *_ = lax.optimization_barrier((own, pots[0], pots[1]))
+    sibling = moved(late, to_sibling)
     outer_pot = moved(own_pot, to_outer)
     sibling_pot = moved(own_pot, to_sibling)
     sibling, outer = lax.optimization_barrier((sibling, outer))
@@ -331,7 +324,7 @@
     home = [moved(parts[2 * a + e], to_home(a, e)) for a in range(2) for e in range(2)]
     parts, home[0] = lax.optimization_barrier((parts, home[0]))
     rows = lax.all_to_all(gram_rows(base, parts), AXES, 0, 0, tiled=True)
-    total = jnp.sum(rows, axis=0)
+    total = jnp.sum(rows, axis=(0, 1))
     total = total.reshape(16, 16) / (N * N * N)
     correlation = lax.dynamic_slice_in_dim(total, 4 * (2 * x_hi + core), 4, 0)
     band = 2 * x_hi + core

time: 120 us -> 119 us (level)
  waiting for transfers between devices: 39.4 us -> 35 us
  starting transfers between devices: 54.5 us -> 57.9 us
    ppermute x16, waiting for transfers between devices: 15.6 us -> 11.1 us  [moved(): return lax.ppermute(array, AXES, pairs)]
    ppermute x16, starting transfers between devices: 35.1 us -> 39.2 us  [moved(): return lax.ppermute(array, AXES, pairs)]
  transfers between devices with their start and end apart: 18 -> 18, of which waited for: 9 -> 8; matrix products, arithmetic and copies ran while one was open for 2% -> 1% of each run, Pallas kernels for 7% -> 8%
where the time goes in v7:
time: 119 us
  starting transfers between devices  57.9 us (49%)
  waiting for transfers between devices  35 us (29%)
  Pallas kernels  21.2 us (18%)
  local copies, waits for them, and re-layouts  3.2 us (3%)
    ppermute x16, starting transfers between devices, moved(): return lax.ppermute(array, AXES, pairs)  39.2 us
    pallas_call x2, Pallas kernels, filter_call(): pl.pallas_call(kernel, out_shape=jax.ShapeDtypeStruct(shape, jnp.float32)...  17.5 us
    all_to_all x1, waiting for transfers between devices, local(): planes = lax.all_to_all(mine, ('x_hi', 'x_lo', 'z'), 0, 0, tiled=True)  15.2 us
    ppermute x16, waiting for transfers between devices, moved(): return lax.ppermute(array, AXES, pairs)  11.1 us
    all_to_all x1, starting transfers between devices, local(): planes = lax.all_to_all(mine, ('x_hi', 'x_lo', 'z'), 0, 0, tiled=True)  9.93 us
    all_to_all x1, starting transfers between devices, local(): rows = lax.all_to_all(gram_rows(base, parts), AXES, 0, 0, tiled=True)  8.8 us
    all_to_all x1, waiting for transfers between devices, local(): rows = lax.all_to_all(gram_rows(base, parts), AXES, 0, 0, tiled=True)  8.63 us
  transfers between devices with their start and end apart: 18, of which 8 were waited for; matrix products, arithmetic and copies ran while one was open for 1% of the time, Pallas kernels for 8%

profile of v7, /device:TPU:1, one launch (start us, length us, event | category | flops | bytes accessed | tf_op | source)
XLA Modules:
  0.0 118.8 jit_solution(13082932779646072201)
XLA Ops:
  0.7 1.3 %dynamic-slice_bitcast_fusion = (f32[4,128,128]{2,1,0:T(8,128)S(1)}, f32[4,128,128]{2,1,0:T(8,128)S(1)}, f32[4,128,128]{2,1,0:T(8,128)S(1)}, f32[4,128,128]{2,1,0:T(8,128)S(1)}) fusion(f32[4,4,128,128]{3,2,1,0:T(8,128)} %param.5, s32[]{:T(128)S(6)} %select_n.118, s32[]{:T(128)S(6)} %select_n.114, s32[]{:T(128)S(6)} %select_n.112, s32[]{:T(128)S(6)} %select_n.116), kind=kLoop, calls=%fused_computation.5 | loop fusion | bytes 2097168 | tf_op jit(solution)/shard_map/jit(dynamic_index_in_dim)/squeeze | solution.py:306
  2.0 4.5 %collective-permute-start = (f32[4,128,128]{2,1,0:T(8,128)S(1)}, f32[4,128,128]{2,1,0:T(8,128)S(1)}, u32[]{:S(2)}, u32[]{:S(2)}) collective-permute-start(f32[4,128,128]{2,1,0:T(8,128)S(1)} %get-tuple-element.38), channel_id=1, source_target_pairs={{0,0},{1,1},{2,2},{3,3},{4,32},{5,33},{6,34},{7,35},{8,8},{9,9},{1... | collective-permute-start | bytes 786440 | tf_op jit(solution)/shard_map/ppermute | solution.py:27
  6.5 1.4 %collective-permute-start.1 = (f32[4,128,128]{2,1,0:T(8,128)S(1)}, f32[4,128,128]{2,1,0:T(8,128)S(1)}, u32[]{:S(2)}, u32[]{:S(2)}) collective-permute-start(f32[4,128,128]{2,1,0:T(8,128)S(1)} %get-tuple-element.37), channel_id=1, source_target_pairs={{0,1},{1,2},{2,3},{3,0},{4,33},{5,34},{6,35},{7,32},{8,9},{9,10},{... | collective-permute-start | bytes 786440 | tf_op jit(solution)/shard_map/ppermute | solution.py:27
  8.0 4.8 %collective-permute-start.2 = (f32[4,128,128]{2,1,0:T(8,128)S(1)}, f32[4,128,128]{2,1,0:T(8,128)S(1)}, u32[]{:S(2)}, u32[]{:S(2)}) collective-permute-start(f32[4,128,128]{2,1,0:T(8,128)S(1)} %get-tuple-element.16), channel_id=1, source_target_pairs={{0,2},{1,3},{2,0},{3,1},{4,34},{5,35},{6,32},{7,33},{8,10},{9,11},... | collective-permute-start | bytes 786440 | tf_op jit(solution)/shard_map/ppermute | solution.py:27
  12.8 3.4 %collective-permute-start.4 = (f32[4,128,128]{2,1,0:T(8,128)S(1)}, f32[4,128,128]{2,1,0:T(8,128)S(1)}, u32[]{:S(2)}, u32[]{:S(2)}) collective-permute-start(f32[4,128,128]{2,1,0:T(8,128)S(1)} %multiply_add_fusion), channel_id=1, source_target_pairs={{0,0},{1,1},{2,2},{3,3},{4,96},{5,97},{6,98},{7,99},{8,8},{9,9},{1... | collective-permute-start | bytes 786440 | tf_op jit(solution)/shard_map/ppermute | solution.py:27
  16.4 3.0 %collective-permute-start.3 = (f32[4,128,128]{2,1,0:T(8,128)S(1)}, f32[4,128,128]{2,1,0:T(8,128)S(1)}, u32[]{:S(2)}, u32[]{:S(2)}) collective-permute-start(f32[4,128,128]{2,1,0:T(8,128)S(1)} %get-tuple-element.36), channel_id=1, source_target_pairs={{0,3},{1,0},{2,1},{3,2},{4,35},{5,32},{6,33},{7,34},{8,11},{9,8},{... | collective-permute-start | bytes 786440 | tf_op jit(solution)/shard_map/ppermute | solution.py:27
  19.4 1.4 %collective-permute-start.8 = (f32[4,128,128]{2,1,0:T(8,128)S(1)}, f32[4,128,128]{2,1,0:T(8,128)S(1)}, u32[]{:S(2)}, u32[]{:S(2)}) collective-permute-start(f32[4,128,128]{2,1,0:T(8,128)S(1)} %multiply_add_fusion), channel_id=1, source_target_pairs={{0,2},{1,3},{2,0},{3,1},{4,98},{5,99},{6,96},{7,97},{8,10},{9,11},... | collective-permute-start | bytes 786440 | tf_op jit(solution)/shard_map/ppermute | solution.py:27
  20.8 2.7 %collective-permute-start.9 = (f32[4,128,128]{2,1,0:T(8,128)S(1)}, f32[4,128,128]{2,1,0:T(8,128)S(1)}, u32[]{:S(2)}, u32[]{:S(2)}) collective-permute-start(f32[4,128,128]{2,1,0:T(8,128)S(1)} %multiply_add_fusion), channel_id=1, source_target_pairs={{0,3},{1,0},{2,1},{3,2},{4,99},{5,96},{6,97},{7,98},{8,11},{9,8},{... | collective-permute-start | bytes 786440 | tf_op jit(solution)/shard_map/ppermute | solution.py:27
  23.6 0.4 collective-permute-start.7
  24.0 1.5 %collective-permute-done.5 = f32[4,128,128]{2,1,0:T(8,128)S(1)} collective-permute-done((f32[4,128,128]{2,1,0:T(8,128)S(1)}, f32[4,128,128]{2,1,0:T(8,128)S(1)}, u32[]{:S(2)}, u32[]{:S(2)}) %collective-permute-start.5) | collective-permute-done | bytes 262176 | tf_op jit(solution)/shard_map/ppermute | solution.py:27
  25.5 5.5 %collective-permute-start.6 = (f32[16,128,128]{2,1,0:T(8,128)S(1)}, f32[16,128,128]{2,1,0:T(8,128)}, u32[]{:S(2)}, u32[]{:S(2)}) collective-permute-start(f32[16,128,128]{2,1,0:T(8,128)S(1)} %constant_dynamic-update-slice_fusion.own), channel_id=1, source_target_pairs={{0,32},{1,33},{2,34},{3,35},{4,36},{5,37},{6,38},{7,39},{8,40},{9,... | collective-permute-start | bytes 3145736 | tf_op jit(solution)/shard_map/ppermute | solution.py:27
  31.1 1.7 %collective-permute-done.9 = f32[4,128,128]{2,1,0:T(8,128)S(1)} collective-permute-done((f32[4,128,128]{2,1,0:T(8,128)S(1)}, f32[4,128,128]{2,1,0:T(8,128)S(1)}, u32[]{:S(2)}, u32[]{:S(2)}) %collective-permute-start.9) | collective-permute-done | bytes 262176 | tf_op jit(solution)/shard_map/ppermute | solution.py:27
  32.8 3.7 %collective-permute-start.11 = (f32[16,128,128]{2,1,0:T(8,128)S(1)}, f32[16,128,128]{2,1,0:T(8,128)}, u32[]{:S(2)}, u32[]{:S(2)}) collective-permute-start(f32[16,128,128]{2,1,0:T(8,128)S(1)} %constant_dynamic-update-slice_fusion.4.own_pot), channel_id=1, source_target_pairs={{0,32},{1,33},{2,34},{3,35},{4,36},{5,37},{6,38},{7,39},{8,40},{9,... | collective-permute-start | bytes 3145736 | tf_op jit(solution)/shard_map/ppermute | solution.py:27
  36.5 1.3 %collective-permute-start.10 = (f32[16,128,128]{2,1,0:T(8,128)S(1)}, f32[16,128,128]{2,1,0:T(8,128)}, u32[]{:S(2)}, u32[]{:S(2)}) collective-permute-start(f32[16,128,128]{2,1,0:T(8,128)S(1)} %constant_dynamic-update-slice_fusion.4.own_pot), channel_id=1, source_target_pairs={{0,56},{1,57},{2,58},{3,59},{4,60},{5,61},{6,62},{7,63},{8,32},{9,... | collective-permute-start | bytes 3145736 | tf_op jit(solution)/shard_map/ppermute | solution.py:27
  37.9 0.3 collective-permute-done.7.outer
  38.1 0.8 collective-permute-done.11.sibling_pot
  38.9 8.2 %inner.1.edges = f32[32,144,128]{2,1,0:T(8,128)S(1)} custom-call(s32[2]{0:T(128)S(1)} %pad_add_fusion.place, f32[16,128,128]{2,1,0:T(8,128)S(1)} %constant_dynamic-update-slice_fusion.own, f32[16,128,128]{2,1,0:T(8,128)} %collective-permute-done.6.sibling, f32[16,128,128]{2,1,0:T(8,128)S(1)} %constant_dynamic-update-slice_fusion.4.own_pot, ...), custom_call_target="tpu_custom_call" | custom-call | flops 1000 | tf_op jit(solution)/shard_map/inner/pallas_call | solution.py:199
  47.1 4.0 %collective-permute-done.10.outer_pot = f32[16,128,128]{2,1,0:T(8,128)} collective-permute-done((f32[16,128,128]{2,1,0:T(8,128)S(1)}, f32[16,128,128]{2,1,0:T(8,128)}, u32[]{:S(2)}, u32[]{:S(2)}) %collective-permute-start.10) | collective-permute-done | bytes 1048608 | tf_op jit(solution)/shard_map/ppermute | solution.py:27
  51.1 9.4 %outer.1 = f32[16,128,128]{2,1,0:T(8,128)} custom-call(s32[2]{0:T(128)S(1)} %pad_add_fusion.place, f32[16,128,128]{2,1,0:T(8,128)S(1)} %collective-permute-done.7.outer, f32[16,128,128]{2,1,0:T(8,128)} %collective-permute-done.10.outer_pot, f32[16,128,128]{2,1,0:T(8,128)S(1)} %constant_dynamic-update-slice_fusion.4.own_pot, f32[32,144,128]{2,1,0:T(8,128)S(1)} %inner.1.edges, ...), custom_call_target="tpu_custom_call" | custom-call | flops 1000 | tf_op jit(solution)/shard_map/outer/pallas_call | solution.py:199
  60.5 9.9 %all-to-all-start = ((f32[16,128,128]{2,1,0:T(8,128)}), f32[16,128,128]{2,1,0:T(8,128)S(1)}, u32[]{:S(2)}, u32[]{:S(2)}) async-start(f32[16,128,128]{2,1,0:T(8,128)} %outer.1), calls=%async_computation | async-start | bytes 2097152 | tf_op jit(solution)/shard_map/all_to_all | solution.py:321
  70.4 15.2 %all-to-all-done.x = f32[16,128,128]{2,1,0:T(8,128)S(1)} async-done(((f32[16,128,128]{2,1,0:T(8,128)}), f32[16,128,128]{2,1,0:T(8,128)S(1)}, u32[]{:S(2)}, u32[]{:S(2)}) %all-to-all-start) | async-done | bytes 1048608 | tf_op jit(solution)/shard_map/all_to_all | solution.py:321
  85.7 2.0 %rotate.1 = (f32[4,128,128]{2,1,0:T(8,128)S(1)}, f32[4,128,128]{2,1,0:T(8,128)S(1)}, f32[4,128,128]{2,1,0:T(8,128)S(1)}, f32[4,128,128]{2,1,0:T(8,128)S(1)}) custom-call(s32[1]{0:T(128)} %bitcast.place, f32[16,16]{1,0:T(8,128)S(1)} %copy-done.1, f32[16,128,128]{2,1,0:T(8,128)S(1)} %all-to-all-done.x), custom_call_target="tpu_custom_call" | custom-call | tf_op jit(solution)/shard_map/rotate/pallas_call | solution.py:245
  87.6 4.4 %collective-permute-start.12 = (f32[4,128,128]{2,1,0:T(8,128)S(1)}, f32[4,128,128]{2,1,0:T(8,128)S(1)}, u32[]{:S(2)}, u32[]{:S(2)}) collective-permute-start(f32[4,128,128]{2,1,0:T(8,128)S(1)} %get-tuple-element.26.o0), channel_id=1, source_target_pairs={{0,0},{1,1},{2,2},{3,3},{4,32},{5,33},{6,34},{7,35},{8,8},{9,9},{1... | collective-permute-start | bytes 786440 | tf_op jit(solution)/shard_map/ppermute | solution.py:27
  92.1 1.3 %collective-permute-start.14 = (f32[4,128,128]{2,1,0:T(8,128)S(1)}, f32[4,128,128]{2,1,0:T(8,128)S(1)}, u32[]{:S(2)}, u32[]{:S(2)}) collective-permute-start(f32[4,128,128]{2,1,0:T(8,128)S(1)} %get-tuple-element.28.o2), channel_id=1, source_target_pairs={{0,64},{1,65},{2,66},{3,67},{4,96},{5,97},{6,98},{7,99},{8,72},{9,... | collective-permute-start | bytes 786440 | tf_op jit(solution)/shard_map/ppermute | solution.py:27
  93.4 1.2 %collective-permute-start.15 = (f32[4,128,128]{2,1,0:T(8,128)S(1)}, f32[4,128,128]{2,1,0:T(8,128)S(1)}, u32[]{:S(2)}, u32[]{:S(2)}) collective-permute-start(f32[4,128,128]{2,1,0:T(8,128)S(1)} %get-tuple-element.29.o3), channel_id=1, source_target_pairs={{0,96},{1,97},{2,98},{3,99},{4,64},{5,65},{6,66},{7,67},{8,104},{9... | collective-permute-start | bytes 786440 | tf_op jit(solution)/shard_map/ppermute | solution.py:27
  94.6 2.8 %collective-permute-done.12 = f32[4,128,128]{2,1,0:T(8,128)S(1)} collective-permute-done((f32[4,128,128]{2,1,0:T(8,128)S(1)}, f32[4,128,128]{2,1,0:T(8,128)S(1)}, u32[]{:S(2)}, u32[]{:S(2)}) %collective-permute-start.12) | collective-permute-done | bytes 262176 | tf_op jit(solution)/shard_map/ppermute | solution.py:27
  97.4 1.7 %gram.1 = f32[128,1,256]{2,1,0:T(1,128)} custom-call(s32[1]{0:T(128)} %bitcast.place, f32[4,128,128]{2,1,0:T(8,128)S(1)} %get-tuple-element.26.o0, f32[4,128,128]{2,1,0:T(8,128)S(1)} %get-tuple-element.27.o1, f32[4,128,128]{2,1,0:T(8,128)S(1)} %get-tuple-element.28.o2, f32[4,128,128]{2,1,0:T(8,128)S(1)} %get-tuple-element.29.o3), custom_call_target="tpu_custom_call" | custom-call | tf_op jit(solution)/shard_map/gram/pallas_call | solution.py:288
  99.1 8.8 %all-to-all-start.1 = ((f32[128,1,256]{2,1,0:T(1,128)}), f32[128,1,256]{2,1,0:T(1,128)S(1)}, u32[]{:S(2)}, u32[]{:S(2)}) async-start(f32[128,1,256]{2,1,0:T(1,128)} %gram.1), calls=%async_computation.1 | async-start | bytes 262144 | tf_op jit(solution)/shard_map/all_to_all | solution.py:326
  108.2 1.1 copy.7
  109.3 8.6 %all-to-all-done.1 = f32[128,1,256]{2,1,0:T(1,128)S(1)} async-done(((f32[128,1,256]{2,1,0:T(1,128)}), f32[128,1,256]{2,1,0:T(1,128)S(1)}, u32[]{:S(2)}, u32[]{:S(2)}) %all-to-all-start.1) | async-done | bytes 131104 | tf_op jit(solution)/shard_map/all_to_all | solution.py:326
  117.9 0.2 reduce_sum.9
  118.2 0.6 constant_dynamic-slice_fusion
  (32 shorter events, 0.8 us)
Async XLA Ops:
  0.6 7.3 %copy-start.2 = (f32[4,128,128]{2,1,0:T(8,128)S(1)}, f32[4,128,128]{2,1,0:T(8,128)}, u32[]{:S(2)}) copy-start(f32[4,128,128]{2,1,0:T(8,128)} %param.6) | copy-start | bytes 786436
  2.0 14.4 %collective-permute-start = (f32[4,128,128]{2,1,0:T(8,128)S(1)}, f32[4,128,128]{2,1,0:T(8,128)S(1)}, u32[]{:S(2)}, u32[]{:S(2)}) collective-permute-start(f32[4,128,128]{2,1,0:T(8,128)S(1)} %get-tuple-element.38), channel_id=1, source_target_pairs={{0,0},{1,1},{2,2},{3,3},{4,32},{5,33},{6,34},{7,35},{8,8},{9,9},{1... | collective-permute-start | bytes 786440 | tf_op jit(solution)/shard_map/ppermute | solution.py:27
  6.5 32.4 %copy-start = (bf16[256,128]{1,0:T(8,128)(2,1)S(1)}, bf16[256,128]{1,0:T(8,128)(2,1)}, u32[]{:S(2)}) copy-start(bf16[256,128]{1,0:T(8,128)(2,1)} %constant.71.clone.matrix) | copy-start | bytes 196612
  6.5 12.8 %collective-permute-start.1 = (f32[4,128,128]{2,1,0:T(8,128)S(1)}, f32[4,128,128]{2,1,0:T(8,128)S(1)}, u32[]{:S(2)}, u32[]{:S(2)}) collective-permute-start(f32[4,128,128]{2,1,0:T(8,128)S(1)} %get-tuple-element.37), channel_id=1, source_target_pairs={{0,1},{1,2},{2,3},{3,0},{4,33},{5,34},{6,35},{7,32},{8,9},{9,10},{... | collective-permute-start | bytes 786440 | tf_op jit(solution)/shard_map/ppermute | solution.py:27
  8.0 12.8 %collective-permute-start.2 = (f32[4,128,128]{2,1,0:T(8,128)S(1)}, f32[4,128,128]{2,1,0:T(8,128)S(1)}, u32[]{:S(2)}, u32[]{:S(2)}) collective-permute-start(f32[4,128,128]{2,1,0:T(8,128)S(1)} %get-tuple-element.16), channel_id=1, source_target_pairs={{0,2},{1,3},{2,0},{3,1},{4,34},{5,35},{6,32},{7,33},{8,10},{9,11},... | collective-permute-start | bytes 786440 | tf_op jit(solution)/shard_map/ppermute | solution.py:27
  12.8 11.1 %collective-permute-start.4 = (f32[4,128,128]{2,1,0:T(8,128)S(1)}, f32[4,128,128]{2,1,0:T(8,128)S(1)}, u32[]{:S(2)}, u32[]{:S(2)}) collective-permute-start(f32[4,128,128]{2,1,0:T(8,128)S(1)} %multiply_add_fusion), channel_id=1, source_target_pairs={{0,0},{1,1},{2,2},{3,3},{4,96},{5,97},{6,98},{7,99},{8,8},{9,9},{1... | collective-permute-start | bytes 786440 | tf_op jit(solution)/shard_map/ppermute | solution.py:27
  16.3 9.2 %collective-permute-start.5 = (f32[4,128,128]{2,1,0:T(8,128)S(1)}, f32[4,128,128]{2,1,0:T(8,128)S(1)}, u32[]{:S(2)}, u32[]{:S(2)}) collective-permute-start(f32[4,128,128]{2,1,0:T(8,128)S(1)} %multiply_add_fusion), channel_id=1, source_target_pairs={{0,1},{1,2},{2,3},{3,0},{4,97},{5,98},{6,99},{7,96},{8,9},{9,10},{... | collective-permute-start | bytes 786440 | tf_op jit(solution)/shard_map/ppermute | solution.py:27
  16.4 7.1 %collective-permute-start.3 = (f32[4,128,128]{2,1,0:T(8,128)S(1)}, f32[4,128,128]{2,1,0:T(8,128)S(1)}, u32[]{:S(2)}, u32[]{:S(2)}) collective-permute-start(f32[4,128,128]{2,1,0:T(8,128)S(1)} %get-tuple-element.36), channel_id=1, source_target_pairs={{0,3},{1,0},{2,1},{3,2},{4,35},{5,32},{6,33},{7,34},{8,11},{9,8},{... | collective-permute-start | bytes 786440 | tf_op jit(solution)/shard_map/ppermute | solution.py:27
  19.4 11.7 %collective-permute-start.8 = (f32[4,128,128]{2,1,0:T(8,128)S(1)}, f32[4,128,128]{2,1,0:T(8,128)S(1)}, u32[]{:S(2)}, u32[]{:S(2)}) collective-permute-start(f32[4,128,128]{2,1,0:T(8,128)S(1)} %multiply_add_fusion), channel_id=1, source_target_pairs={{0,2},{1,3},{2,0},{3,1},{4,98},{5,99},{6,96},{7,97},{8,10},{9,11},... | collective-permute-start | bytes 786440 | tf_op jit(solution)/shard_map/ppermute | solution.py:27
  20.8 12.0 %collective-permute-start.9 = (f32[4,128,128]{2,1,0:T(8,128)S(1)}, f32[4,128,128]{2,1,0:T(8,128)S(1)}, u32[]{:S(2)}, u32[]{:S(2)}) collective-permute-start(f32[4,128,128]{2,1,0:T(8,128)S(1)} %multiply_add_fusion), channel_id=1, source_target_pairs={{0,3},{1,0},{2,1},{3,2},{4,99},{5,96},{6,97},{7,98},{8,11},{9,8},{... | collective-permute-start | bytes 786440 | tf_op jit(solution)/shard_map/ppermute | solution.py:27
  23.6 14.6 %collective-permute-start.7 = (f32[16,128,128]{2,1,0:T(8,128)S(1)}, f32[16,128,128]{2,1,0:T(8,128)S(1)}, u32[]{:S(2)}, u32[]{:S(2)}) collective-permute-start(f32[16,128,128]{2,1,0:T(8,128)S(1)} %constant_dynamic-update-slice_fusion.own), channel_id=1, source_target_pairs={{0,56},{1,57},{2,58},{3,59},{4,60},{5,61},{6,62},{7,63},{8,32},{9,... | collective-permute-start | bytes 3145736 | tf_op jit(solution)/shard_map/ppermute | solution.py:27
  25.5 12.3 %collective-permute-start.6 = (f32[16,128,128]{2,1,0:T(8,128)S(1)}, f32[16,128,128]{2,1,0:T(8,128)}, u32[]{:S(2)}, u32[]{:S(2)}) collective-permute-start(f32[16,128,128]{2,1,0:T(8,128)S(1)} %constant_dynamic-update-slice_fusion.own), channel_id=1, source_target_pairs={{0,32},{1,33},{2,34},{3,35},{4,36},{5,37},{6,38},{7,39},{8,40},{9,... | collective-permute-start | bytes 3145736 | tf_op jit(solution)/shard_map/ppermute | solution.py:27
  32.8 6.1 %collective-permute-start.11 = (f32[16,128,128]{2,1,0:T(8,128)S(1)}, f32[16,128,128]{2,1,0:T(8,128)}, u32[]{:S(2)}, u32[]{:S(2)}) collective-permute-start(f32[16,128,128]{2,1,0:T(8,128)S(1)} %constant_dynamic-update-slice_fusion.4.own_pot), channel_id=1, source_target_pairs={{0,32},{1,33},{2,34},{3,35},{4,36},{5,37},{6,38},{7,39},{8,40},{9,... | collective-permute-start | bytes 3145736 | tf_op jit(solution)/shard_map/ppermute | solution.py:27
  36.5 14.6 %collective-permute-start.10 = (f32[16,128,128]{2,1,0:T(8,128)S(1)}, f32[16,128,128]{2,1,0:T(8,128)}, u32[]{:S(2)}, u32[]{:S(2)}) collective-permute-start(f32[16,128,128]{2,1,0:T(8,128)S(1)} %constant_dynamic-update-slice_fusion.4.own_pot), channel_id=1, source_target_pairs={{0,56},{1,57},{2,58},{3,59},{4,60},{5,61},{6,62},{7,63},{8,32},{9,... | collective-permute-start | bytes 3145736 | tf_op jit(solution)/shard_map/ppermute | solution.py:27
  47.1 38.6 %copy-start.1 = (f32[16,16]{1,0:T(8,128)S(1)}, f32[16,16]{1,0:T(8,128)}, u32[]{:S(2)}) copy-start(f32[16,16]{1,0:T(8,128)} %rotation.1) | copy-start | bytes 3076
  60.5 25.2 %all-to-all-start = ((f32[16,128,128]{2,1,0:T(8,128)}), f32[16,128,128]{2,1,0:T(8,128)S(1)}, u32[]{:S(2)}, u32[]{:S(2)}) async-start(f32[16,128,128]{2,1,0:T(8,128)} %outer.1), calls=%async_computation | async-start | bytes 2097152 | tf_op jit(solution)/shard_map/all_to_all | solution.py:321
  87.6 9.8 %collective-permute-start.12 = (f32[4,128,128]{2,1,0:T(8,128)S(1)}, f32[4,128,128]{2,1,0:T(8,128)S(1)}, u32[]{:S(2)}, u32[]{:S(2)}) collective-permute-start(f32[4,128,128]{2,1,0:T(8,128)S(1)} %get-tuple-element.26.o0), channel_id=1, source_target_pairs={{0,0},{1,1},{2,2},{3,3},{4,32},{5,33},{6,34},{7,35},{8,8},{9,9},{1... | collective-permute-start | bytes 786440 | tf_op jit(solution)/shard_map/ppermute | solution.py:27
  92.0 15.9 %collective-permute-start.13 = (f32[4,128,128]{2,1,0:T(8,128)S(1)}, f32[4,128,128]{2,1,0:T(8,128)S(1)}, u32[]{:S(2)}, u32[]{:S(2)}) collective-permute-start(f32[4,128,128]{2,1,0:T(8,128)S(1)} %get-tuple-element.27.o1), channel_id=1, source_target_pairs={{0,32},{1,33},{2,34},{3,35},{4,0},{5,1},{6,2},{7,3},{8,40},{9,41},... | collective-permute-start | bytes 786440 | tf_op jit(solution)/shard_map/ppermute | solution.py:27
  92.1 15.8 %collective-permute-start.14 = (f32[4,128,128]{2,1,0:T(8,128)S(1)}, f32[4,128,128]{2,1,0:T(8,128)S(1)}, u32[]{:S(2)}, u32[]{:S(2)}) collective-permute-start(f32[4,128,128]{2,1,0:T(8,128)S(1)} %get-tuple-element.28.o2), channel_id=1, source_target_pairs={{0,64},{1,65},{2,66},{3,67},{4,96},{5,97},{6,98},{7,99},{8,72},{9,... | collective-permute-start | bytes 786440 | tf_op jit(solution)/shard_map/ppermute | solution.py:27
  93.4 14.5 %collective-permute-start.15 = (f32[4,128,128]{2,1,0:T(8,128)S(1)}, f32[4,128,128]{2,1,0:T(8,128)S(1)}, u32[]{:S(2)}, u32[]{:S(2)}) collective-permute-start(f32[4,128,128]{2,1,0:T(8,128)S(1)} %get-tuple-element.29.o3), channel_id=1, source_target_pairs={{0,96},{1,97},{2,98},{3,99},{4,64},{5,65},{6,66},{7,67},{8,104},{9... | collective-permute-start | bytes 786440 | tf_op jit(solution)/shard_map/ppermute | solution.py:27
  99.1 18.8 %all-to-all-start.1 = ((f32[128,1,256]{2,1,0:T(1,128)}), f32[128,1,256]{2,1,0:T(1,128)S(1)}, u32[]{:S(2)}, u32[]{:S(2)}) async-start(f32[128,1,256]{2,1,0:T(1,128)} %gram.1), calls=%async_computation.1 | async-start | bytes 262144 | tf_op jit(solution)/shard_map/all_to_all | solution.py:326

commit v8 on v7

--- a/solution.py
+++ b/solution.py
@@ -308,6 +308,7 @@
     diagonal = FACTOR * potential + DIAG
     blocks[2], diagonal = lax.optimization_barrier((blocks[2], diagonal))
     orbs = [moved(block, to_orbital(s)) for s, block in enumerate(blocks)]
+    orbs[0], diagonal = lax.optimization_barrier((orbs[0], diagonal))
     pots = [moved(diagonal, pot_to_orbital(s)) for s in range(4)]
     own = jnp.concatenate(orbs, axis=0)
     own_pot = jnp.concatenate(pots, axis=0)

time: 119 us -> 116 us (0.975)
  starting transfers between devices: 57.9 us -> 50.1 us
  waiting for transfers between devices: 35 us -> 39.5 us
    ppermute x16, starting transfers between devices: 39.2 us -> 33.7 us  [moved(): return lax.ppermute(array, AXES, pairs)]
    ppermute x16, waiting for transfers between devices: 11.1 us -> 16.5 us  [moved(): return lax.ppermute(array, AXES, pairs)]
    all_to_all x1, starting transfers between devices: 8.8 us -> 6.76 us  [local(): rows = lax.all_to_all(gram_rows(base, parts), AXES, 0, 0, tiled=True)]
  transfers between devices with their start and end apart: 18 -> 18, of which waited for: 8 -> 9; matrix products, arithmetic and copies ran while one was open for 1% -> 1% of each run, Pallas kernels for 8% -> 9%
where the time goes in v8:
time: 116 us; the launch traced here: 115 us
  starting transfers between devices  50.1 us (43%)
  waiting for transfers between devices  39.5 us (34%)
  Pallas kernels  21.2 us (18%)
  local copies, waits for them, and re-layouts  3.2 us (3%)
    ppermute x16, starting transfers between devices, moved(): return lax.ppermute(array, AXES, pairs)  33.7 us
    pallas_call x2, Pallas kernels, filter_call(): pl.pallas_call(kernel, out_shape=jax.ShapeDtypeStruct(shape, jnp.float32)...  17.5 us
    ppermute x16, waiting for transfers between devices, moved(): return lax.ppermute(array, AXES, pairs)  16.5 us
    all_to_all x1, waiting for transfers between devices, local(): planes = lax.all_to_all(mine, ('x_hi', 'x_lo', 'z'), 0, 0, tiled=True)  15.1 us
    all_to_all x1, starting transfers between devices, local(): planes = lax.all_to_all(mine, ('x_hi', 'x_lo', 'z'), 0, 0, tiled=True)  9.61 us
    all_to_all x1, waiting for transfers between devices, local(): rows = lax.all_to_all(gram_rows(base, parts), AXES, 0, 0, tiled=True)  8 us
    all_to_all x1, starting transfers between devices, local(): rows = lax.all_to_all(gram_rows(base, parts), AXES, 0, 0, tiled=True)  6.76 us
  transfers between devices with their start and end apart: 18, of which 9 were waited for; matrix products, arithmetic and copies ran while one was open for 1% of the time, Pallas kernels for 9%

profile of v8, /device:TPU:1, one launch (start us, length us, event | category | flops | bytes accessed | tf_op | source)
XLA Modules:
  0.0 115.4 jit_solution(8129329024548693083)
XLA Ops:
  0.7 1.3 %dynamic-slice_bitcast_fusion = (f32[4,128,128]{2,1,0:T(8,128)S(1)}, f32[4,128,128]{2,1,0:T(8,128)S(1)}, f32[4,128,128]{2,1,0:T(8,128)S(1)}, f32[4,128,128]{2,1,0:T(8,128)S(1)}) fusion(f32[4,4,128,128]{3,2,1,0:T(8,128)} %param.5, s32[]{:T(128)S(6)} %select_n.118, s32[]{:T(128)S(6)} %select_n.114, s32[]{:T(128)S(6)} %select_n.112, s32[]{:T(128)S(6)} %select_n.116), kind=kLoop, calls=%fused_computation.5 | loop fusion | bytes 2097168 | tf_op jit(solution)/shard_map/jit(dynamic_index_in_dim)/squeeze | solution.py:306
  2.0 4.5 %collective-permute-start = (f32[4,128,128]{2,1,0:T(8,128)S(1)}, f32[4,128,128]{2,1,0:T(8,128)S(1)}, u32[]{:S(2)}, u32[]{:S(2)}) collective-permute-start(f32[4,128,128]{2,1,0:T(8,128)S(1)} %get-tuple-element.42), channel_id=1, source_target_pairs={{0,0},{1,1},{2,2},{3,3},{4,32},{5,33},{6,34},{7,35},{8,8},{9,9},{1... | collective-permute-start | bytes 786440 | tf_op jit(solution)/shard_map/ppermute | solution.py:27
  6.5 1.4 %collective-permute-start.1 = (f32[4,128,128]{2,1,0:T(8,128)S(1)}, f32[4,128,128]{2,1,0:T(8,128)S(1)}, u32[]{:S(2)}, u32[]{:S(2)}) collective-permute-start(f32[4,128,128]{2,1,0:T(8,128)S(1)} %get-tuple-element.43), channel_id=1, source_target_pairs={{0,1},{1,2},{2,3},{3,0},{4,33},{5,34},{6,35},{7,32},{8,9},{9,10},{... | collective-permute-start | bytes 786440 | tf_op jit(solution)/shard_map/ppermute | solution.py:27
  8.0 4.8 %collective-permute-start.2 = (f32[4,128,128]{2,1,0:T(8,128)S(1)}, f32[4,128,128]{2,1,0:T(8,128)S(1)}, u32[]{:S(2)}, u32[]{:S(2)}) collective-permute-start(f32[4,128,128]{2,1,0:T(8,128)S(1)} %get-tuple-element.20), channel_id=1, source_target_pairs={{0,2},{1,3},{2,0},{3,1},{4,34},{5,35},{6,32},{7,33},{8,10},{9,11},... | collective-permute-start | bytes 786440 | tf_op jit(solution)/shard_map/ppermute | solution.py:27
  12.8 0.5 collective-permute-start.3
  13.3 4.9 %collective-permute-start.4 = (f32[4,128,128]{2,1,0:T(8,128)S(1)}, f32[4,128,128]{2,1,0:T(8,128)S(1)}, u32[]{:S(2)}, u32[]{:S(2)}) collective-permute-start(f32[4,128,128]{2,1,0:T(8,128)S(1)} %multiply_add_fusion), channel_id=1, source_target_pairs={{0,0},{1,1},{2,2},{3,3},{4,96},{5,97},{6,98},{7,99},{8,8},{9,9},{1... | collective-permute-start | bytes 786440 | tf_op jit(solution)/shard_map/ppermute | solution.py:27
  18.2 0.5 collective-permute-start.5
  18.8 4.2 %collective-permute-start.8 = (f32[4,128,128]{2,1,0:T(8,128)S(1)}, f32[4,128,128]{2,1,0:T(8,128)S(1)}, u32[]{:S(2)}, u32[]{:S(2)}) collective-permute-start(f32[4,128,128]{2,1,0:T(8,128)S(1)} %multiply_add_fusion), channel_id=1, source_target_pairs={{0,2},{1,3},{2,0},{3,1},{4,98},{5,99},{6,96},{7,97},{8,10},{9,11},... | collective-permute-start | bytes 786440 | tf_op jit(solution)/shard_map/ppermute | solution.py:27
  23.0 1.0 collective-permute-start.9
  24.2 3.7 %collective-permute-done.5 = f32[4,128,128]{2,1,0:T(8,128)S(1)} collective-permute-done((f32[4,128,128]{2,1,0:T(8,128)S(1)}, f32[4,128,128]{2,1,0:T(8,128)S(1)}, u32[]{:S(2)}, u32[]{:S(2)}) %collective-permute-start.5) | collective-permute-done | bytes 262176 | tf_op jit(solution)/shard_map/ppermute | solution.py:27
  28.0 2.3 %collective-permute-done.8 = f32[4,128,128]{2,1,0:T(8,128)S(1)} collective-permute-done((f32[4,128,128]{2,1,0:T(8,128)S(1)}, f32[4,128,128]{2,1,0:T(8,128)S(1)}, u32[]{:S(2)}, u32[]{:S(2)}) %collective-permute-start.8) | collective-permute-done | bytes 262176 | tf_op jit(solution)/shard_map/ppermute | solution.py:27
  30.3 1.2 %collective-permute-done.9 = f32[4,128,128]{2,1,0:T(8,128)S(1)} collective-permute-done((f32[4,128,128]{2,1,0:T(8,128)S(1)}, f32[4,128,128]{2,1,0:T(8,128)S(1)}, u32[]{:S(2)}, u32[]{:S(2)}) %collective-permute-start.9) | collective-permute-done | bytes 262176 | tf_op jit(solution)/shard_map/ppermute | solution.py:27
  31.5 3.2 %collective-permute-start.11 = (f32[16,128,128]{2,1,0:T(8,128)S(1)}, f32[16,128,128]{2,1,0:T(8,128)}, u32[]{:S(2)}, u32[]{:S(2)}) collective-permute-start(f32[16,128,128]{2,1,0:T(8,128)S(1)} %constant_dynamic-update-slice_fusion.4.own_pot), channel_id=1, source_target_pairs={{0,32},{1,33},{2,34},{3,35},{4,36},{5,37},{6,38},{7,39},{8,40},{9,... | collective-permute-start | bytes 3145736 | tf_op jit(solution)/shard_map/ppermute | solution.py:27
  34.8 1.3 %collective-permute-start.10 = (f32[16,128,128]{2,1,0:T(8,128)S(1)}, f32[16,128,128]{2,1,0:T(8,128)}, u32[]{:S(2)}, u32[]{:S(2)}) collective-permute-start(f32[16,128,128]{2,1,0:T(8,128)S(1)} %constant_dynamic-update-slice_fusion.4.own_pot), channel_id=1, source_target_pairs={{0,56},{1,57},{2,58},{3,59},{4,60},{5,61},{6,62},{7,63},{8,32},{9,... | collective-permute-start | bytes 3145736 | tf_op jit(solution)/shard_map/ppermute | solution.py:27
  36.1 2.6 %collective-permute-done.7.outer = f32[16,128,128]{2,1,0:T(8,128)S(1)} collective-permute-done((f32[16,128,128]{2,1,0:T(8,128)S(1)}, f32[16,128,128]{2,1,0:T(8,128)S(1)}, u32[]{:S(2)}, u32[]{:S(2)}) %collective-permute-start.7) | collective-permute-done | bytes 1048608 | tf_op jit(solution)/shard_map/ppermute | solution.py:27
  38.7 8.2 %inner.1.edges = f32[32,144,128]{2,1,0:T(8,128)S(1)} custom-call(s32[2]{0:T(128)S(1)} %pad_add_fusion.place, f32[16,128,128]{2,1,0:T(8,128)S(1)} %constant_dynamic-update-slice_fusion.own, f32[16,128,128]{2,1,0:T(8,128)} %collective-permute-done.6.sibling, f32[16,128,128]{2,1,0:T(8,128)S(1)} %constant_dynamic-update-slice_fusion.4.own_pot, ...), custom_call_target="tpu_custom_call" | custom-call | flops 1000 | tf_op jit(solution)/shard_map/inner/pallas_call | solution.py:199
  46.9 3.1 %collective-permute-done.10.outer_pot = f32[16,128,128]{2,1,0:T(8,128)} collective-permute-done((f32[16,128,128]{2,1,0:T(8,128)S(1)}, f32[16,128,128]{2,1,0:T(8,128)}, u32[]{:S(2)}, u32[]{:S(2)}) %collective-permute-start.10) | collective-permute-done | bytes 1048608 | tf_op jit(solution)/shard_map/ppermute | solution.py:27
  50.0 9.4 %outer.1 = f32[16,128,128]{2,1,0:T(8,128)} custom-call(s32[2]{0:T(128)S(1)} %pad_add_fusion.place, f32[16,128,128]{2,1,0:T(8,128)S(1)} %collective-permute-done.7.outer, f32[16,128,128]{2,1,0:T(8,128)} %collective-permute-done.10.outer_pot, f32[16,128,128]{2,1,0:T(8,128)S(1)} %constant_dynamic-update-slice_fusion.4.own_pot, f32[32,144,128]{2,1,0:T(8,128)S(1)} %inner.1.edges, ...), custom_call_target="tpu_custom_call" | custom-call | flops 1000 | tf_op jit(solution)/shard_map/outer/pallas_call | solution.py:199
  59.4 9.6 %all-to-all-start = ((f32[16,128,128]{2,1,0:T(8,128)}), f32[16,128,128]{2,1,0:T(8,128)S(1)}, u32[]{:S(2)}, u32[]{:S(2)}) async-start(f32[16,128,128]{2,1,0:T(8,128)} %outer.1), calls=%async_computation | async-start | bytes 2097152 | tf_op jit(solution)/shard_map/all_to_all | solution.py:322
  69.0 15.1 %all-to-all-done.x = f32[16,128,128]{2,1,0:T(8,128)S(1)} async-done(((f32[16,128,128]{2,1,0:T(8,128)}), f32[16,128,128]{2,1,0:T(8,128)S(1)}, u32[]{:S(2)}, u32[]{:S(2)}) %all-to-all-start) | async-done | bytes 1048608 | tf_op jit(solution)/shard_map/all_to_all | solution.py:322
  84.1 2.0 %rotate.1 = (f32[4,128,128]{2,1,0:T(8,128)S(1)}, f32[4,128,128]{2,1,0:T(8,128)S(1)}, f32[4,128,128]{2,1,0:T(8,128)S(1)}, f32[4,128,128]{2,1,0:T(8,128)S(1)}) custom-call(s32[1]{0:T(128)} %bitcast.place, f32[16,16]{1,0:T(8,128)S(1)} %copy-done.1, f32[16,128,128]{2,1,0:T(8,128)S(1)} %all-to-all-done.x), custom_call_target="tpu_custom_call" | custom-call | tf_op jit(solution)/shard_map/rotate/pallas_call | solution.py:245
  86.1 4.6 %collective-permute-start.12 = (f32[4,128,128]{2,1,0:T(8,128)S(1)}, f32[4,128,128]{2,1,0:T(8,128)S(1)}, u32[]{:S(2)}, u32[]{:S(2)}) collective-permute-start(f32[4,128,128]{2,1,0:T(8,128)S(1)} %get-tuple-element.30.o0), channel_id=1, source_target_pairs={{0,0},{1,1},{2,2},{3,3},{4,32},{5,33},{6,34},{7,35},{8,8},{9,9},{1... | collective-permute-start | bytes 786440 | tf_op jit(solution)/shard_map/ppermute | solution.py:27
  90.8 1.2 %collective-permute-start.14 = (f32[4,128,128]{2,1,0:T(8,128)S(1)}, f32[4,128,128]{2,1,0:T(8,128)S(1)}, u32[]{:S(2)}, u32[]{:S(2)}) collective-permute-start(f32[4,128,128]{2,1,0:T(8,128)S(1)} %get-tuple-element.32.o2), channel_id=1, source_target_pairs={{0,64},{1,65},{2,66},{3,67},{4,96},{5,97},{6,98},{7,99},{8,72},{9,... | collective-permute-start | bytes 786440 | tf_op jit(solution)/shard_map/ppermute | solution.py:27
  92.0 1.3 %collective-permute-start.15 = (f32[4,128,128]{2,1,0:T(8,128)S(1)}, f32[4,128,128]{2,1,0:T(8,128)S(1)}, u32[]{:S(2)}, u32[]{:S(2)}) collective-permute-start(f32[4,128,128]{2,1,0:T(8,128)S(1)} %get-tuple-element.33.o3), channel_id=1, source_target_pairs={{0,96},{1,97},{2,98},{3,99},{4,64},{5,65},{6,66},{7,67},{8,104},{9... | collective-permute-start | bytes 786440 | tf_op jit(solution)/shard_map/ppermute | solution.py:27
  93.3 2.8 %collective-permute-done.12 = f32[4,128,128]{2,1,0:T(8,128)S(1)} collective-permute-done((f32[4,128,128]{2,1,0:T(8,128)S(1)}, f32[4,128,128]{2,1,0:T(8,128)S(1)}, u32[]{:S(2)}, u32[]{:S(2)}) %collective-permute-start.12) | collective-permute-done | bytes 262176 | tf_op jit(solution)/shard_map/ppermute | solution.py:27
  96.1 1.7 %gram.1 = f32[128,1,256]{2,1,0:T(1,128)} custom-call(s32[1]{0:T(128)} %bitcast.place, f32[4,128,128]{2,1,0:T(8,128)S(1)} %get-tuple-element.30.o0, f32[4,128,128]{2,1,0:T(8,128)S(1)} %get-tuple-element.31.o1, f32[4,128,128]{2,1,0:T(8,128)S(1)} %get-tuple-element.32.o2, f32[4,128,128]{2,1,0:T(8,128)S(1)} %get-tuple-element.33.o3), custom_call_target="tpu_custom_call" | custom-call | tf_op jit(solution)/shard_map/gram/pallas_call | solution.py:288
  97.8 6.8 %all-to-all-start.1 = ((f32[128,1,256]{2,1,0:T(1,128)}), f32[128,1,256]{2,1,0:T(1,128)S(1)}, u32[]{:S(2)}, u32[]{:S(2)}) async-start(f32[128,1,256]{2,1,0:T(1,128)} %gram.1), calls=%async_computation.1 | async-start | bytes 262144 | tf_op jit(solution)/shard_map/all_to_all | solution.py:327
  104.6 0.6 collective-permute-done.15
  105.5 1.1 copy.7
  106.6 8.0 %all-to-all-done.1 = f32[128,1,256]{2,1,0:T(1,128)S(1)} async-done(((f32[128,1,256]{2,1,0:T(1,128)}), f32[128,1,256]{2,1,0:T(1,128)S(1)}, u32[]{:S(2)}, u32[]{:S(2)}) %all-to-all-start.1) | async-done | bytes 131104 | tf_op jit(solution)/shard_map/all_to_all | solution.py:327
  114.6 0.2 reduce_sum.9
  114.8 0.6 constant_dynamic-slice_fusion
  (32 shorter events, 0.8 us)
Async XLA Ops:
  0.6 7.3 %copy-start.2 = (f32[4,128,128]{2,1,0:T(8,128)S(1)}, f32[4,128,128]{2,1,0:T(8,128)}, u32[]{:S(2)}) copy-start(f32[4,128,128]{2,1,0:T(8,128)} %param.6) | copy-start | bytes 786436
  2.0 11.3 %collective-permute-start = (f32[4,128,128]{2,1,0:T(8,128)S(1)}, f32[4,128,128]{2,1,0:T(8,128)S(1)}, u32[]{:S(2)}, u32[]{:S(2)}) collective-permute-start(f32[4,128,128]{2,1,0:T(8,128)S(1)} %get-tuple-element.42), channel_id=1, source_target_pairs={{0,0},{1,1},{2,2},{3,3},{4,32},{5,33},{6,34},{7,35},{8,8},{9,9},{1... | collective-permute-start | bytes 786440 | tf_op jit(solution)/shard_map/ppermute | solution.py:27
  6.5 32.2 %copy-start = (bf16[256,128]{1,0:T(8,128)(2,1)S(1)}, bf16[256,128]{1,0:T(8,128)(2,1)}, u32[]{:S(2)}) copy-start(bf16[256,128]{1,0:T(8,128)(2,1)} %constant.71.clone.matrix) | copy-start | bytes 196612
  6.5 12.2 %collective-permute-start.1 = (f32[4,128,128]{2,1,0:T(8,128)S(1)}, f32[4,128,128]{2,1,0:T(8,128)S(1)}, u32[]{:S(2)}, u32[]{:S(2)}) collective-permute-start(f32[4,128,128]{2,1,0:T(8,128)S(1)} %get-tuple-element.43), channel_id=1, source_target_pairs={{0,1},{1,2},{2,3},{3,0},{4,33},{5,34},{6,35},{7,32},{8,9},{9,10},{... | collective-permute-start | bytes 786440 | tf_op jit(solution)/shard_map/ppermute | solution.py:27
  8.0 15.0 %collective-permute-start.2 = (f32[4,128,128]{2,1,0:T(8,128)S(1)}, f32[4,128,128]{2,1,0:T(8,128)S(1)}, u32[]{:S(2)}, u32[]{:S(2)}) collective-permute-start(f32[4,128,128]{2,1,0:T(8,128)S(1)} %get-tuple-element.20), channel_id=1, source_target_pairs={{0,2},{1,3},{2,0},{3,1},{4,34},{5,35},{6,32},{7,33},{8,10},{9,11},... | collective-permute-start | bytes 786440 | tf_op jit(solution)/shard_map/ppermute | solution.py:27
  12.8 11.2 %collective-permute-start.3 = (f32[4,128,128]{2,1,0:T(8,128)S(1)}, f32[4,128,128]{2,1,0:T(8,128)S(1)}, u32[]{:S(2)}, u32[]{:S(2)}) collective-permute-start(f32[4,128,128]{2,1,0:T(8,128)S(1)} %get-tuple-element.40), channel_id=1, source_target_pairs={{0,3},{1,0},{2,1},{3,2},{4,35},{5,32},{6,33},{7,34},{8,11},{9,8},{... | collective-permute-start | bytes 786440 | tf_op jit(solution)/shard_map/ppermute | solution.py:27
  13.3 10.9 %collective-permute-start.4 = (f32[4,128,128]{2,1,0:T(8,128)S(1)}, f32[4,128,128]{2,1,0:T(8,128)S(1)}, u32[]{:S(2)}, u32[]{:S(2)}) collective-permute-start(f32[4,128,128]{2,1,0:T(8,128)S(1)} %multiply_add_fusion), channel_id=1, source_target_pairs={{0,0},{1,1},{2,2},{3,3},{4,96},{5,97},{6,98},{7,99},{8,8},{9,9},{1... | collective-permute-start | bytes 786440 | tf_op jit(solution)/shard_map/ppermute | solution.py:27
  18.2 9.7 %collective-permute-start.5 = (f32[4,128,128]{2,1,0:T(8,128)S(1)}, f32[4,128,128]{2,1,0:T(8,128)S(1)}, u32[]{:S(2)}, u32[]{:S(2)}) collective-permute-start(f32[4,128,128]{2,1,0:T(8,128)S(1)} %multiply_add_fusion), channel_id=1, source_target_pairs={{0,1},{1,2},{2,3},{3,0},{4,97},{5,98},{6,99},{7,96},{8,9},{9,10},{... | collective-permute-start | bytes 786440 | tf_op jit(solution)/shard_map/ppermute | solution.py:27
  18.8 11.5 %collective-permute-start.8 = (f32[4,128,128]{2,1,0:T(8,128)S(1)}, f32[4,128,128]{2,1,0:T(8,128)S(1)}, u32[]{:S(2)}, u32[]{:S(2)}) collective-permute-start(f32[4,128,128]{2,1,0:T(8,128)S(1)} %multiply_add_fusion), channel_id=1, source_target_pairs={{0,2},{1,3},{2,0},{3,1},{4,98},{5,99},{6,96},{7,97},{8,10},{9,11},... | collective-permute-start | bytes 786440 | tf_op jit(solution)/shard_map/ppermute | solution.py:27
  23.0 8.5 %collective-permute-start.9 = (f32[4,128,128]{2,1,0:T(8,128)S(1)}, f32[4,128,128]{2,1,0:T(8,128)S(1)}, u32[]{:S(2)}, u32[]{:S(2)}) collective-permute-start(f32[4,128,128]{2,1,0:T(8,128)S(1)} %multiply_add_fusion), channel_id=1, source_target_pairs={{0,3},{1,0},{2,1},{3,2},{4,99},{5,96},{6,97},{7,98},{8,11},{9,8},{... | collective-permute-start | bytes 786440 | tf_op jit(solution)/shard_map/ppermute | solution.py:27
  24.1 14.6 %collective-permute-start.7 = (f32[16,128,128]{2,1,0:T(8,128)S(1)}, f32[16,128,128]{2,1,0:T(8,128)S(1)}, u32[]{:S(2)}, u32[]{:S(2)}) collective-permute-start(f32[16,128,128]{2,1,0:T(8,128)S(1)} %constant_dynamic-update-slice_fusion.own), channel_id=1, source_target_pairs={{0,56},{1,57},{2,58},{3,59},{4,60},{5,61},{6,62},{7,63},{8,32},{9,... | collective-permute-start | bytes 3145736 | tf_op jit(solution)/shard_map/ppermute | solution.py:27
  27.9 10.8 %collective-permute-start.6 = (f32[16,128,128]{2,1,0:T(8,128)S(1)}, f32[16,128,128]{2,1,0:T(8,128)}, u32[]{:S(2)}, u32[]{:S(2)}) collective-permute-start(f32[16,128,128]{2,1,0:T(8,128)S(1)} %constant_dynamic-update-slice_fusion.own), channel_id=1, source_target_pairs={{0,32},{1,33},{2,34},{3,35},{4,36},{5,37},{6,38},{7,39},{8,40},{9,... | collective-permute-start | bytes 3145736 | tf_op jit(solution)/shard_map/ppermute | solution.py:27
  31.5 7.2 %collective-permute-start.11 = (f32[16,128,128]{2,1,0:T(8,128)S(1)}, f32[16,128,128]{2,1,0:T(8,128)}, u32[]{:S(2)}, u32[]{:S(2)}) collective-permute-start(f32[16,128,128]{2,1,0:T(8,128)S(1)} %constant_dynamic-update-slice_fusion.4.own_pot), channel_id=1, source_target_pairs={{0,32},{1,33},{2,34},{3,35},{4,36},{5,37},{6,38},{7,39},{8,40},{9,... | collective-permute-start | bytes 3145736 | tf_op jit(solution)/shard_map/ppermute | solution.py:27
  34.8 15.3 %collective-permute-start.10 = (f32[16,128,128]{2,1,0:T(8,128)S(1)}, f32[16,128,128]{2,1,0:T(8,128)}, u32[]{:S(2)}, u32[]{:S(2)}) collective-permute-start(f32[16,128,128]{2,1,0:T(8,128)S(1)} %constant_dynamic-update-slice_fusion.4.own_pot), channel_id=1, source_target_pairs={{0,56},{1,57},{2,58},{3,59},{4,60},{5,61},{6,62},{7,63},{8,32},{9,... | collective-permute-start | bytes 3145736 | tf_op jit(solution)/shard_map/ppermute | solution.py:27
  46.9 37.2 %copy-start.1 = (f32[16,16]{1,0:T(8,128)S(1)}, f32[16,16]{1,0:T(8,128)}, u32[]{:S(2)}) copy-start(f32[16,16]{1,0:T(8,128)} %rotation.1) | copy-start | bytes 3076
  59.4 24.7 %all-to-all-start = ((f32[16,128,128]{2,1,0:T(8,128)}), f32[16,128,128]{2,1,0:T(8,128)S(1)}, u32[]{:S(2)}, u32[]{:S(2)}) async-start(f32[16,128,128]{2,1,0:T(8,128)} %outer.1), calls=%async_computation | async-start | bytes 2097152 | tf_op jit(solution)/shard_map/all_to_all | solution.py:322
  86.1 10.1 %collective-permute-start.12 = (f32[4,128,128]{2,1,0:T(8,128)S(1)}, f32[4,128,128]{2,1,0:T(8,128)S(1)}, u32[]{:S(2)}, u32[]{:S(2)}) collective-permute-start(f32[4,128,128]{2,1,0:T(8,128)S(1)} %get-tuple-element.30.o0), channel_id=1, source_target_pairs={{0,0},{1,1},{2,2},{3,3},{4,32},{5,33},{6,34},{7,35},{8,8},{9,9},{1... | collective-permute-start | bytes 786440 | tf_op jit(solution)/shard_map/ppermute | solution.py:27
  90.7 13.9 %collective-permute-start.13 = (f32[4,128,128]{2,1,0:T(8,128)S(1)}, f32[4,128,128]{2,1,0:T(8,128)S(1)}, u32[]{:S(2)}, u32[]{:S(2)}) collective-permute-start(f32[4,128,128]{2,1,0:T(8,128)S(1)} %get-tuple-element.31.o1), channel_id=1, source_target_pairs={{0,32},{1,33},{2,34},{3,35},{4,0},{5,1},{6,2},{7,3},{8,40},{9,41},... | collective-permute-start | bytes 786440 | tf_op jit(solution)/shard_map/ppermute | solution.py:27
  90.8 13.8 %collective-permute-start.14 = (f32[4,128,128]{2,1,0:T(8,128)S(1)}, f32[4,128,128]{2,1,0:T(8,128)S(1)}, u32[]{:S(2)}, u32[]{:S(2)}) collective-permute-start(f32[4,128,128]{2,1,0:T(8,128)S(1)} %get-tuple-element.32.o2), channel_id=1, source_target_pairs={{0,64},{1,65},{2,66},{3,67},{4,96},{5,97},{6,98},{7,99},{8,72},{9,... | collective-permute-start | bytes 786440 | tf_op jit(solution)/shard_map/ppermute | solution.py:27
  92.0 13.3 %collective-permute-start.15 = (f32[4,128,128]{2,1,0:T(8,128)S(1)}, f32[4,128,128]{2,1,0:T(8,128)S(1)}, u32[]{:S(2)}, u32[]{:S(2)}) collective-permute-start(f32[4,128,128]{2,1,0:T(8,128)S(1)} %get-tuple-element.33.o3), channel_id=1, source_target_pairs={{0,96},{1,97},{2,98},{3,99},{4,64},{5,65},{6,66},{7,67},{8,104},{9... | collective-permute-start | bytes 786440 | tf_op jit(solution)/shard_map/ppermute | solution.py:27
  97.8 16.8 %all-to-all-start.1 = ((f32[128,1,256]{2,1,0:T(1,128)}), f32[128,1,256]{2,1,0:T(1,128)S(1)}, u32[]{:S(2)}, u32[]{:S(2)}) async-start(f32[128,1,256]{2,1,0:T(1,128)} %gram.1), calls=%async_computation.1 | async-start | bytes 262144 | tf_op jit(solution)/shard_map/all_to_all | solution.py:327
